TPU v7x, 256 devices: a whole 4x4x8 slice. The times are simulated.
256 devices in a mesh: rows: 16 (over x_hi, z), cols: 4 (over x_lo, core), dp: 4 (over y).
Axes of the slice: x: 4 (x_hi: 2, x_lo: 2; x = x_hi * 2 + x_lo), y: 4, z: 8, core: 2. Of those that a mesh axis runs over, the one named last changes fastest.
Arguments:
- fields: float32 [1024, 64, 384], P(('dp', 'rows'), 'cols'), parts along dimension 0, may hold values from -6 to 6
- logit_scale: float32 [6], replicated, may hold values from 4 to 25
- w_qkv: bfloat16 [384, 1152], replicated, may hold values from -0.3125 to 0.3125
- w_proj: bfloat16 [384, 384], replicated, may hold values from -0.3125 to 0.3125
- w_merge: bfloat16 [1536, 768], P(None, 'cols'), may hold values from -0.15625 to 0.15625
- w_up: bfloat16 [768, 3072], P('rows', 'cols'), may hold values from -0.21875 to 0.21875
- w_down: bfloat16 [3072, 768], P('cols', 'rows'), may hold values from -0.109375 to 0.109375
- cotangent: bfloat16 [512, 32, 768], P(('dp', 'rows'), 'cols'), parts along dimension 0, may hold values from -0.59765625 to 0.59765625
Outputs:
- coarse: float32 [512, 32, 768], P(('dp', 'rows'), 'cols'), parts along dimension 0
- grad_coarse: float32 [512, 32, 768], P(('dp', 'rows'), 'cols'), parts along dimension 0
- grad_up: float32 [768, 12288], P('rows', ('dp', 'cols')), parts along dimension 1
- grad_down: float32 [3072, 3072], P('cols', ('dp', 'rows')), parts along dimension 1
There are 4 independent parts, one for each index of `dp`. A program takes and returns all parts, laid end to end along the dimension named above; an argument that names none is the same for every part. Nothing has to cross between parts.
All inputs are finite; a program needn't handle non-finite values.
Results may differ from a plain program's by a relative error of at most 0.02.
Values may be sent and summed in bfloat16 or wider, within the bound.
No kernel may reach another device: no remote copies, remote signals or barrier semaphores. Data moves between devices by JAX's collectives and lax.ppermute only.
A program may use at most 64 MiB of HBM per device.

v0:
```python
import jax
import jax.numpy as jnp
from jax import lax
from jax.experimental import pallas as pl
from jax.experimental.pallas import tpu as pltpu
from jax.sharding import Mesh
from jax.sharding import PartitionSpec as P


NX, NZ, NL, NCORE = 2, 8, 2, 2
ROWS = ("xh", "z")
COLS = ("xl", "core")
GRID = ("xh", "z", "xl", "core")
NROW, NCOL = NX * NZ, NL * NCORE

eps_norm = 1e-05
eps_unit = 1e-06
BF = jnp.bfloat16
F32 = jnp.float32


def dot(a, b):
    return jnp.dot(a, b, preferred_element_type=F32)


def dot_nt(a, b):
    return lax.dot_general(a, b, (((1,), (1,)), ((), ())), preferred_element_type=F32)


def dot_tn(a, b):
    return lax.dot_general(a, b, (((0,), (0,)), ((), ())), preferred_element_type=F32)


def layer_norm(value):
    average = jnp.mean(value, axis=-1, keepdims=True)
    centred = value - average
    spread = jnp.mean(centred * centred, axis=-1, keepdims=True)
    inverse = lax.rsqrt(spread + eps_norm)
    return (centred * inverse, inverse)


def norm_slope(upstream, normed, inverse):
    first_mean = jnp.mean(upstream, axis=-1, keepdims=True)
    second_mean = jnp.mean(upstream * normed, axis=-1, keepdims=True)
    return inverse * (upstream - first_mean - normed * second_mean)


def exact_gelu(value):
    return jax.nn.gelu(value, approximate=False)


def to_grid(array, dr, dc):
    pairs = [
        (r * NCOL + c, ((r + dr) % NROW) * NCOL + (c + dc) % NCOL)
        for r in range(NROW)
        for c in range(NCOL)
    ]
    return lax.ppermute(array, GRID, pairs)


def swap_core(array):
    return lax.ppermute(array, "core", [(0, 1), (1, 0)])


def swap_xl(array):
    return lax.ppermute(array, "xl", [(0, 1), (1, 0)])


def swap_half(array):
    return lax.ppermute(array, "xh", [(0, 1), (1, 0)])


def along_z(array, step):
    return lax.ppermute(array, "z", [(i, (i + step) % NZ) for i in range(NZ)])


def gather_cols(rows):
    near = jnp.concatenate([rows, swap_xl(rows)], axis=0)
    return jnp.concatenate([near, swap_core(near)], axis=0)


def scatter_cols(rows):
    rows = rows.astype(BF)
    half, quarter = rows.shape[0] // 2, rows.shape[0] // 4
    near = rows[:half].astype(F32) + swap_core(rows[half:]).astype(F32)
    return near[:quarter] + swap_xl(near[quarter:].astype(BF)).astype(F32)


def gather_rows(shard):
    other = swap_half(shard)
    first = lax.axis_index("xh") == 0
    own = jnp.stack([jnp.where(first, shard, other), jnp.where(first, other, shard)])
    z = lax.axis_index("z")
    full = jnp.zeros((NX, NZ, *shard.shape), shard.dtype)

    def put(full, block, k):
        return lax.dynamic_update_slice_in_dim(full, block[:, None], (z + k) % NZ, 1)

    full = put(full, own, 0)
    left = right = own
    for k in (1, 2, 3):
        left, right = along_z(left, -1), along_z(right, 1)
        full = put(full, left, k)
        full = put(full, right, NZ - k)
    far = [along_z(left[0], -1), along_z(right[1], 1)]
    far = jnp.stack(far)
    return put(full, far, 4)


def scatter_rows(terms):
    blocks = [term.reshape(NX, NZ, -1, term.shape[-1]) for term in terms]
    z = lax.axis_index("z")

    def block(k):
        return jnp.stack([lax.dynamic_index_in_dim(b, (z + k) % NZ, 1, False) for b in blocks], 1)

    far = block(4)
    left, right = along_z(far[0], -1), along_z(far[1], 1)
    near_left, near_right = block(NZ - 3), block(3)
    left = jnp.stack([near_left[0] + left, near_left[1]])
    right = jnp.stack([near_right[0], near_right[1] + right])
    for k in (2, 1):
        left, right = along_z(left, -1), along_z(right, 1)
        left, right = left + block(NZ - k), right + block(k)
    left, right = along_z(left, -1), along_z(right, 1)
    both = left.astype(F32) + right.astype(F32) + block(0).astype(F32)
    first = lax.axis_index("xh") == 0
    other = swap_half(jnp.where(first, both[1], both[0]).astype(BF))
    return jnp.where(first, both[0], both[1]) + other.astype(F32)


def order_kernel(fields_ref, cot_ref, *outs):
    n = fields_ref.shape[0]
    to = lax.broadcasted_iota(jnp.int32, (n, n), 0)
    at = lax.broadcasted_iota(jnp.int32, (n, n), 1)
    c4, r4 = to & 3, (to >> 2) & 3
    pr, pc = (to >> 4) & 1, (to >> 5) & 1
    qb, qa = (to >> 6) & 1, (to >> 7) & 1
    source = (qa * 8 + r4 * 2 + pr) * 16 + qb * 8 + c4 * 2 + pc
    pick = jnp.where(at == source, 1.0, 0.0).astype(BF)
    moved = dot(pick, fields_ref[...].astype(BF)).astype(BF)
    m = cot_ref.shape[0]
    to = lax.broadcasted_iota(jnp.int32, (m, m), 0)
    at = lax.broadcasted_iota(jnp.int32, (m, m), 1)
    source = (((to >> 5) & 1) * 4 + ((to >> 2) & 3)) * 8 + ((to >> 4) & 1) * 4 + (to & 3)
    pick = jnp.where(at == source, 1.0, 0.0).astype(BF)
    cot = dot(pick, cot_ref[...]).astype(BF)
    wide = fields_ref.shape[1]
    for k in range(4):
        outs[k][:64] = moved[k * 64 : (k + 1) * 64]
        outs[k][64:80] = cot[k * 16 : (k + 1) * 16, :wide]
        outs[k][80:] = cot[k * 16 : (k + 1) * 16, wide:]


def window_kernel(scale_ref, x0, x1, x2, x3, qkv_ref, proj_ref, out_ref, cot_ref):
    quads = (x0[...], x1[...], x2[...], x3[...])
    x = jnp.concatenate([q[k * 16 : (k + 1) * 16] for k in range(4) for q in quads], axis=0)
    channels = x.shape[1]
    heads = channels // 64
    raw = dot(x, qkv_ref[...])
    mixed = []
    for h in range(heads):
        q = raw[:, h * 64 : (h + 1) * 64]
        k = raw[:, channels + h * 64 : channels + (h + 1) * 64]
        v = raw[:, 2 * channels + h * 64 : 2 * channels + (h + 1) * 64].astype(BF)
        q = q * lax.rsqrt(jnp.sum(q * q, axis=-1, keepdims=True) + eps_unit)
        k = k * lax.rsqrt(jnp.sum(k * k, axis=-1, keepdims=True) + eps_unit)
        scores = dot_nt(q.astype(BF), k.astype(BF))
        weights = jnp.exp(scores * scale_ref[h])
        total = jnp.sum(weights, axis=-1, keepdims=True)
        mixed.append(dot(weights.astype(BF), v) / total)
    mixed = jnp.concatenate(mixed, axis=1).astype(BF)
    normed, _ = layer_norm(dot(mixed, proj_ref[...]))
    stream = (x.astype(F32) + normed).astype(BF)
    own = stream.shape[0] // 4
    for k in range(4):
        out_ref[:, k * channels : (k + 1) * channels] = stream[k * own : (k + 1) * own]
        cot_ref[k * 16 : (k + 1) * 16, :channels] = quads[k][64:80]
        cot_ref[k * 16 : (k + 1) * 16, channels:] = quads[k][80:]


def level_kernel(merged_ref, own_ref, core_ref, near_ref, far_ref, place_ref, level_ref, bf_ref):
    merged = merged_ref[...]
    parts = [dot_nt(merged, r[...]) for r in (own_ref, core_ref, near_ref, far_ref)]
    xl, core = place_ref[0] == 0, place_ref[1] == 0
    low = [jnp.where(xl, parts[k], parts[k + 2]) for k in (0, 1)]
    high = [jnp.where(xl, parts[k + 2], parts[k]) for k in (0, 1)]
    ordered = []
    for pair in (low, high):
        ordered += [jnp.where(core, pair[0], pair[1]), jnp.where(core, pair[1], pair[0])]
    level, _ = layer_norm(jnp.concatenate(ordered, axis=1))
    level_ref[...] = level
    bf_ref[...] = level.astype(BF)


def whole(count):
    return [pl.BlockSpec(memory_space=pltpu.VMEM)] * count


def whole_step(fields, logit_scale, w_qkv, w_proj, w_merge, w_up, w_down, cotangent):
    tile_rows, tile_cols, channels = fields.shape
    wide = cotangent.shape[-1]
    tokens = tile_rows * tile_cols
    own = tokens // 4

    tile_quads = pl.pallas_call(
        order_kernel,
        out_shape=[jax.ShapeDtypeStruct((96, channels), BF)] * 4,
        in_specs=whole(2),
        out_specs=whole(4),
        name="order",
    )(fields.reshape(tokens, channels), cotangent.reshape(own, wide))

    def to_window(quads):
        return (
            quads[3],
            to_grid(quads[2], 0, -1),
            to_grid(quads[1], -1, 0),
            to_grid(quads[0], -1, -1),
        )

    def to_tile(quads):
        return (
            to_grid(quads[3], 1, 1),
            to_grid(quads[2], 1, 0),
            to_grid(quads[1], 0, 1),
            quads[0],
        )

    x = to_window(tile_quads)

    weights = gather_rows(jnp.stack([w_up, w_down.T]))
    up_full = weights[:, :, 0].reshape(wide, -1)
    down_full = weights[:, :, 1].reshape(wide, -1)

    merge_own = w_merge.T
    merge_near = swap_xl(merge_own)
    merge_core = swap_core(merge_own)
    merge_far = swap_core(merge_near)

    merged, cot = pl.pallas_call(
        window_kernel,
        out_shape=[
            jax.ShapeDtypeStruct((own, 4 * channels), BF),
            jax.ShapeDtypeStruct((own, wide), BF),
        ],
        in_specs=[pl.BlockSpec(memory_space=pltpu.SMEM)] + whole(6),
        out_specs=whole(2),
        cost_estimate=pl.CostEstimate(
            flops=2 * tokens * channels * (4 * channels + 2 * tokens),
            transcendentals=tokens * tokens * 6,
            bytes_accessed=2_000_000,
        ),
        name="window",
    )(logit_scale, *x, w_qkv, w_proj)
    place = jnp.stack([lax.axis_index("xl"), lax.axis_index("core")])
    level, level_own = pl.pallas_call(
        level_kernel,
        out_shape=[jax.ShapeDtypeStruct((own, wide), F32), jax.ShapeDtypeStruct((own, wide), BF)],
        in_specs=whole(5) + [pl.BlockSpec(memory_space=pltpu.SMEM)],
        out_specs=whole(2),
        cost_estimate=pl.CostEstimate(
            flops=8 * own * channels * wide, transcendentals=own, bytes_accessed=3_000_000
        ),
        name="level",
    )(merged, merge_own, merge_core, merge_near, merge_far, place)
    level_b = gather_cols(level_own)

    hidden_pre = dot(level_b, up_full)
    hidden = exact_gelu(hidden_pre).astype(BF)

    branch_norm, branch_inv = layer_norm(scatter_cols(dot_nt(hidden, down_full)))
    coarse = level + branch_norm
    upstream = cot.astype(F32)
    slope_own = norm_slope(upstream, branch_norm, branch_inv).astype(BF)
    slope_out = gather_cols(slope_own)
    slope_hidden = dot(slope_out, down_full)
    _, pullback = jax.vjp(exact_gelu, hidden_pre)
    slope_pre = pullback(slope_hidden)[0].astype(BF)
    term_down = dot_tn(slope_out, hidden).astype(BF)
    term_up = dot_tn(level_b, slope_pre).astype(BF)
    grads = scatter_rows((term_down, term_up))
    grad_coarse = upstream + scatter_cols(dot_nt(slope_pre, up_full))

    both = jnp.concatenate([coarse, grad_coarse], axis=1).astype(BF)
    quads = to_tile([both[k * 16 : (k + 1) * 16] for k in range(4)])
    both = jnp.stack(quads).reshape(2, 2, 4, 4, 2 * wide).transpose(0, 2, 1, 3, 4)
    both = both.reshape(tile_rows // 2, tile_cols // 2, 2 * wide).astype(F32)
    return (both[..., :wide], both[..., wide:], grads[1], grads[0].T)


def solution(mesh):
    finer = Mesh(
        mesh.devices.reshape(NX, NZ, NL, NCORE, mesh.shape["dp"]),
        ("xh", "z", "xl", "core", "dp"),
    )
    rows = ("dp", *ROWS)
    in_specs = (
        P(rows, COLS, None),
        P(),
        P(),
        P(),
        P(None, COLS),
        P(ROWS, COLS),
        P(COLS, ROWS),
        P(rows, COLS, None),
    )
    out_specs = (
        P(rows, COLS, None),
        P(rows, COLS, None),
        P(ROWS, ("dp", *COLS)),
        P(COLS, rows),
    )
    return jax.shard_map(
        whole_step, mesh=finer, in_specs=in_specs, out_specs=out_specs, check_vma=False
    )
```

profile of v0, /device:TPU:1, one launch (start us, length us, event | category | flops | bytes accessed | tf_op | source)
XLA Modules:
  0.0 129.2 jit_solution(6458862009107439295)
XLA Ops:
  0.6 1.0 pad_maximum_fusion.11
  1.6 3.6 %collective-permute-start.8 = (bf16[2,48,768]{2,1,0:T(8,128)(2,1)S(1)}, bf16[2,48,768]{2,1,0:T(8,128)(2,1)S(1)}, u32[]{:S(2)}, u32[]{:S(2)}) collective-permute-start(bf16[2,48,768]{2,1,0:T(8,128)(2,1)S(1)} %pad_maximum_fusion.11), channel_id=1, source_target_pairs={{0,128},{128,0},{1,129},{129,1},{2,130},{130,2},{3,131},{131,3},{4... | collective-permute-start | bytes 442376 | tf_op jit(solution)/shard_map/ppermute | solution.py:70
  5.3 2.0 %order.1 = (bf16[96,384]{1,0:T(8,128)(2,1)}, bf16[96,384]{1,0:T(8,128)(2,1)}, bf16[96,384]{1,0:T(8,128)(2,1)}, bf16[96,384]{1,0:T(8,128)(2,1)}) custom-call(f32[256,384]{1,0:T(8,128)} %bitcast.105, bf16[64,768]{1,0:T(8,128)(2,1)} %bitcast.112), custom_call_target="tpu_custom_call" | custom-call | tf_op jit(solution)/shard_map/order/pallas_call | solution.py:206
  7.3 1.0 collective-permute-start
  8.2 5.5 %collective-permute-start.1 = (bf16[96,384]{1,0:T(8,128)(2,1)}, bf16[96,384]{1,0:T(8,128)(2,1)S(1)}, u32[]{:S(2)}, u32[]{:S(2)}) collective-permute-start(bf16[96,384]{1,0:T(8,128)(2,1)} %get-tuple-element.14), channel_id=1, source_target_pairs={{0,240},{4,244},{8,248},{12,252},{16,0},{20,4},{24,8},{28,12},{32,... | collective-permute-start | bytes 221192 | tf_op jit(solution)/shard_map/ppermute | solution.py:58
  13.7 2.1 %collective-permute-start.2 = (bf16[96,384]{1,0:T(8,128)(2,1)}, bf16[96,384]{1,0:T(8,128)(2,1)S(1)}, u32[]{:S(2)}, u32[]{:S(2)}) collective-permute-start(bf16[96,384]{1,0:T(8,128)(2,1)} %get-tuple-element.15), channel_id=1, source_target_pairs={{0,252},{4,240},{8,244},{12,248},{16,12},{20,0},{24,4},{28,8},{32,... | collective-permute-start | bytes 221192 | tf_op jit(solution)/shard_map/ppermute | solution.py:58
  15.9 0.9 select_bitcast_fusion.1
  17.0 1.5 %collective-permute-start.10 = (bf16[2,2,48,768]{3,2,1,0:T(8,128)(2,1)S(1)}, bf16[2,2,48,768]{3,2,1,0:T(8,128)(2,1)}, u32[]{:S(2)}, u32[]{:S(2)}) collective-permute-start(bf16[2,2,48,768]{3,2,1,0:T(8,128)(2,1)S(1)} %get-tuple-element.50), channel_id=1, source_target_pairs={{0,16},{16,32},{32,48},{48,64},{64,80},{80,96},{96,112},{112,0},{1... | collective-permute-start | bytes 884744 | tf_op jit(solution)/shard_map/ppermute | solution.py:74
  18.4 0.7 pad_add_fusion.place_ref
  20.0 6.7 %window.1 = (bf16[64,1536]{1,0:T(8,128)(2,1)}, bf16[64,768]{1,0:T(8,128)(2,1)}) custom-call(f32[6]{0:T(128)} %scale_ref.1, bf16[96,384]{1,0:T(8,128)(2,1)} %get-tuple-element.12.x0, bf16[96,384]{1,0:T(8,128)(2,1)} %copy-done.4, bf16[96,384]{1,0:T(8,128)(2,1)} %copy-done.5, bf16[96,384]{1,0:T(8,128)(2,1)} %copy-done.6, bf16[384,1152]{1,0:T(8,128)(2,1)} %qkv_ref.1, ...), custom_call_target="tpu_custom_call" | custom-call | flops 402653184 | bytes 2000000 | tf_op jit(solution)/shard_map/window/pallas_call | solution.py:241
  27.0 4.3 %collective-permute-start.11 = (bf16[2,2,48,768]{3,2,1,0:T(8,128)(2,1)}, bf16[2,2,48,768]{3,2,1,0:T(8,128)(2,1)S(1)}, u32[]{:S(2)}, u32[]{:S(2)}) collective-permute-start(bf16[2,2,48,768]{3,2,1,0:T(8,128)(2,1)} %collective-permute-done.9), channel_id=1, source_target_pairs={{0,112},{16,0},{32,16},{48,32},{64,48},{80,64},{96,80},{112,96},{1... | collective-permute-start | bytes 884744 | tf_op jit(solution)/shard_map/ppermute | solution.py:74
  31.2 1.0 copy_dynamic-update-slice_fusion.5
  32.2 1.0 copy_dynamic-update-slice_fusion.4
  33.2 0.8 collective-permute-done.4.near_ref
  34.0 1.2 collective-permute-start.5
  35.2 2.3 %collective-permute-done.11 = bf16[2,2,48,768]{3,2,1,0:T(8,128)(2,1)S(1)} collective-permute-done((bf16[2,2,48,768]{3,2,1,0:T(8,128)(2,1)}, bf16[2,2,48,768]{3,2,1,0:T(8,128)(2,1)S(1)}, u32[]{:S(2)}, u32[]{:S(2)}) %collective-permute-start.11) | collective-permute-done | bytes 294944 | tf_op jit(solution)/shard_map/ppermute | solution.py:74
  37.5 3.3 %collective-permute-start.13 = (bf16[2,2,48,768]{3,2,1,0:T(8,128)(2,1)S(1)}, bf16[2,2,48,768]{3,2,1,0:T(8,128)(2,1)S(1)}, u32[]{:S(2)}, u32[]{:S(2)}) collective-permute-start(bf16[2,2,48,768]{3,2,1,0:T(8,128)(2,1)S(1)} %collective-permute-done.11), channel_id=1, source_target_pairs={{0,112},{16,0},{32,16},{48,32},{64,48},{80,64},{96,80},{112,96},{1... | collective-permute-start | bytes 884744 | tf_op jit(solution)/shard_map/ppermute | solution.py:74
  40.9 8.2 %collective-permute-done.14 = bf16[2,2,48,768]{3,2,1,0:T(8,128)(2,1)S(1)} collective-permute-done((bf16[2,2,48,768]{3,2,1,0:T(8,128)(2,1)S(1)}, bf16[2,2,48,768]{3,2,1,0:T(8,128)(2,1)S(1)}, u32[]{:S(2)}, u32[]{:S(2)}) %collective-permute-start.14) | collective-permute-done | bytes 294944 | tf_op jit(solution)/shard_map/ppermute | solution.py:74
  49.2 2.7 %collective-permute-start.15 = (bf16[2,48,768]{2,1,0:T(8,128)(2,1)S(1)}, bf16[2,48,768]{2,1,0:T(8,128)(2,1)S(1)}, u32[]{:S(2)}, u32[]{:S(2)}) collective-permute-start(bf16[2,48,768]{2,1,0:T(8,128)(2,1)S(1)} %slice_bitcast_fusion.3), channel_id=1, source_target_pairs={{0,112},{16,0},{32,16},{48,32},{64,48},{80,64},{96,80},{112,96},{1... | collective-permute-start | bytes 442376 | tf_op jit(solution)/shard_map/ppermute | solution.py:74
  52.1 3.5 %level.1 = (f32[64,768]{1,0:T(8,128)}, bf16[64,768]{1,0:T(8,128)(2,1)}) custom-call(bf16[64,1536]{1,0:T(8,128)(2,1)} %get-tuple-element.16.merged_ref, bf16[192,1536]{1,0:T(8,128)(2,1)} %bitcast.102, bf16[192,1536]{1,0:T(8,128)(2,1)} %collective-permute-done.3.core_ref, bf16[192,1536]{1,0:T(8,128)(2,1)} %collective-permute-done.4.near_ref, ...), custom_call_target="tpu_custom_call" | custom-call | flops 150994944 | bytes 3000000 | tf_op jit(solution)/shard_map/level/pallas_call | solution.py:257
  55.8 3.4 %collective-permute-done.6 = bf16[64,768]{1,0:T(8,128)(2,1)S(1)} collective-permute-done((bf16[64,768]{1,0:T(8,128)(2,1)}, bf16[64,768]{1,0:T(8,128)(2,1)S(1)}, u32[]{:S(2)}, u32[]{:S(2)}) %collective-permute-start.6) | collective-permute-done | bytes 98336 | tf_op jit(solution)/shard_map/ppermute | solution.py:66
  59.3 4.2 %collective-permute-start.7 = (bf16[128,768]{1,0:T(8,128)(2,1)S(1)}, bf16[128,768]{1,0:T(8,128)(2,1)S(1)}, u32[]{:S(2)}, u32[]{:S(2)}) collective-permute-start(bf16[128,768]{1,0:T(8,128)(2,1)S(1)} %pad_maximum_fusion.3), channel_id=1, source_target_pairs={{0,4},{4,0},{1,5},{5,1},{2,6},{6,2},{3,7},{7,3},{8,12},{12,8},{9,1... | collective-permute-start | bytes 589832 | tf_op jit(solution)/shard_map/ppermute | solution.py:62
  63.4 1.1 collective-permute-done.7
  64.5 2.4 %multiply_convert_fusion = (bf16[256,768]{1,0:T(8,128)(2,1)S(1)}, f32[256,768]{1,0:T(8,128)S(1)}, f32[256,768]{1,0:T(8,128)S(1)}) fusion(bf16[256,768]{1,0:T(8,128)(2,1)S(1)} %constant_dynamic-update-slice_fusion, bf16[768,768]{1,0:T(8,128)(2,1)S(1)} %bitcast.95), kind=kOutput, calls=%fused_computation.7 | convolution fusion | flops 314769408 | bytes 3538944 | tf_op jit(solution)/shard_map/dot_general | solution.py:23
  67.9 1.1 collective-permute-done.17
  69.2 4.0 %collective-permute-done.18 = bf16[64,768]{1,0:T(8,128)(2,1)S(1)} collective-permute-done((bf16[64,768]{1,0:T(8,128)(2,1)S(1)}, bf16[64,768]{1,0:T(8,128)(2,1)S(1)}, u32[]{:S(2)}, u32[]{:S(2)}) %collective-permute-start.18) | collective-permute-done | bytes 98336 | tf_op jit(solution)/shard_map/ppermute | solution.py:66
  74.2 3.2 %collective-permute-done.19 = bf16[64,768]{1,0:T(8,128)(2,1)S(1)} collective-permute-done((bf16[64,768]{1,0:T(8,128)(2,1)S(1)}, bf16[64,768]{1,0:T(8,128)(2,1)S(1)}, u32[]{:S(2)}, u32[]{:S(2)}) %collective-permute-start.19) | collective-permute-done | bytes 98336 | tf_op jit(solution)/shard_map/ppermute | solution.py:66
  77.4 2.5 %collective-permute-start.20 = (bf16[128,768]{1,0:T(8,128)(2,1)S(1)}, bf16[128,768]{1,0:T(8,128)(2,1)S(1)}, u32[]{:S(2)}, u32[]{:S(2)}) collective-permute-start(bf16[128,768]{1,0:T(8,128)(2,1)S(1)} %pad_maximum_fusion.4), channel_id=1, source_target_pairs={{0,4},{4,0},{1,5},{5,1},{2,6},{6,2},{3,7},{7,3},{8,12},{12,8},{9,1... | collective-permute-start | bytes 589832 | tf_op jit(solution)/shard_map/ppermute | solution.py:62
  79.9 1.1 collective-permute-done.20
  81.0 0.6 add_convert_fusion
  81.6 0.5 convolution_convert_fusion
  84.1 2.9 %collective-permute-start.26 = (bf16[2,48,768]{2,1,0:T(8,128)(2,1)S(1)}, bf16[2,48,768]{2,1,0:T(8,128)(2,1)S(1)}, u32[]{:S(2)}, u32[]{:S(2)}) collective-permute-start(bf16[2,48,768]{2,1,0:T(8,128)(2,1)S(1)} %get-tuple-element.48), channel_id=1, source_target_pairs={{0,112},{16,0},{32,16},{48,32},{64,48},{80,64},{96,80},{112,96},{1... | collective-permute-start | bytes 442376 | tf_op jit(solution)/shard_map/ppermute | solution.py:74
  87.1 2.3 %collective-permute-done.30 = bf16[2,48,768]{2,1,0:T(8,128)(2,1)S(1)} collective-permute-done((bf16[2,48,768]{2,1,0:T(8,128)(2,1)S(1)}, bf16[2,48,768]{2,1,0:T(8,128)(2,1)S(1)}, u32[]{:S(2)}, u32[]{:S(2)}) %collective-permute-start.30) | collective-permute-done | bytes 147488 | tf_op jit(solution)/shard_map/ppermute | solution.py:74
  90.0 3.5 %collective-permute-start.27 = (bf16[2,2,48,768]{3,2,1,0:T(8,128)(2,1)S(1)}, bf16[2,2,48,768]{3,2,1,0:T(8,128)(2,1)S(1)}, u32[]{:S(2)}, u32[]{:S(2)}) collective-permute-start(bf16[2,2,48,768]{3,2,1,0:T(8,128)(2,1)S(1)} %fusion.9), channel_id=1, source_target_pairs={{0,112},{16,0},{32,16},{48,32},{64,48},{80,64},{96,80},{112,96},{1... | collective-permute-start | bytes 884744 | tf_op jit(solution)/shard_map/ppermute | solution.py:74
  93.6 4.4 %collective-permute-done.31 = bf16[2,2,48,768]{3,2,1,0:T(8,128)(2,1)S(1)} collective-permute-done((bf16[2,2,48,768]{3,2,1,0:T(8,128)(2,1)S(1)}, bf16[2,2,48,768]{3,2,1,0:T(8,128)(2,1)S(1)}, u32[]{:S(2)}, u32[]{:S(2)}) %collective-permute-start.31) | collective-permute-done | bytes 294944 | tf_op jit(solution)/shard_map/ppermute | solution.py:74
  98.1 0.5 collective-permute-done.27
  98.7 3.5 %collective-permute-start.28 = (bf16[2,2,48,768]{3,2,1,0:T(8,128)(2,1)S(1)}, bf16[2,2,48,768]{3,2,1,0:T(8,128)(2,1)S(1)}, u32[]{:S(2)}, u32[]{:S(2)}) collective-permute-start(bf16[2,2,48,768]{3,2,1,0:T(8,128)(2,1)S(1)} %maximum_add_fusion), channel_id=1, source_target_pairs={{0,112},{16,0},{32,16},{48,32},{64,48},{80,64},{96,80},{112,96},{1... | collective-permute-start | bytes 884744 | tf_op jit(solution)/shard_map/ppermute | solution.py:74
  102.3 3.6 %collective-permute-done.32 = bf16[2,2,48,768]{3,2,1,0:T(8,128)(2,1)S(1)} collective-permute-done((bf16[2,2,48,768]{3,2,1,0:T(8,128)(2,1)S(1)}, bf16[2,2,48,768]{3,2,1,0:T(8,128)(2,1)S(1)}, u32[]{:S(2)}, u32[]{:S(2)}) %collective-permute-start.32) | collective-permute-done | bytes 294944 | tf_op jit(solution)/shard_map/ppermute | solution.py:74
  106.0 0.6 collective-permute-done.28
  106.6 3.5 %collective-permute-start.29 = (bf16[2,2,48,768]{3,2,1,0:T(8,128)(2,1)S(1)}, bf16[2,2,48,768]{3,2,1,0:T(8,128)(2,1)S(1)}, u32[]{:S(2)}, u32[]{:S(2)}) collective-permute-start(bf16[2,2,48,768]{3,2,1,0:T(8,128)(2,1)S(1)} %maximum_add_fusion.1), channel_id=1, source_target_pairs={{0,112},{16,0},{32,16},{48,32},{64,48},{80,64},{96,80},{112,96},{1... | collective-permute-start | bytes 884744 | tf_op jit(solution)/shard_map/ppermute | solution.py:74
  110.1 3.1 %collective-permute-start.25 = (bf16[16,1536]{1,0:T(8,128)(2,1)S(1)}, bf16[16,1536]{1,0:T(8,128)(2,1)S(1)}, u32[]{:S(2)}, u32[]{:S(2)}) collective-permute-start(bf16[16,1536]{1,0:T(8,128)(2,1)S(1)} %get-tuple-element.57), channel_id=1, source_target_pairs={{0,4},{4,8},{8,12},{12,0},{16,20},{20,24},{24,28},{28,16},{32,36},... | collective-permute-start | bytes 147464 | tf_op jit(solution)/shard_map/ppermute | solution.py:58
  113.2 1.2 collective-permute-done.25
  114.4 5.4 %collective-permute-done.24 = bf16[16,1536]{1,0:T(8,128)(2,1)S(1)} collective-permute-done((bf16[16,1536]{1,0:T(8,128)(2,1)S(1)}, bf16[16,1536]{1,0:T(8,128)(2,1)S(1)}, u32[]{:S(2)}, u32[]{:S(2)}) %collective-permute-start.24) | collective-permute-done | bytes 49184 | tf_op jit(solution)/shard_map/ppermute | solution.py:58
  119.8 1.9 %collective-permute-done.23 = bf16[16,1536]{1,0:T(8,128)(2,1)S(1)} collective-permute-done((bf16[16,1536]{1,0:T(8,128)(2,1)S(1)}, bf16[16,1536]{1,0:T(8,128)(2,1)S(1)}, u32[]{:S(2)}, u32[]{:S(2)}) %collective-permute-start.23) | collective-permute-done | bytes 49184 | tf_op jit(solution)/shard_map/ppermute | solution.py:58
  122.2 1.3 collective-permute-start.34
  123.5 0.8 fusion.39
  124.3 4.1 %collective-permute-done.34 = bf16[2,48,768]{2,1,0:T(8,128)(2,1)S(1)} collective-permute-done((bf16[2,48,768]{2,1,0:T(8,128)(2,1)S(1)}, bf16[2,48,768]{2,1,0:T(8,128)(2,1)S(1)}, u32[]{:S(2)}, u32[]{:S(2)}) %collective-permute-start.34) | collective-permute-done | bytes 147488 | tf_op jit(solution)/shard_map/ppermute | solution.py:70
  128.4 0.7 slice_bitcast_fusion
  (102 shorter events, 7.5 us)
Async XLA Ops:
  0.6 18.5 %copy-start.1 = (bf16[1536,192]{0,1:T(8,128)(2,1)S(1)}, bf16[1536,192]{0,1:T(8,128)(2,1)}, u32[]{:S(2)}) copy-start(bf16[1536,192]{0,1:T(8,128)(2,1)} %param.12) | copy-start | bytes 1769476
  1.6 14.3 %collective-permute-start.8 = (bf16[2,48,768]{2,1,0:T(8,128)(2,1)S(1)}, bf16[2,48,768]{2,1,0:T(8,128)(2,1)S(1)}, u32[]{:S(2)}, u32[]{:S(2)}) collective-permute-start(bf16[2,48,768]{2,1,0:T(8,128)(2,1)S(1)} %pad_maximum_fusion.11), channel_id=1, source_target_pairs={{0,128},{128,0},{1,129},{129,1},{2,130},{130,2},{3,131},{131,3},{4... | collective-permute-start | bytes 442376 | tf_op jit(solution)/shard_map/ppermute | solution.py:70
  7.3 11.8 %collective-permute-start = (bf16[96,384]{1,0:T(8,128)(2,1)}, bf16[96,384]{1,0:T(8,128)(2,1)S(1)}, u32[]{:S(2)}, u32[]{:S(2)}) collective-permute-start(bf16[96,384]{1,0:T(8,128)(2,1)} %get-tuple-element.13), channel_id=1, source_target_pairs={{0,12},{4,0},{8,4},{12,8},{16,28},{20,16},{24,20},{28,24},{32,44},... | collective-permute-start | bytes 221192 | tf_op jit(solution)/shard_map/ppermute | solution.py:58
  8.2 11.1 %collective-permute-start.1 = (bf16[96,384]{1,0:T(8,128)(2,1)}, bf16[96,384]{1,0:T(8,128)(2,1)S(1)}, u32[]{:S(2)}, u32[]{:S(2)}) collective-permute-start(bf16[96,384]{1,0:T(8,128)(2,1)} %get-tuple-element.14), channel_id=1, source_target_pairs={{0,240},{4,244},{8,248},{12,252},{16,0},{20,4},{24,8},{28,12},{32,... | collective-permute-start | bytes 221192 | tf_op jit(solution)/shard_map/ppermute | solution.py:58
  13.7 5.6 %collective-permute-start.2 = (bf16[96,384]{1,0:T(8,128)(2,1)}, bf16[96,384]{1,0:T(8,128)(2,1)S(1)}, u32[]{:S(2)}, u32[]{:S(2)}) collective-permute-start(bf16[96,384]{1,0:T(8,128)(2,1)} %get-tuple-element.15), channel_id=1, source_target_pairs={{0,252},{4,240},{8,244},{12,248},{16,12},{20,0},{24,4},{28,8},{32,... | collective-permute-start | bytes 221192 | tf_op jit(solution)/shard_map/ppermute | solution.py:58
  16.9 10.1 %collective-permute-start.9 = (bf16[2,2,48,768]{3,2,1,0:T(8,128)(2,1)S(1)}, bf16[2,2,48,768]{3,2,1,0:T(8,128)(2,1)}, u32[]{:S(2)}, u32[]{:S(2)}) collective-permute-start(bf16[2,2,48,768]{3,2,1,0:T(8,128)(2,1)S(1)} %get-tuple-element.50), channel_id=1, source_target_pairs={{0,112},{16,0},{32,16},{48,32},{64,48},{80,64},{96,80},{112,96},{1... | collective-permute-start | bytes 884744 | tf_op jit(solution)/shard_map/ppermute | solution.py:74
  17.0 14.2 %collective-permute-start.10 = (bf16[2,2,48,768]{3,2,1,0:T(8,128)(2,1)S(1)}, bf16[2,2,48,768]{3,2,1,0:T(8,128)(2,1)}, u32[]{:S(2)}, u32[]{:S(2)}) collective-permute-start(bf16[2,2,48,768]{3,2,1,0:T(8,128)(2,1)S(1)} %get-tuple-element.50), channel_id=1, source_target_pairs={{0,16},{16,32},{32,48},{48,64},{64,80},{80,96},{96,112},{112,0},{1... | collective-permute-start | bytes 884744 | tf_op jit(solution)/shard_map/ppermute | solution.py:74
  19.1 0.6 copy-start.4
  19.1 32.9 %collective-permute-start.3 = (bf16[192,1536]{1,0:T(8,128)(2,1)S(1)}, bf16[192,1536]{1,0:T(8,128)(2,1)}, u32[]{:S(2)}, u32[]{:S(2)}) collective-permute-start(bf16[192,1536]{1,0:T(8,128)(2,1)S(1)} %bitcast.103), channel_id=1, source_target_pairs={{0,4},{4,0},{1,5},{5,1},{2,6},{6,2},{3,7},{7,3},{8,12},{12,8},{9,1... | collective-permute-start | bytes 1769480 | tf_op jit(solution)/shard_map/ppermute | solution.py:62
  19.4 0.6 copy-start.5
  19.4 14.6 %collective-permute-start.4 = (bf16[192,1536]{1,0:T(8,128)(2,1)S(1)}, bf16[192,1536]{1,0:T(8,128)(2,1)}, u32[]{:S(2)}, u32[]{:S(2)}) collective-permute-start(bf16[192,1536]{1,0:T(8,128)(2,1)S(1)} %bitcast.104), channel_id=1, source_target_pairs={{0,8},{8,0},{1,9},{9,1},{2,10},{10,2},{3,11},{11,3},{4,12},{12,4},... | collective-permute-start | bytes 1769480 | tf_op jit(solution)/shard_map/ppermute | solution.py:66
  19.4 0.6 copy-start.6
  27.0 10.6 %collective-permute-start.11 = (bf16[2,2,48,768]{3,2,1,0:T(8,128)(2,1)}, bf16[2,2,48,768]{3,2,1,0:T(8,128)(2,1)S(1)}, u32[]{:S(2)}, u32[]{:S(2)}) collective-permute-start(bf16[2,2,48,768]{3,2,1,0:T(8,128)(2,1)} %collective-permute-done.9), channel_id=1, source_target_pairs={{0,112},{16,0},{32,16},{48,32},{64,48},{80,64},{96,80},{112,96},{1... | collective-permute-start | bytes 884744 | tf_op jit(solution)/shard_map/ppermute | solution.py:74
  31.2 9.6 %collective-permute-start.12 = (bf16[2,2,48,768]{3,2,1,0:T(8,128)(2,1)}, bf16[2,2,48,768]{3,2,1,0:T(8,128)(2,1)S(1)}, u32[]{:S(2)}, u32[]{:S(2)}) collective-permute-start(bf16[2,2,48,768]{3,2,1,0:T(8,128)(2,1)} %collective-permute-done.10), channel_id=1, source_target_pairs={{0,16},{16,32},{32,48},{48,64},{64,80},{80,96},{96,112},{112,0},{1... | collective-permute-start | bytes 884744 | tf_op jit(solution)/shard_map/ppermute | solution.py:74
  34.0 18.0 %collective-permute-start.5 = (bf16[192,1536]{1,0:T(8,128)(2,1)}, bf16[192,1536]{1,0:T(8,128)(2,1)}, u32[]{:S(2)}, u32[]{:S(2)}) collective-permute-start(bf16[192,1536]{1,0:T(8,128)(2,1)} %collective-permute-done.4.near_ref), channel_id=1, source_target_pairs={{0,4},{4,0},{1,5},{5,1},{2,6},{6,2},{3,7},{7,3},{8,12},{12,8},{9,1... | collective-permute-start | bytes 1769480 | tf_op jit(solution)/shard_map/ppermute | solution.py:62
  37.5 11.7 %collective-permute-start.13 = (bf16[2,2,48,768]{3,2,1,0:T(8,128)(2,1)S(1)}, bf16[2,2,48,768]{3,2,1,0:T(8,128)(2,1)S(1)}, u32[]{:S(2)}, u32[]{:S(2)}) collective-permute-start(bf16[2,2,48,768]{3,2,1,0:T(8,128)(2,1)S(1)} %collective-permute-done.11), channel_id=1, source_target_pairs={{0,112},{16,0},{32,16},{48,32},{64,48},{80,64},{96,80},{112,96},{1... | collective-permute-start | bytes 884744 | tf_op jit(solution)/shard_map/ppermute | solution.py:74
  40.8 8.3 %collective-permute-start.14 = (bf16[2,2,48,768]{3,2,1,0:T(8,128)(2,1)S(1)}, bf16[2,2,48,768]{3,2,1,0:T(8,128)(2,1)S(1)}, u32[]{:S(2)}, u32[]{:S(2)}) collective-permute-start(bf16[2,2,48,768]{3,2,1,0:T(8,128)(2,1)S(1)} %collective-permute-done.12), channel_id=1, source_target_pairs={{0,16},{16,32},{32,48},{48,64},{64,80},{80,96},{96,112},{112,0},{1... | collective-permute-start | bytes 884744 | tf_op jit(solution)/shard_map/ppermute | solution.py:74
  49.1 6.4 %collective-permute-start.16 = (bf16[2,48,768]{2,1,0:T(8,128)(2,1)S(1)}, bf16[2,48,768]{2,1,0:T(8,128)(2,1)S(1)}, u32[]{:S(2)}, u32[]{:S(2)}) collective-permute-start(bf16[2,48,768]{2,1,0:T(8,128)(2,1)S(1)} %slice_bitcast_fusion.2), channel_id=1, source_target_pairs={{0,16},{16,32},{32,48},{48,64},{64,80},{80,96},{96,112},{112,0},{1... | collective-permute-start | bytes 442376 | tf_op jit(solution)/shard_map/ppermute | solution.py:74
  49.2 6.3 %collective-permute-start.15 = (bf16[2,48,768]{2,1,0:T(8,128)(2,1)S(1)}, bf16[2,48,768]{2,1,0:T(8,128)(2,1)S(1)}, u32[]{:S(2)}, u32[]{:S(2)}) collective-permute-start(bf16[2,48,768]{2,1,0:T(8,128)(2,1)S(1)} %slice_bitcast_fusion.3), channel_id=1, source_target_pairs={{0,112},{16,0},{32,16},{48,32},{64,48},{80,64},{96,80},{112,96},{1... | collective-permute-start | bytes 442376 | tf_op jit(solution)/shard_map/ppermute | solution.py:74
  55.6 3.7 %collective-permute-start.6 = (bf16[64,768]{1,0:T(8,128)(2,1)}, bf16[64,768]{1,0:T(8,128)(2,1)S(1)}, u32[]{:S(2)}, u32[]{:S(2)}) collective-permute-start(bf16[64,768]{1,0:T(8,128)(2,1)} %get-tuple-element.18), channel_id=1, source_target_pairs={{0,8},{8,0},{1,9},{9,1},{2,10},{10,2},{3,11},{11,3},{4,12},{12,4},... | collective-permute-start | bytes 294920 | tf_op jit(solution)/shard_map/ppermute | solution.py:66
  55.6 3.6 %copy-start.2 = (bf16[64,768]{1,0:T(8,128)(2,1)S(1)}, bf16[64,768]{1,0:T(8,128)(2,1)}, u32[]{:S(2)}) copy-start(bf16[64,768]{1,0:T(8,128)(2,1)} %get-tuple-element.18) | copy-start | bytes 294916
  59.3 5.2 %collective-permute-start.7 = (bf16[128,768]{1,0:T(8,128)(2,1)S(1)}, bf16[128,768]{1,0:T(8,128)(2,1)S(1)}, u32[]{:S(2)}, u32[]{:S(2)}) collective-permute-start(bf16[128,768]{1,0:T(8,128)(2,1)S(1)} %pad_maximum_fusion.3), channel_id=1, source_target_pairs={{0,4},{4,0},{1,5},{5,1},{2,6},{6,2},{3,7},{7,3},{8,12},{12,8},{9,1... | collective-permute-start | bytes 589832 | tf_op jit(solution)/shard_map/ppermute | solution.py:62
  66.9 6.6 %copy-start = (bf16[64,768]{1,0:T(8,128)(2,1)S(1)}, bf16[64,768]{1,0:T(8,128)(2,1)}, u32[]{:S(2)}) copy-start(bf16[64,768]{1,0:T(8,128)(2,1)} %get-tuple-element.19) | copy-start | bytes 294916
  66.9 6.8 %copy-start.3 = (f32[64,768]{1,0:T(8,128)S(1)}, f32[64,768]{1,0:T(8,128)}, u32[]{:S(2)}) copy-start(f32[64,768]{1,0:T(8,128)} %get-tuple-element.17) | copy-start | bytes 589828
  67.5 1.5 %collective-permute-start.17 = (bf16[128,768]{1,0:T(8,128)(2,1)S(1)}, bf16[128,768]{1,0:T(8,128)(2,1)S(1)}, u32[]{:S(2)}, u32[]{:S(2)}) collective-permute-start(bf16[128,768]{1,0:T(8,128)(2,1)S(1)} %slice.121), channel_id=1, source_target_pairs={{0,4},{4,0},{1,5},{5,1},{2,6},{6,2},{3,7},{7,3},{8,12},{12,8},{9,1... | collective-permute-start | bytes 589832 | tf_op jit(solution)/shard_map/ppermute | solution.py:62
  69.1 4.1 %collective-permute-start.18 = (bf16[64,768]{1,0:T(8,128)(2,1)S(1)}, bf16[64,768]{1,0:T(8,128)(2,1)S(1)}, u32[]{:S(2)}, u32[]{:S(2)}) collective-permute-start(bf16[64,768]{1,0:T(8,128)(2,1)S(1)} %slice.221), channel_id=1, source_target_pairs={{0,8},{8,0},{1,9},{9,1},{2,10},{10,2},{3,11},{11,3},{4,12},{12,4},... | collective-permute-start | bytes 294920 | tf_op jit(solution)/shard_map/ppermute | solution.py:66
  73.9 3.6 %collective-permute-start.19 = (bf16[64,768]{1,0:T(8,128)(2,1)S(1)}, bf16[64,768]{1,0:T(8,128)(2,1)S(1)}, u32[]{:S(2)}, u32[]{:S(2)}) collective-permute-start(bf16[64,768]{1,0:T(8,128)(2,1)S(1)} %get-tuple-element.43), channel_id=1, source_target_pairs={{0,8},{8,0},{1,9},{9,1},{2,10},{10,2},{3,11},{11,3},{4,12},{12,4},... | collective-permute-start | bytes 294920 | tf_op jit(solution)/shard_map/ppermute | solution.py:66
  77.4 3.5 %collective-permute-start.20 = (bf16[128,768]{1,0:T(8,128)(2,1)S(1)}, bf16[128,768]{1,0:T(8,128)(2,1)S(1)}, u32[]{:S(2)}, u32[]{:S(2)}) collective-permute-start(bf16[128,768]{1,0:T(8,128)(2,1)S(1)} %pad_maximum_fusion.4), channel_id=1, source_target_pairs={{0,4},{4,0},{1,5},{5,1},{2,6},{6,2},{3,7},{7,3},{8,12},{12,8},{9,1... | collective-permute-start | bytes 589832 | tf_op jit(solution)/shard_map/ppermute | solution.py:62
  83.0 6.3 %collective-permute-start.30 = (bf16[2,48,768]{2,1,0:T(8,128)(2,1)S(1)}, bf16[2,48,768]{2,1,0:T(8,128)(2,1)S(1)}, u32[]{:S(2)}, u32[]{:S(2)}) collective-permute-start(bf16[2,48,768]{2,1,0:T(8,128)(2,1)S(1)} %get-tuple-element.49), channel_id=1, source_target_pairs={{0,16},{16,32},{32,48},{48,64},{64,80},{80,96},{96,112},{112,0},{1... | collective-permute-start | bytes 442376 | tf_op jit(solution)/shard_map/ppermute | solution.py:74
  83.6 9.8 %collective-permute-start.21 = (bf16[128,768]{1,0:T(8,128)(2,1)S(1)}, bf16[128,768]{1,0:T(8,128)(2,1)S(1)}, u32[]{:S(2)}, u32[]{:S(2)}) collective-permute-start(bf16[128,768]{1,0:T(8,128)(2,1)S(1)} %slice.125), channel_id=1, source_target_pairs={{0,4},{4,0},{1,5},{5,1},{2,6},{6,2},{3,7},{7,3},{8,12},{12,8},{9,1... | collective-permute-start | bytes 589832 | tf_op jit(solution)/shard_map/ppermute | solution.py:62
  84.1 5.8 %collective-permute-start.26 = (bf16[2,48,768]{2,1,0:T(8,128)(2,1)S(1)}, bf16[2,48,768]{2,1,0:T(8,128)(2,1)S(1)}, u32[]{:S(2)}, u32[]{:S(2)}) collective-permute-start(bf16[2,48,768]{2,1,0:T(8,128)(2,1)S(1)} %get-tuple-element.48), channel_id=1, source_target_pairs={{0,112},{16,0},{32,16},{48,32},{64,48},{80,64},{96,80},{112,96},{1... | collective-permute-start | bytes 442376 | tf_op jit(solution)/shard_map/ppermute | solution.py:74
  89.4 8.6 %collective-permute-start.31 = (bf16[2,2,48,768]{3,2,1,0:T(8,128)(2,1)S(1)}, bf16[2,2,48,768]{3,2,1,0:T(8,128)(2,1)S(1)}, u32[]{:S(2)}, u32[]{:S(2)}) collective-permute-start(bf16[2,2,48,768]{3,2,1,0:T(8,128)(2,1)S(1)} %pad_maximum_fusion.2), channel_id=1, source_target_pairs={{0,16},{16,32},{32,48},{48,64},{64,80},{80,96},{96,112},{112,0},{1... | collective-permute-start | bytes 884744 | tf_op jit(solution)/shard_map/ppermute | solution.py:74
  90.0 8.7 %collective-permute-start.27 = (bf16[2,2,48,768]{3,2,1,0:T(8,128)(2,1)S(1)}, bf16[2,2,48,768]{3,2,1,0:T(8,128)(2,1)S(1)}, u32[]{:S(2)}, u32[]{:S(2)}) collective-permute-start(bf16[2,2,48,768]{3,2,1,0:T(8,128)(2,1)S(1)} %fusion.9), channel_id=1, source_target_pairs={{0,112},{16,0},{32,16},{48,32},{64,48},{80,64},{96,80},{112,96},{1... | collective-permute-start | bytes 884744 | tf_op jit(solution)/shard_map/ppermute | solution.py:74
  93.5 8.7 %collective-permute-start.22 = (bf16[64,768]{1,0:T(8,128)(2,1)S(1)}, bf16[64,768]{1,0:T(8,128)(2,1)S(1)}, u32[]{:S(2)}, u32[]{:S(2)}) collective-permute-start(bf16[64,768]{1,0:T(8,128)(2,1)S(1)} %slice.220), channel_id=1, source_target_pairs={{0,8},{8,0},{1,9},{9,1},{2,10},{10,2},{3,11},{11,3},{4,12},{12,4},... | collective-permute-start | bytes 294920 | tf_op jit(solution)/shard_map/ppermute | solution.py:66
  98.1 7.8 %collective-permute-start.32 = (bf16[2,2,48,768]{3,2,1,0:T(8,128)(2,1)S(1)}, bf16[2,2,48,768]{3,2,1,0:T(8,128)(2,1)S(1)}, u32[]{:S(2)}, u32[]{:S(2)}) collective-permute-start(bf16[2,2,48,768]{3,2,1,0:T(8,128)(2,1)S(1)} %maximum_add_fusion.2), channel_id=1, source_target_pairs={{0,16},{16,32},{32,48},{48,64},{64,80},{80,96},{96,112},{112,0},{1... | collective-permute-start | bytes 884744 | tf_op jit(solution)/shard_map/ppermute | solution.py:74
  98.7 7.8 %collective-permute-start.28 = (bf16[2,2,48,768]{3,2,1,0:T(8,128)(2,1)S(1)}, bf16[2,2,48,768]{3,2,1,0:T(8,128)(2,1)S(1)}, u32[]{:S(2)}, u32[]{:S(2)}) collective-permute-start(bf16[2,2,48,768]{3,2,1,0:T(8,128)(2,1)S(1)} %maximum_add_fusion), channel_id=1, source_target_pairs={{0,112},{16,0},{32,16},{48,32},{64,48},{80,64},{96,80},{112,96},{1... | collective-permute-start | bytes 884744 | tf_op jit(solution)/shard_map/ppermute | solution.py:74
  105.9 16.2 %collective-permute-start.33 = (bf16[2,2,48,768]{3,2,1,0:T(8,128)(2,1)S(1)}, bf16[2,2,48,768]{3,2,1,0:T(8,128)(2,1)S(1)}, u32[]{:S(2)}, u32[]{:S(2)}) collective-permute-start(bf16[2,2,48,768]{3,2,1,0:T(8,128)(2,1)S(1)} %maximum_add_fusion.3), channel_id=1, source_target_pairs={{0,16},{16,32},{32,48},{48,64},{64,80},{80,96},{96,112},{112,0},{1... | collective-permute-start | bytes 884744 | tf_op jit(solution)/shard_map/ppermute | solution.py:74
  106.6 15.5 %collective-permute-start.29 = (bf16[2,2,48,768]{3,2,1,0:T(8,128)(2,1)S(1)}, bf16[2,2,48,768]{3,2,1,0:T(8,128)(2,1)S(1)}, u32[]{:S(2)}, u32[]{:S(2)}) collective-permute-start(bf16[2,2,48,768]{3,2,1,0:T(8,128)(2,1)S(1)} %maximum_add_fusion.1), channel_id=1, source_target_pairs={{0,112},{16,0},{32,16},{48,32},{64,48},{80,64},{96,80},{112,96},{1... | collective-permute-start | bytes 884744 | tf_op jit(solution)/shard_map/ppermute | solution.py:74
  110.1 4.3 %collective-permute-start.25 = (bf16[16,1536]{1,0:T(8,128)(2,1)S(1)}, bf16[16,1536]{1,0:T(8,128)(2,1)S(1)}, u32[]{:S(2)}, u32[]{:S(2)}) collective-permute-start(bf16[16,1536]{1,0:T(8,128)(2,1)S(1)} %get-tuple-element.57), channel_id=1, source_target_pairs={{0,4},{4,8},{8,12},{12,0},{16,20},{20,24},{24,28},{28,16},{32,36},... | collective-permute-start | bytes 147464 | tf_op jit(solution)/shard_map/ppermute | solution.py:58
  113.2 6.6 %collective-permute-start.24 = (bf16[16,1536]{1,0:T(8,128)(2,1)S(1)}, bf16[16,1536]{1,0:T(8,128)(2,1)S(1)}, u32[]{:S(2)}, u32[]{:S(2)}) collective-permute-start(bf16[16,1536]{1,0:T(8,128)(2,1)S(1)} %get-tuple-element.55), channel_id=1, source_target_pairs={{0,16},{4,20},{8,24},{12,28},{16,32},{20,36},{24,40},{28,44},{32,4... | collective-permute-start | bytes 147464 | tf_op jit(solution)/shard_map/ppermute | solution.py:58
  113.2 8.5 %collective-permute-start.23 = (bf16[16,1536]{1,0:T(8,128)(2,1)S(1)}, bf16[16,1536]{1,0:T(8,128)(2,1)S(1)}, u32[]{:S(2)}, u32[]{:S(2)}) collective-permute-start(bf16[16,1536]{1,0:T(8,128)(2,1)S(1)} %get-tuple-element.54), channel_id=1, source_target_pairs={{0,20},{4,24},{8,28},{12,16},{16,36},{20,40},{24,44},{28,32},{32,5... | collective-permute-start | bytes 147464 | tf_op jit(solution)/shard_map/ppermute | solution.py:58
  122.2 6.2 %collective-permute-start.34 = (bf16[2,48,768]{2,1,0:T(8,128)(2,1)S(1)}, bf16[2,48,768]{2,1,0:T(8,128)(2,1)S(1)}, u32[]{:S(2)}, u32[]{:S(2)}) collective-permute-start(bf16[2,48,768]{2,1,0:T(8,128)(2,1)S(1)} %fusion.17), channel_id=1, source_target_pairs={{0,128},{128,0},{1,129},{129,1},{2,130},{130,2},{3,131},{131,3},{4... | collective-permute-start | bytes 442376 | tf_op jit(solution)/shard_map/ppermute | solution.py:70
where the time goes:
time: 130 us; the launch traced here: 129 us
  starting transfers between devices  51.9 us (40%)
  waiting for transfers between devices  49.5 us (38%)
  Pallas kernels  12.2 us (9%)
  local copies, waits for them, and re-layouts  5.36 us (4%)
  matrix products  5.06 us (4%)
  other arithmetic  4.02 us (3%)
    ppermute x16, starting transfers between devices, along_z(): return lax.ppermute(array, 'z', [(i, (i + step) % NZ) for i in range(NZ)])  25.6 us
    ppermute x16, waiting for transfers between devices, along_z(): return lax.ppermute(array, 'z', [(i, (i + step) % NZ) for i in range(NZ)])  22.3 us
    ppermute x6, starting transfers between devices, to_grid(): return lax.ppermute(array, GRID, pairs)  11.8 us
    ppermute x5, waiting for transfers between devices, swap_xl(): return lax.ppermute(array, 'xl', [(0, 1), (1, 0)])  11.3 us
    ppermute x6, starting transfers between devices, swap_core(): return lax.ppermute(array, 'core', [(0, 1), (1, 0)])  9 us
    ppermute x6, waiting for transfers between devices, to_grid(): return lax.ppermute(array, GRID, pairs)  8.49 us
    pallas_call x1, Pallas kernels, whole_step(): pl.pallas_call(window_kernel, out_shape=[jax.ShapeDtypeStruct((own, 4 * c...  6.72 us
    ppermute x2, starting transfers between devices, swap_half(): return lax.ppermute(array, 'xh', [(0, 1), (1, 0)])  4.93 us
  transfers between devices with their start and end apart: 35, of which 19 were waited for; matrix products, arithmetic and copies ran while one was open for 5% of the time, Pallas kernels for 9%

commit v1 on v0

--- a/solution.py
+++ b/solution.py
@@ -74,9 +74,19 @@
     return lax.ppermute(array, "z", [(i, (i + step) % NZ) for i in range(NZ)])
 
 
+def across_z(array, step):
+    pairs = []
+    for h in range(NX):
+        for i in range(NZ):
+            pairs.append((h * NZ + i, (1 - h) * NZ + (i + step) % NZ))
+    return lax.ppermute(array, ROWS, pairs)
+
+
 def gather_cols(rows):
-    near = jnp.concatenate([rows, swap_xl(rows)], axis=0)
-    return jnp.concatenate([near, swap_core(near)], axis=0)
+    other = swap_xl(rows)
+    near = jnp.concatenate([rows, other], axis=0)
+    across = swap_core(near)
+    return jnp.concatenate([near, across], axis=0)
 
 
 def scatter_cols(rows):
@@ -114,6 +124,8 @@
     def block(k):
         return jnp.stack([lax.dynamic_index_in_dim(b, (z + k) % NZ, 1, False) for b in blocks], 1)
 
+    own = block(0)
+    own_other = swap_half(jnp.where(lax.axis_index("xh") == 0, own[1], own[0]))
     far = block(4)
     left, right = along_z(far[0], -1), along_z(far[1], 1)
     near_left, near_right = block(NZ - 3), block(3)
@@ -122,11 +134,20 @@
     for k in (2, 1):
         left, right = along_z(left, -1), along_z(right, 1)
         left, right = left + block(NZ - k), right + block(k)
-    left, right = along_z(left, -1), along_z(right, 1)
-    both = left.astype(F32) + right.astype(F32) + block(0).astype(F32)
     first = lax.axis_index("xh") == 0
-    other = swap_half(jnp.where(first, both[1], both[0]).astype(BF))
-    return jnp.where(first, both[0], both[1]) + other.astype(F32)
+
+    def mine(v):
+        return jnp.where(first, v[0], v[1])
+
+    def theirs(v):
+        return jnp.where(first, v[1], v[0])
+
+    near = [along_z(mine(left), -1), along_z(mine(right), 1)]
+    cross = [across_z(theirs(left), -1), across_z(theirs(right), 1)]
+    total = mine(own).astype(F32) + own_other.astype(F32)
+    for part in near + cross:
+        total = total + part.astype(F32)
+    return total
 
 
 def order_kernel(fields_ref, cot_ref, *outs):
@@ -179,10 +200,10 @@
         cot_ref[k * 16 : (k + 1) * 16, channels:] = quads[k][80:]
 
 
-def level_kernel(merged_ref, own_ref, core_ref, near_ref, far_ref, place_ref, level_ref, bf_ref):
+def level_kernel(merged_ref, own_ref, core_ref, near_ref, far_ref, level_ref, bf_ref):
     merged = merged_ref[...]
     parts = [dot_nt(merged, r[...]) for r in (own_ref, core_ref, near_ref, far_ref)]
-    xl, core = place_ref[0] == 0, place_ref[1] == 0
+    xl, core = lax.axis_index("xl") == 0, lax.axis_index("core") == 0
     low = [jnp.where(xl, parts[k], parts[k + 2]) for k in (0, 1)]
     high = [jnp.where(xl, parts[k + 2], parts[k]) for k in (0, 1)]
     ordered = []
@@ -252,18 +273,22 @@
             bytes_accessed=2_000_000,
         ),
         name="window",
-    )(logit_scale, *x, w_qkv, w_proj)
-    place = jnp.stack([lax.axis_index("xl"), lax.axis_index("core")])
+    )(
+        logit_scale,
+        *x,
+        pltpu.with_memory_space_constraint(w_qkv, pltpu.VMEM),
+        pltpu.with_memory_space_constraint(w_proj, pltpu.VMEM),
+    )
     level, level_own = pl.pallas_call(
         level_kernel,
         out_shape=[jax.ShapeDtypeStruct((own, wide), F32), jax.ShapeDtypeStruct((own, wide), BF)],
-        in_specs=whole(5) + [pl.BlockSpec(memory_space=pltpu.SMEM)],
+        in_specs=whole(5),
         out_specs=whole(2),
         cost_estimate=pl.CostEstimate(
             flops=8 * own * channels * wide, transcendentals=own, bytes_accessed=3_000_000
         ),
         name="level",
-    )(merged, merge_own, merge_core, merge_near, merge_far, place)
+    )(merged, merge_own, merge_core, merge_near, merge_far)
     level_b = gather_cols(level_own)
 
     hidden_pre = dot(level_b, up_full)

time: 130 us -> 127 us (0.977)
  starting transfers between devices: 51.9 us -> 48.5 us
    ppermute x16, starting transfers between devices: 25.6 us -> 20.6 us  [along_z(): return lax.ppermute(array, 'z', [(i, (i + step) % NZ) for i in range(NZ)])]
    ppermute x2, waiting for transfers between devices: 4.1 us -> 0.01 us  [swap_half(): return lax.ppermute(array, 'xh', [(0, 1), (1, 0)])]
    ppermute x0 -> x2, starting transfers between devices: none -> 3.05 us  [across_z(): return lax.ppermute(array, ROWS, pairs)]
    ppermute x0 -> x2, waiting for transfers between devices: none -> 2.08 us  [across_z(): return lax.ppermute(array, ROWS, pairs)]
    ppermute x16, waiting for transfers between devices: 22.3 us -> 23.7 us  [along_z(): return lax.ppermute(array, 'z', [(i, (i + step) % NZ) for i in range(NZ)])]
  transfers between devices with their start and end apart: 35 -> 37, of which waited for: 19 -> 20; matrix products, arithmetic and copies ran while one was open for 5% -> 5% of each run, Pallas kernels for 9% -> 9%
where the time goes in v1:
time: 127 us; the launch traced here: 126 us
  waiting for transfers between devices  48.8 us (38%)
  starting transfers between devices  48.5 us (38%)
  Pallas kernels  11.8 us (9%)
  local copies, waits for them, and re-layouts  5.36 us (4%)
  matrix products  5.06 us (4%)
  other arithmetic  5.01 us (4%)
    ppermute x16, waiting for transfers between devices, along_z(): return lax.ppermute(array, 'z', [(i, (i + step) % NZ) for i in range(NZ)])  23.7 us
    ppermute x16, starting transfers between devices, along_z(): return lax.ppermute(array, 'z', [(i, (i + step) % NZ) for i in range(NZ)])  20.6 us
    ppermute x5, waiting for transfers between devices, swap_xl(): return lax.ppermute(array, 'xl', [(0, 1), (1, 0)])  12.2 us
    ppermute x6, starting transfers between devices, to_grid(): return lax.ppermute(array, GRID, pairs)  11 us
    ppermute x6, starting transfers between devices, swap_core(): return lax.ppermute(array, 'core', [(0, 1), (1, 0)])  9 us
    ppermute x6, waiting for transfers between devices, to_grid(): return lax.ppermute(array, GRID, pairs)  7.6 us
    pallas_call x1, Pallas kernels, whole_step(): pl.pallas_call(window_kernel, out_shape=[jax.ShapeDtypeStruct((own, 4 * c...  6.34 us
    ppermute x2, starting transfers between devices, swap_half(): return lax.ppermute(array, 'xh', [(0, 1), (1, 0)])  4.23 us
  transfers between devices with their start and end apart: 37, of which 20 were waited for; matrix products, arithmetic and copies ran while one was open for 5% of the time, Pallas kernels for 9%

profile of v1, /device:TPU:1, one launch (start us, length us, event | category | flops | bytes accessed | tf_op | source)
XLA Modules:
  0.0 125.8 jit_solution(614889356887939450)
XLA Ops:
  0.7 1.1 pad_maximum_fusion.12
  1.7 3.6 %collective-permute-start.8 = (bf16[2,48,768]{2,1,0:T(8,128)(2,1)S(1)}, bf16[2,48,768]{2,1,0:T(8,128)(2,1)S(1)}, u32[]{:S(2)}, u32[]{:S(2)}) collective-permute-start(bf16[2,48,768]{2,1,0:T(8,128)(2,1)S(1)} %pad_maximum_fusion.12), channel_id=1, source_target_pairs={{0,128},{128,0},{1,129},{129,1},{2,130},{130,2},{3,131},{131,3},{4... | collective-permute-start | bytes 442376 | tf_op jit(solution)/shard_map/ppermute | solution.py:70
  5.4 2.0 %order.1 = (bf16[96,384]{1,0:T(8,128)(2,1)}, bf16[96,384]{1,0:T(8,128)(2,1)}, bf16[96,384]{1,0:T(8,128)(2,1)}, bf16[96,384]{1,0:T(8,128)(2,1)}) custom-call(f32[256,384]{1,0:T(8,128)} %bitcast.112, bf16[64,768]{1,0:T(8,128)(2,1)} %bitcast.119), custom_call_target="tpu_custom_call" | custom-call | tf_op jit(solution)/shard_map/order/pallas_call | solution.py:227
  7.4 1.0 collective-permute-start
  8.3 5.5 %collective-permute-start.1 = (bf16[96,384]{1,0:T(8,128)(2,1)}, bf16[96,384]{1,0:T(8,128)(2,1)S(1)}, u32[]{:S(2)}, u32[]{:S(2)}) collective-permute-start(bf16[96,384]{1,0:T(8,128)(2,1)} %get-tuple-element.14), channel_id=1, source_target_pairs={{0,240},{4,244},{8,248},{12,252},{16,0},{20,4},{24,8},{28,12},{32,... | collective-permute-start | bytes 221192 | tf_op jit(solution)/shard_map/ppermute | solution.py:58
  13.8 2.1 %collective-permute-start.2 = (bf16[96,384]{1,0:T(8,128)(2,1)}, bf16[96,384]{1,0:T(8,128)(2,1)S(1)}, u32[]{:S(2)}, u32[]{:S(2)}) collective-permute-start(bf16[96,384]{1,0:T(8,128)(2,1)} %get-tuple-element.15), channel_id=1, source_target_pairs={{0,252},{4,240},{8,244},{12,248},{16,12},{20,0},{24,4},{28,8},{32,... | collective-permute-start | bytes 221192 | tf_op jit(solution)/shard_map/ppermute | solution.py:58
  16.0 0.9 select_bitcast_fusion.6
  17.1 1.5 %collective-permute-start.10 = (bf16[2,2,48,768]{3,2,1,0:T(8,128)(2,1)S(1)}, bf16[2,2,48,768]{3,2,1,0:T(8,128)(2,1)}, u32[]{:S(2)}, u32[]{:S(2)}) collective-permute-start(bf16[2,2,48,768]{3,2,1,0:T(8,128)(2,1)S(1)} %get-tuple-element.54), channel_id=1, source_target_pairs={{0,16},{16,32},{32,48},{48,64},{64,80},{80,96},{96,112},{112,0},{1... | collective-permute-start | bytes 884744 | tf_op jit(solution)/shard_map/ppermute | solution.py:74
  19.8 6.3 %window.1 = (bf16[64,1536]{1,0:T(8,128)(2,1)}, bf16[64,768]{1,0:T(8,128)(2,1)}) custom-call(f32[6]{0:T(128)} %scale_ref.1, bf16[96,384]{1,0:T(8,128)(2,1)} %get-tuple-element.12.x0, bf16[96,384]{1,0:T(8,128)(2,1)} %copy-done.6, bf16[96,384]{1,0:T(8,128)(2,1)} %copy-done.7, bf16[96,384]{1,0:T(8,128)(2,1)} %copy-done.8, bf16[384,1152]{1,0:T(8,128)(2,1)S(1)} %copy-done, ...), custom_call_target="tpu_custom_call" | custom-call | flops 402653184 | bytes 2000000 | tf_op jit(solution)/shard_map/window/pallas_call | solution.py:262
  26.3 4.6 %collective-permute-start.11 = (bf16[2,2,48,768]{3,2,1,0:T(8,128)(2,1)}, bf16[2,2,48,768]{3,2,1,0:T(8,128)(2,1)S(1)}, u32[]{:S(2)}, u32[]{:S(2)}) collective-permute-start(bf16[2,2,48,768]{3,2,1,0:T(8,128)(2,1)} %collective-permute-done.9), channel_id=1, source_target_pairs={{0,112},{16,0},{32,16},{48,32},{64,48},{80,64},{96,80},{112,96},{1... | collective-permute-start | bytes 884744 | tf_op jit(solution)/shard_map/ppermute | solution.py:74
  30.9 1.0 copy_dynamic-update-slice_fusion.5
  31.9 1.0 copy_dynamic-update-slice_fusion.4
  33.4 1.2 collective-permute-start.5
  34.6 2.6 %collective-permute-done.11 = bf16[2,2,48,768]{3,2,1,0:T(8,128)(2,1)S(1)} collective-permute-done((bf16[2,2,48,768]{3,2,1,0:T(8,128)(2,1)}, bf16[2,2,48,768]{3,2,1,0:T(8,128)(2,1)S(1)}, u32[]{:S(2)}, u32[]{:S(2)}) %collective-permute-start.11) | collective-permute-done | bytes 294944 | tf_op jit(solution)/shard_map/ppermute | solution.py:74
  37.2 3.3 %collective-permute-start.13 = (bf16[2,2,48,768]{3,2,1,0:T(8,128)(2,1)S(1)}, bf16[2,2,48,768]{3,2,1,0:T(8,128)(2,1)S(1)}, u32[]{:S(2)}, u32[]{:S(2)}) collective-permute-start(bf16[2,2,48,768]{3,2,1,0:T(8,128)(2,1)S(1)} %collective-permute-done.11), channel_id=1, source_target_pairs={{0,112},{16,0},{32,16},{48,32},{64,48},{80,64},{96,80},{112,96},{1... | collective-permute-start | bytes 884744 | tf_op jit(solution)/shard_map/ppermute | solution.py:74
  40.6 8.2 %collective-permute-done.14 = bf16[2,2,48,768]{3,2,1,0:T(8,128)(2,1)S(1)} collective-permute-done((bf16[2,2,48,768]{3,2,1,0:T(8,128)(2,1)S(1)}, bf16[2,2,48,768]{3,2,1,0:T(8,128)(2,1)S(1)}, u32[]{:S(2)}, u32[]{:S(2)}) %collective-permute-start.14) | collective-permute-done | bytes 294944 | tf_op jit(solution)/shard_map/ppermute | solution.py:74
  49.0 2.7 %collective-permute-start.15 = (bf16[2,48,768]{2,1,0:T(8,128)(2,1)S(1)}, bf16[2,48,768]{2,1,0:T(8,128)(2,1)S(1)}, u32[]{:S(2)}, u32[]{:S(2)}) collective-permute-start(bf16[2,48,768]{2,1,0:T(8,128)(2,1)S(1)} %slice_bitcast_fusion.3), channel_id=1, source_target_pairs={{0,112},{16,0},{32,16},{48,32},{64,48},{80,64},{96,80},{112,96},{1... | collective-permute-start | bytes 442376 | tf_op jit(solution)/shard_map/ppermute | solution.py:74
  51.8 3.5 %level.1 = (f32[64,768]{1,0:T(8,128)}, bf16[64,768]{1,0:T(8,128)(2,1)}) custom-call(bf16[64,1536]{1,0:T(8,128)(2,1)} %get-tuple-element.16.merged_ref, bf16[192,1536]{1,0:T(8,128)(2,1)} %bitcast.109, bf16[192,1536]{1,0:T(8,128)(2,1)} %collective-permute-done.3.core_ref, bf16[192,1536]{1,0:T(8,128)(2,1)} %collective-permute-done.4.near_ref, ...), custom_call_target="tpu_custom_call" | custom-call | flops 150994944 | bytes 3000000 | tf_op jit(solution)/shard_map/level/pallas_call | solution.py:282
  55.5 3.4 %collective-permute-done.6 = bf16[64,768]{1,0:T(8,128)(2,1)S(1)} collective-permute-done((bf16[64,768]{1,0:T(8,128)(2,1)}, bf16[64,768]{1,0:T(8,128)(2,1)S(1)}, u32[]{:S(2)}, u32[]{:S(2)}) %collective-permute-start.6) | collective-permute-done | bytes 98336 | tf_op jit(solution)/shard_map/ppermute | solution.py:66
  59.0 4.2 %collective-permute-start.7 = (bf16[128,768]{1,0:T(8,128)(2,1)S(1)}, bf16[128,768]{1,0:T(8,128)(2,1)S(1)}, u32[]{:S(2)}, u32[]{:S(2)}) collective-permute-start(bf16[128,768]{1,0:T(8,128)(2,1)S(1)} %pad_maximum_fusion.3), channel_id=1, source_target_pairs={{0,4},{4,0},{1,5},{5,1},{2,6},{6,2},{3,7},{7,3},{8,12},{12,8},{9,1... | collective-permute-start | bytes 589832 | tf_op jit(solution)/shard_map/ppermute | solution.py:62
  63.1 1.1 collective-permute-done.7
  64.2 2.4 %multiply_convert_fusion = (bf16[256,768]{1,0:T(8,128)(2,1)S(1)}, f32[256,768]{1,0:T(8,128)S(1)}, f32[256,768]{1,0:T(8,128)S(1)}) fusion(bf16[256,768]{1,0:T(8,128)(2,1)S(1)} %constant_dynamic-update-slice_fusion, bf16[768,768]{1,0:T(8,128)(2,1)S(1)} %bitcast.102), kind=kOutput, calls=%fused_computation.7 | convolution fusion | flops 314769408 | bytes 3538944 | tf_op jit(solution)/shard_map/dot_general | solution.py:23
  67.6 1.1 collective-permute-done.17
  68.9 4.0 %collective-permute-done.18 = bf16[64,768]{1,0:T(8,128)(2,1)S(1)} collective-permute-done((bf16[64,768]{1,0:T(8,128)(2,1)S(1)}, bf16[64,768]{1,0:T(8,128)(2,1)S(1)}, u32[]{:S(2)}, u32[]{:S(2)}) %collective-permute-start.18) | collective-permute-done | bytes 98336 | tf_op jit(solution)/shard_map/ppermute | solution.py:66
  73.9 3.2 %collective-permute-done.19 = bf16[64,768]{1,0:T(8,128)(2,1)S(1)} collective-permute-done((bf16[64,768]{1,0:T(8,128)(2,1)S(1)}, bf16[64,768]{1,0:T(8,128)(2,1)S(1)}, u32[]{:S(2)}, u32[]{:S(2)}) %collective-permute-start.19) | collective-permute-done | bytes 98336 | tf_op jit(solution)/shard_map/ppermute | solution.py:66
  77.1 2.5 %collective-permute-start.20 = (bf16[128,768]{1,0:T(8,128)(2,1)S(1)}, bf16[128,768]{1,0:T(8,128)(2,1)S(1)}, u32[]{:S(2)}, u32[]{:S(2)}) collective-permute-start(bf16[128,768]{1,0:T(8,128)(2,1)S(1)} %pad_maximum_fusion.4), channel_id=1, source_target_pairs={{0,4},{4,0},{1,5},{5,1},{2,6},{6,2},{3,7},{7,3},{8,12},{12,8},{9,1... | collective-permute-start | bytes 589832 | tf_op jit(solution)/shard_map/ppermute | solution.py:62
  79.6 1.1 collective-permute-done.20
  80.7 0.6 add_convert_fusion
  83.8 2.7 %collective-permute-start.27 = (bf16[2,48,768]{2,1,0:T(8,128)(2,1)S(1)}, bf16[2,48,768]{2,1,0:T(8,128)(2,1)S(1)}, u32[]{:S(2)}, u32[]{:S(2)}) collective-permute-start(bf16[2,48,768]{2,1,0:T(8,128)(2,1)S(1)} %get-tuple-element.52), channel_id=1, source_target_pairs={{0,112},{16,0},{32,16},{48,32},{64,48},{80,64},{96,80},{112,96},{1... | collective-permute-start | bytes 442376 | tf_op jit(solution)/shard_map/ppermute | solution.py:74
  86.4 0.7 select_bitcast_fusion.4
  87.1 0.6 collective-permute-start.26
  87.7 2.5 %collective-permute-done.31 = bf16[2,48,768]{2,1,0:T(8,128)(2,1)S(1)} collective-permute-done((bf16[2,48,768]{2,1,0:T(8,128)(2,1)S(1)}, bf16[2,48,768]{2,1,0:T(8,128)(2,1)S(1)}, u32[]{:S(2)}, u32[]{:S(2)}) %collective-permute-start.31) | collective-permute-done | bytes 147488 | tf_op jit(solution)/shard_map/ppermute | solution.py:74
  90.6 2.7 %collective-permute-start.28 = (bf16[2,2,48,768]{3,2,1,0:T(8,128)(2,1)S(1)}, bf16[2,2,48,768]{3,2,1,0:T(8,128)(2,1)S(1)}, u32[]{:S(2)}, u32[]{:S(2)}) collective-permute-start(bf16[2,2,48,768]{3,2,1,0:T(8,128)(2,1)S(1)} %fusion.9), channel_id=1, source_target_pairs={{0,112},{16,0},{32,16},{48,32},{64,48},{80,64},{96,80},{112,96},{1... | collective-permute-start | bytes 884744 | tf_op jit(solution)/shard_map/ppermute | solution.py:74
  93.4 1.1 collective-permute-done.22
  94.5 2.2 %collective-permute-start.25 = (bf16[16,1536]{1,0:T(8,128)(2,1)S(1)}, bf16[16,1536]{1,0:T(8,128)(2,1)S(1)}, u32[]{:S(2)}, u32[]{:S(2)}) collective-permute-start(bf16[16,1536]{1,0:T(8,128)(2,1)S(1)} %get-tuple-element.61), channel_id=1, source_target_pairs={{0,4},{4,8},{8,12},{12,0},{16,20},{20,24},{24,28},{28,16},{32,36},... | collective-permute-start | bytes 147464 | tf_op jit(solution)/shard_map/ppermute | solution.py:58
  96.7 2.5 %collective-permute-done.32 = bf16[2,2,48,768]{3,2,1,0:T(8,128)(2,1)S(1)} collective-permute-done((bf16[2,2,48,768]{3,2,1,0:T(8,128)(2,1)S(1)}, bf16[2,2,48,768]{3,2,1,0:T(8,128)(2,1)S(1)}, u32[]{:S(2)}, u32[]{:S(2)}) %collective-permute-start.32) | collective-permute-done | bytes 294944 | tf_op jit(solution)/shard_map/ppermute | solution.py:74
  99.6 4.3 %collective-permute-done.24 = bf16[16,1536]{1,0:T(8,128)(2,1)S(1)} collective-permute-done((bf16[16,1536]{1,0:T(8,128)(2,1)S(1)}, bf16[16,1536]{1,0:T(8,128)(2,1)S(1)}, u32[]{:S(2)}, u32[]{:S(2)}) %collective-permute-start.24) | collective-permute-done | bytes 49184 | tf_op jit(solution)/shard_map/ppermute | solution.py:58
  103.8 3.0 %collective-permute-done.23 = bf16[16,1536]{1,0:T(8,128)(2,1)S(1)} collective-permute-done((bf16[16,1536]{1,0:T(8,128)(2,1)S(1)}, bf16[16,1536]{1,0:T(8,128)(2,1)S(1)}, u32[]{:S(2)}, u32[]{:S(2)}) %collective-permute-start.23) | collective-permute-done | bytes 49184 | tf_op jit(solution)/shard_map/ppermute | solution.py:58
  107.3 4.6 %collective-permute-done.33 = bf16[2,2,48,768]{3,2,1,0:T(8,128)(2,1)S(1)} collective-permute-done((bf16[2,2,48,768]{3,2,1,0:T(8,128)(2,1)S(1)}, bf16[2,2,48,768]{3,2,1,0:T(8,128)(2,1)S(1)}, u32[]{:S(2)}, u32[]{:S(2)}) %collective-permute-start.33) | collective-permute-done | bytes 294944 | tf_op jit(solution)/shard_map/ppermute | solution.py:74
  112.1 2.2 %collective-permute-done.29 = bf16[2,2,48,768]{3,2,1,0:T(8,128)(2,1)S(1)} collective-permute-done((bf16[2,2,48,768]{3,2,1,0:T(8,128)(2,1)S(1)}, bf16[2,2,48,768]{3,2,1,0:T(8,128)(2,1)S(1)}, u32[]{:S(2)}, u32[]{:S(2)}) %collective-permute-start.29) | collective-permute-done | bytes 294944 | tf_op jit(solution)/shard_map/ppermute | solution.py:74
  114.4 3.0 %collective-permute-start.35 = (bf16[2,48,768]{2,1,0:T(8,128)(2,1)S(1)}, bf16[2,48,768]{2,1,0:T(8,128)(2,1)S(1)}, u32[]{:S(2)}, u32[]{:S(2)}) collective-permute-start(bf16[2,48,768]{2,1,0:T(8,128)(2,1)S(1)} %get-tuple-element.49), channel_id=1, source_target_pairs={{0,240},{16,128},{32,144},{48,160},{64,176},{80,192},{96,208},{112... | collective-permute-start | bytes 442376 | tf_op jit(solution)/shard_map/ppermute | solution.py:82
  117.3 2.7 %collective-permute-start.30 = (bf16[2,48,768]{2,1,0:T(8,128)(2,1)S(1)}, bf16[2,48,768]{2,1,0:T(8,128)(2,1)S(1)}, u32[]{:S(2)}, u32[]{:S(2)}) collective-permute-start(bf16[2,48,768]{2,1,0:T(8,128)(2,1)S(1)} %get-tuple-element.48), channel_id=1, source_target_pairs={{0,112},{16,0},{32,16},{48,32},{64,48},{80,64},{96,80},{112,96},{1... | collective-permute-start | bytes 442376 | tf_op jit(solution)/shard_map/ppermute | solution.py:74
  120.0 0.8 fusion.43
  120.8 0.9 collective-permute-done.36
  121.7 1.2 collective-permute-done.35
  122.9 1.1 collective-permute-done.30
  124.0 1.0 fusion.14
  125.0 0.7 slice_bitcast_fusion
  (110 shorter events, 8.6 us)
Async XLA Ops:
  0.6 17.9 %copy-start.3 = (bf16[1536,192]{0,1:T(8,128)(2,1)S(1)}, bf16[1536,192]{0,1:T(8,128)(2,1)}, u32[]{:S(2)}) copy-start(bf16[1536,192]{0,1:T(8,128)(2,1)} %param.12) | copy-start | bytes 1769476
  0.6 19.1 %copy-start = (bf16[384,1152]{1,0:T(8,128)(2,1)S(1)}, bf16[384,1152]{1,0:T(8,128)(2,1)}, u32[]{:S(2)}) copy-start(bf16[384,1152]{1,0:T(8,128)(2,1)} %qkv_ref.1) | copy-start | bytes 2654212
  0.7 19.1 %copy-start.1 = (bf16[384,384]{1,0:T(8,128)(2,1)S(1)}, bf16[384,384]{1,0:T(8,128)(2,1)}, u32[]{:S(2)}) copy-start(bf16[384,384]{1,0:T(8,128)(2,1)} %proj_ref.1) | copy-start | bytes 884740
  1.7 14.3 %collective-permute-start.8 = (bf16[2,48,768]{2,1,0:T(8,128)(2,1)S(1)}, bf16[2,48,768]{2,1,0:T(8,128)(2,1)S(1)}, u32[]{:S(2)}, u32[]{:S(2)}) collective-permute-start(bf16[2,48,768]{2,1,0:T(8,128)(2,1)S(1)} %pad_maximum_fusion.12), channel_id=1, source_target_pairs={{0,128},{128,0},{1,129},{129,1},{2,130},{130,2},{3,131},{131,3},{4... | collective-permute-start | bytes 442376 | tf_op jit(solution)/shard_map/ppermute | solution.py:70
  7.4 11.2 %collective-permute-start = (bf16[96,384]{1,0:T(8,128)(2,1)}, bf16[96,384]{1,0:T(8,128)(2,1)S(1)}, u32[]{:S(2)}, u32[]{:S(2)}) collective-permute-start(bf16[96,384]{1,0:T(8,128)(2,1)} %get-tuple-element.13), channel_id=1, source_target_pairs={{0,12},{4,0},{8,4},{12,8},{16,28},{20,16},{24,20},{28,24},{32,44},... | collective-permute-start | bytes 221192 | tf_op jit(solution)/shard_map/ppermute | solution.py:58
  8.3 10.5 %collective-permute-start.1 = (bf16[96,384]{1,0:T(8,128)(2,1)}, bf16[96,384]{1,0:T(8,128)(2,1)S(1)}, u32[]{:S(2)}, u32[]{:S(2)}) collective-permute-start(bf16[96,384]{1,0:T(8,128)(2,1)} %get-tuple-element.14), channel_id=1, source_target_pairs={{0,240},{4,244},{8,248},{12,252},{16,0},{20,4},{24,8},{28,12},{32,... | collective-permute-start | bytes 221192 | tf_op jit(solution)/shard_map/ppermute | solution.py:58
  13.8 5.3 %collective-permute-start.2 = (bf16[96,384]{1,0:T(8,128)(2,1)}, bf16[96,384]{1,0:T(8,128)(2,1)S(1)}, u32[]{:S(2)}, u32[]{:S(2)}) collective-permute-start(bf16[96,384]{1,0:T(8,128)(2,1)} %get-tuple-element.15), channel_id=1, source_target_pairs={{0,252},{4,240},{8,244},{12,248},{16,12},{20,0},{24,4},{28,8},{32,... | collective-permute-start | bytes 221192 | tf_op jit(solution)/shard_map/ppermute | solution.py:58
  17.0 9.4 %collective-permute-start.9 = (bf16[2,2,48,768]{3,2,1,0:T(8,128)(2,1)S(1)}, bf16[2,2,48,768]{3,2,1,0:T(8,128)(2,1)}, u32[]{:S(2)}, u32[]{:S(2)}) collective-permute-start(bf16[2,2,48,768]{3,2,1,0:T(8,128)(2,1)S(1)} %get-tuple-element.54), channel_id=1, source_target_pairs={{0,112},{16,0},{32,16},{48,32},{64,48},{80,64},{96,80},{112,96},{1... | collective-permute-start | bytes 884744 | tf_op jit(solution)/shard_map/ppermute | solution.py:74
  17.1 13.9 %collective-permute-start.10 = (bf16[2,2,48,768]{3,2,1,0:T(8,128)(2,1)S(1)}, bf16[2,2,48,768]{3,2,1,0:T(8,128)(2,1)}, u32[]{:S(2)}, u32[]{:S(2)}) collective-permute-start(bf16[2,2,48,768]{3,2,1,0:T(8,128)(2,1)S(1)} %get-tuple-element.54), channel_id=1, source_target_pairs={{0,16},{16,32},{32,48},{48,64},{64,80},{80,96},{96,112},{112,0},{1... | collective-permute-start | bytes 884744 | tf_op jit(solution)/shard_map/ppermute | solution.py:74
  18.5 0.6 copy-start.6
  18.5 33.2 %collective-permute-start.3 = (bf16[192,1536]{1,0:T(8,128)(2,1)S(1)}, bf16[192,1536]{1,0:T(8,128)(2,1)}, u32[]{:S(2)}, u32[]{:S(2)}) collective-permute-start(bf16[192,1536]{1,0:T(8,128)(2,1)S(1)} %bitcast.110), channel_id=1, source_target_pairs={{0,4},{4,0},{1,5},{5,1},{2,6},{6,2},{3,7},{7,3},{8,12},{12,8},{9,1... | collective-permute-start | bytes 1769480 | tf_op jit(solution)/shard_map/ppermute | solution.py:62
  18.8 0.6 copy-start.7
  18.8 14.6 %collective-permute-start.4 = (bf16[192,1536]{1,0:T(8,128)(2,1)S(1)}, bf16[192,1536]{1,0:T(8,128)(2,1)}, u32[]{:S(2)}, u32[]{:S(2)}) collective-permute-start(bf16[192,1536]{1,0:T(8,128)(2,1)S(1)} %bitcast.111), channel_id=1, source_target_pairs={{0,8},{8,0},{1,9},{9,1},{2,10},{10,2},{3,11},{11,3},{4,12},{12,4},... | collective-permute-start | bytes 1769480 | tf_op jit(solution)/shard_map/ppermute | solution.py:66
  19.1 0.6 copy-start.8
  26.3 10.9 %collective-permute-start.11 = (bf16[2,2,48,768]{3,2,1,0:T(8,128)(2,1)}, bf16[2,2,48,768]{3,2,1,0:T(8,128)(2,1)S(1)}, u32[]{:S(2)}, u32[]{:S(2)}) collective-permute-start(bf16[2,2,48,768]{3,2,1,0:T(8,128)(2,1)} %collective-permute-done.9), channel_id=1, source_target_pairs={{0,112},{16,0},{32,16},{48,32},{64,48},{80,64},{96,80},{112,96},{1... | collective-permute-start | bytes 884744 | tf_op jit(solution)/shard_map/ppermute | solution.py:74
  30.9 9.6 %collective-permute-start.12 = (bf16[2,2,48,768]{3,2,1,0:T(8,128)(2,1)}, bf16[2,2,48,768]{3,2,1,0:T(8,128)(2,1)S(1)}, u32[]{:S(2)}, u32[]{:S(2)}) collective-permute-start(bf16[2,2,48,768]{3,2,1,0:T(8,128)(2,1)} %collective-permute-done.10), channel_id=1, source_target_pairs={{0,16},{16,32},{32,48},{48,64},{64,80},{80,96},{96,112},{112,0},{1... | collective-permute-start | bytes 884744 | tf_op jit(solution)/shard_map/ppermute | solution.py:74
  33.4 18.3 %collective-permute-start.5 = (bf16[192,1536]{1,0:T(8,128)(2,1)}, bf16[192,1536]{1,0:T(8,128)(2,1)}, u32[]{:S(2)}, u32[]{:S(2)}) collective-permute-start(bf16[192,1536]{1,0:T(8,128)(2,1)} %collective-permute-done.4.near_ref), channel_id=1, source_target_pairs={{0,4},{4,0},{1,5},{5,1},{2,6},{6,2},{3,7},{7,3},{8,12},{12,8},{9,1... | collective-permute-start | bytes 1769480 | tf_op jit(solution)/shard_map/ppermute | solution.py:62
  37.2 11.7 %collective-permute-start.13 = (bf16[2,2,48,768]{3,2,1,0:T(8,128)(2,1)S(1)}, bf16[2,2,48,768]{3,2,1,0:T(8,128)(2,1)S(1)}, u32[]{:S(2)}, u32[]{:S(2)}) collective-permute-start(bf16[2,2,48,768]{3,2,1,0:T(8,128)(2,1)S(1)} %collective-permute-done.11), channel_id=1, source_target_pairs={{0,112},{16,0},{32,16},{48,32},{64,48},{80,64},{96,80},{112,96},{1... | collective-permute-start | bytes 884744 | tf_op jit(solution)/shard_map/ppermute | solution.py:74
  40.5 8.3 %collective-permute-start.14 = (bf16[2,2,48,768]{3,2,1,0:T(8,128)(2,1)S(1)}, bf16[2,2,48,768]{3,2,1,0:T(8,128)(2,1)S(1)}, u32[]{:S(2)}, u32[]{:S(2)}) collective-permute-start(bf16[2,2,48,768]{3,2,1,0:T(8,128)(2,1)S(1)} %collective-permute-done.12), channel_id=1, source_target_pairs={{0,16},{16,32},{32,48},{48,64},{64,80},{80,96},{96,112},{112,0},{1... | collective-permute-start | bytes 884744 | tf_op jit(solution)/shard_map/ppermute | solution.py:74
  48.8 6.4 %collective-permute-start.16 = (bf16[2,48,768]{2,1,0:T(8,128)(2,1)S(1)}, bf16[2,48,768]{2,1,0:T(8,128)(2,1)S(1)}, u32[]{:S(2)}, u32[]{:S(2)}) collective-permute-start(bf16[2,48,768]{2,1,0:T(8,128)(2,1)S(1)} %slice_bitcast_fusion.2), channel_id=1, source_target_pairs={{0,16},{16,32},{32,48},{48,64},{64,80},{80,96},{96,112},{112,0},{1... | collective-permute-start | bytes 442376 | tf_op jit(solution)/shard_map/ppermute | solution.py:74
  49.0 6.3 %collective-permute-start.15 = (bf16[2,48,768]{2,1,0:T(8,128)(2,1)S(1)}, bf16[2,48,768]{2,1,0:T(8,128)(2,1)S(1)}, u32[]{:S(2)}, u32[]{:S(2)}) collective-permute-start(bf16[2,48,768]{2,1,0:T(8,128)(2,1)S(1)} %slice_bitcast_fusion.3), channel_id=1, source_target_pairs={{0,112},{16,0},{32,16},{48,32},{64,48},{80,64},{96,80},{112,96},{1... | collective-permute-start | bytes 442376 | tf_op jit(solution)/shard_map/ppermute | solution.py:74
  55.3 3.7 %collective-permute-start.6 = (bf16[64,768]{1,0:T(8,128)(2,1)}, bf16[64,768]{1,0:T(8,128)(2,1)S(1)}, u32[]{:S(2)}, u32[]{:S(2)}) collective-permute-start(bf16[64,768]{1,0:T(8,128)(2,1)} %get-tuple-element.18), channel_id=1, source_target_pairs={{0,8},{8,0},{1,9},{9,1},{2,10},{10,2},{3,11},{11,3},{4,12},{12,4},... | collective-permute-start | bytes 294920 | tf_op jit(solution)/shard_map/ppermute | solution.py:66
  55.3 3.6 %copy-start.4 = (bf16[64,768]{1,0:T(8,128)(2,1)S(1)}, bf16[64,768]{1,0:T(8,128)(2,1)}, u32[]{:S(2)}) copy-start(bf16[64,768]{1,0:T(8,128)(2,1)} %get-tuple-element.18) | copy-start | bytes 294916
  59.0 5.2 %collective-permute-start.7 = (bf16[128,768]{1,0:T(8,128)(2,1)S(1)}, bf16[128,768]{1,0:T(8,128)(2,1)S(1)}, u32[]{:S(2)}, u32[]{:S(2)}) collective-permute-start(bf16[128,768]{1,0:T(8,128)(2,1)S(1)} %pad_maximum_fusion.3), channel_id=1, source_target_pairs={{0,4},{4,0},{1,5},{5,1},{2,6},{6,2},{3,7},{7,3},{8,12},{12,8},{9,1... | collective-permute-start | bytes 589832 | tf_op jit(solution)/shard_map/ppermute | solution.py:62
  66.6 6.6 %copy-start.2 = (bf16[64,768]{1,0:T(8,128)(2,1)S(1)}, bf16[64,768]{1,0:T(8,128)(2,1)}, u32[]{:S(2)}) copy-start(bf16[64,768]{1,0:T(8,128)(2,1)} %get-tuple-element.19) | copy-start | bytes 294916
  66.6 6.8 %copy-start.5 = (f32[64,768]{1,0:T(8,128)S(1)}, f32[64,768]{1,0:T(8,128)}, u32[]{:S(2)}) copy-start(f32[64,768]{1,0:T(8,128)} %get-tuple-element.17) | copy-start | bytes 589828
  67.2 1.5 %collective-permute-start.17 = (bf16[128,768]{1,0:T(8,128)(2,1)S(1)}, bf16[128,768]{1,0:T(8,128)(2,1)S(1)}, u32[]{:S(2)}, u32[]{:S(2)}) collective-permute-start(bf16[128,768]{1,0:T(8,128)(2,1)S(1)} %slice.141), channel_id=1, source_target_pairs={{0,4},{4,0},{1,5},{5,1},{2,6},{6,2},{3,7},{7,3},{8,12},{12,8},{9,1... | collective-permute-start | bytes 589832 | tf_op jit(solution)/shard_map/ppermute | solution.py:62
  68.8 4.1 %collective-permute-start.18 = (bf16[64,768]{1,0:T(8,128)(2,1)S(1)}, bf16[64,768]{1,0:T(8,128)(2,1)S(1)}, u32[]{:S(2)}, u32[]{:S(2)}) collective-permute-start(bf16[64,768]{1,0:T(8,128)(2,1)S(1)} %slice.259), channel_id=1, source_target_pairs={{0,8},{8,0},{1,9},{9,1},{2,10},{10,2},{3,11},{11,3},{4,12},{12,4},... | collective-permute-start | bytes 294920 | tf_op jit(solution)/shard_map/ppermute | solution.py:66
  73.6 3.6 %collective-permute-start.19 = (bf16[64,768]{1,0:T(8,128)(2,1)S(1)}, bf16[64,768]{1,0:T(8,128)(2,1)S(1)}, u32[]{:S(2)}, u32[]{:S(2)}) collective-permute-start(bf16[64,768]{1,0:T(8,128)(2,1)S(1)} %get-tuple-element.43), channel_id=1, source_target_pairs={{0,8},{8,0},{1,9},{9,1},{2,10},{10,2},{3,11},{11,3},{4,12},{12,4},... | collective-permute-start | bytes 294920 | tf_op jit(solution)/shard_map/ppermute | solution.py:66
  77.1 3.5 %collective-permute-start.20 = (bf16[128,768]{1,0:T(8,128)(2,1)S(1)}, bf16[128,768]{1,0:T(8,128)(2,1)S(1)}, u32[]{:S(2)}, u32[]{:S(2)}) collective-permute-start(bf16[128,768]{1,0:T(8,128)(2,1)S(1)} %pad_maximum_fusion.4), channel_id=1, source_target_pairs={{0,4},{4,0},{1,5},{5,1},{2,6},{6,2},{3,7},{7,3},{8,12},{12,8},{9,1... | collective-permute-start | bytes 589832 | tf_op jit(solution)/shard_map/ppermute | solution.py:62
  82.3 8.1 %collective-permute-start.21 = (bf16[128,768]{1,0:T(8,128)(2,1)S(1)}, bf16[128,768]{1,0:T(8,128)(2,1)S(1)}, u32[]{:S(2)}, u32[]{:S(2)}) collective-permute-start(bf16[128,768]{1,0:T(8,128)(2,1)S(1)} %slice.145), channel_id=1, source_target_pairs={{0,4},{4,0},{1,5},{5,1},{2,6},{6,2},{3,7},{7,3},{8,12},{12,8},{9,1... | collective-permute-start | bytes 589832 | tf_op jit(solution)/shard_map/ppermute | solution.py:62
  83.7 6.6 %collective-permute-start.31 = (bf16[2,48,768]{2,1,0:T(8,128)(2,1)S(1)}, bf16[2,48,768]{2,1,0:T(8,128)(2,1)S(1)}, u32[]{:S(2)}, u32[]{:S(2)}) collective-permute-start(bf16[2,48,768]{2,1,0:T(8,128)(2,1)S(1)} %get-tuple-element.53), channel_id=1, source_target_pairs={{0,16},{16,32},{32,48},{48,64},{64,80},{80,96},{96,112},{112,0},{1... | collective-permute-start | bytes 442376 | tf_op jit(solution)/shard_map/ppermute | solution.py:74
  83.8 6.6 %collective-permute-start.27 = (bf16[2,48,768]{2,1,0:T(8,128)(2,1)S(1)}, bf16[2,48,768]{2,1,0:T(8,128)(2,1)S(1)}, u32[]{:S(2)}, u32[]{:S(2)}) collective-permute-start(bf16[2,48,768]{2,1,0:T(8,128)(2,1)S(1)} %get-tuple-element.52), channel_id=1, source_target_pairs={{0,112},{16,0},{32,16},{48,32},{64,48},{80,64},{96,80},{112,96},{1... | collective-permute-start | bytes 442376 | tf_op jit(solution)/shard_map/ppermute | solution.py:74
  87.1 33.7 %collective-permute-start.26 = (bf16[2,48,768]{2,1,0:T(8,128)(2,1)}, bf16[2,48,768]{2,1,0:T(8,128)(2,1)}, u32[]{:S(2)}, u32[]{:S(2)}) collective-permute-start(bf16[2,48,768]{2,1,0:T(8,128)(2,1)} %select_bitcast_fusion.4), channel_id=1, source_target_pairs={{0,128},{128,0},{1,129},{129,1},{2,130},{130,2},{3,131},{131,3},{4... | collective-permute-start | bytes 442376 | tf_op jit(solution)/shard_map/ppermute | solution.py:70
  90.3 8.9 %collective-permute-start.32 = (bf16[2,2,48,768]{3,2,1,0:T(8,128)(2,1)S(1)}, bf16[2,2,48,768]{3,2,1,0:T(8,128)(2,1)S(1)}, u32[]{:S(2)}, u32[]{:S(2)}) collective-permute-start(bf16[2,2,48,768]{3,2,1,0:T(8,128)(2,1)S(1)} %pad_maximum_fusion.2), channel_id=1, source_target_pairs={{0,16},{16,32},{32,48},{48,64},{64,80},{80,96},{96,112},{112,0},{1... | collective-permute-start | bytes 884744 | tf_op jit(solution)/shard_map/ppermute | solution.py:74
  90.5 4.0 %collective-permute-start.22 = (bf16[64,768]{1,0:T(8,128)(2,1)S(1)}, bf16[64,768]{1,0:T(8,128)(2,1)S(1)}, u32[]{:S(2)}, u32[]{:S(2)}) collective-permute-start(bf16[64,768]{1,0:T(8,128)(2,1)S(1)} %slice.258), channel_id=1, source_target_pairs={{0,8},{8,0},{1,9},{9,1},{2,10},{10,2},{3,11},{11,3},{4,12},{12,4},... | collective-permute-start | bytes 294920 | tf_op jit(solution)/shard_map/ppermute | solution.py:66
  90.6 16.5 %collective-permute-start.28 = (bf16[2,2,48,768]{3,2,1,0:T(8,128)(2,1)S(1)}, bf16[2,2,48,768]{3,2,1,0:T(8,128)(2,1)S(1)}, u32[]{:S(2)}, u32[]{:S(2)}) collective-permute-start(bf16[2,2,48,768]{3,2,1,0:T(8,128)(2,1)S(1)} %fusion.9), channel_id=1, source_target_pairs={{0,112},{16,0},{32,16},{48,32},{64,48},{80,64},{96,80},{112,96},{1... | collective-permute-start | bytes 884744 | tf_op jit(solution)/shard_map/ppermute | solution.py:74
  94.5 4.9 %collective-permute-start.25 = (bf16[16,1536]{1,0:T(8,128)(2,1)S(1)}, bf16[16,1536]{1,0:T(8,128)(2,1)S(1)}, u32[]{:S(2)}, u32[]{:S(2)}) collective-permute-start(bf16[16,1536]{1,0:T(8,128)(2,1)S(1)} %get-tuple-element.61), channel_id=1, source_target_pairs={{0,4},{4,8},{8,12},{12,0},{16,20},{20,24},{24,28},{28,16},{32,36},... | collective-permute-start | bytes 147464 | tf_op jit(solution)/shard_map/ppermute | solution.py:58
  96.7 7.2 %collective-permute-start.24 = (bf16[16,1536]{1,0:T(8,128)(2,1)S(1)}, bf16[16,1536]{1,0:T(8,128)(2,1)S(1)}, u32[]{:S(2)}, u32[]{:S(2)}) collective-permute-start(bf16[16,1536]{1,0:T(8,128)(2,1)S(1)} %get-tuple-element.59), channel_id=1, source_target_pairs={{0,16},{4,20},{8,24},{12,28},{16,32},{20,36},{24,40},{28,44},{32,4... | collective-permute-start | bytes 147464 | tf_op jit(solution)/shard_map/ppermute | solution.py:58
  99.2 7.7 %collective-permute-start.23 = (bf16[16,1536]{1,0:T(8,128)(2,1)S(1)}, bf16[16,1536]{1,0:T(8,128)(2,1)S(1)}, u32[]{:S(2)}, u32[]{:S(2)}) collective-permute-start(bf16[16,1536]{1,0:T(8,128)(2,1)S(1)} %get-tuple-element.58), channel_id=1, source_target_pairs={{0,20},{4,24},{8,28},{12,16},{16,36},{20,40},{24,44},{28,32},{32,5... | collective-permute-start | bytes 147464 | tf_op jit(solution)/shard_map/ppermute | solution.py:58
  99.5 12.5 %collective-permute-start.33 = (bf16[2,2,48,768]{3,2,1,0:T(8,128)(2,1)S(1)}, bf16[2,2,48,768]{3,2,1,0:T(8,128)(2,1)S(1)}, u32[]{:S(2)}, u32[]{:S(2)}) collective-permute-start(bf16[2,2,48,768]{3,2,1,0:T(8,128)(2,1)S(1)} %maximum_add_fusion.2), channel_id=1, source_target_pairs={{0,16},{16,32},{32,48},{48,64},{64,80},{80,96},{96,112},{112,0},{1... | collective-permute-start | bytes 884744 | tf_op jit(solution)/shard_map/ppermute | solution.py:74
  107.2 7.1 %collective-permute-start.29 = (bf16[2,2,48,768]{3,2,1,0:T(8,128)(2,1)S(1)}, bf16[2,2,48,768]{3,2,1,0:T(8,128)(2,1)S(1)}, u32[]{:S(2)}, u32[]{:S(2)}) collective-permute-start(bf16[2,2,48,768]{3,2,1,0:T(8,128)(2,1)S(1)} %maximum_add_fusion), channel_id=1, source_target_pairs={{0,112},{16,0},{32,16},{48,32},{64,48},{80,64},{96,80},{112,96},{1... | collective-permute-start | bytes 884744 | tf_op jit(solution)/shard_map/ppermute | solution.py:74
  112.0 9.7 %collective-permute-start.36 = (bf16[2,48,768]{2,1,0:T(8,128)(2,1)S(1)}, bf16[2,48,768]{2,1,0:T(8,128)(2,1)S(1)}, u32[]{:S(2)}, u32[]{:S(2)}) collective-permute-start(bf16[2,48,768]{2,1,0:T(8,128)(2,1)S(1)} %get-tuple-element.51), channel_id=1, source_target_pairs={{0,144},{16,160},{32,176},{48,192},{64,208},{80,224},{96,240},{112... | collective-permute-start | bytes 442376 | tf_op jit(solution)/shard_map/ppermute | solution.py:82
  114.4 8.5 %collective-permute-start.35 = (bf16[2,48,768]{2,1,0:T(8,128)(2,1)S(1)}, bf16[2,48,768]{2,1,0:T(8,128)(2,1)S(1)}, u32[]{:S(2)}, u32[]{:S(2)}) collective-permute-start(bf16[2,48,768]{2,1,0:T(8,128)(2,1)S(1)} %get-tuple-element.49), channel_id=1, source_target_pairs={{0,240},{16,128},{32,144},{48,160},{64,176},{80,192},{96,208},{112... | collective-permute-start | bytes 442376 | tf_op jit(solution)/shard_map/ppermute | solution.py:82
  117.3 5.5 %collective-permute-start.34 = (bf16[2,48,768]{2,1,0:T(8,128)(2,1)S(1)}, bf16[2,48,768]{2,1,0:T(8,128)(2,1)S(1)}, u32[]{:S(2)}, u32[]{:S(2)}) collective-permute-start(bf16[2,48,768]{2,1,0:T(8,128)(2,1)S(1)} %get-tuple-element.50), channel_id=1, source_target_pairs={{0,16},{16,32},{32,48},{48,64},{64,80},{80,96},{96,112},{112,0},{1... | collective-permute-start | bytes 442376 | tf_op jit(solution)/shard_map/ppermute | solution.py:74
  117.3 6.6 %collective-permute-start.30 = (bf16[2,48,768]{2,1,0:T(8,128)(2,1)S(1)}, bf16[2,48,768]{2,1,0:T(8,128)(2,1)S(1)}, u32[]{:S(2)}, u32[]{:S(2)}) collective-permute-start(bf16[2,48,768]{2,1,0:T(8,128)(2,1)S(1)} %get-tuple-element.48), channel_id=1, source_target_pairs={{0,112},{16,0},{32,16},{48,32},{64,48},{80,64},{96,80},{112,96},{1... | collective-permute-start | bytes 442376 | tf_op jit(solution)/shard_map/ppermute | solution.py:74

commit v2 on v1

--- a/solution.py
+++ b/solution.py
@@ -214,6 +214,10 @@
     bf_ref[...] = level.astype(BF)
 
 
+def in_vmem(array):
+    return pltpu.with_memory_space_constraint(array, pltpu.VMEM)
+
+
 def whole(count):
     return [pl.BlockSpec(memory_space=pltpu.VMEM)] * count
 
@@ -276,8 +280,8 @@
     )(
         logit_scale,
         *x,
-        pltpu.with_memory_space_constraint(w_qkv, pltpu.VMEM),
-        pltpu.with_memory_space_constraint(w_proj, pltpu.VMEM),
+        in_vmem(w_qkv),
+        in_vmem(w_proj),
     )
     level, level_own = pl.pallas_call(
         level_kernel,
@@ -288,7 +292,7 @@
             flops=8 * own * channels * wide, transcendentals=own, bytes_accessed=3_000_000
         ),
         name="level",
-    )(merged, merge_own, merge_core, merge_near, merge_far)
+    )(merged, *(in_vmem(w) for w in (merge_own, merge_core, merge_near, merge_far)))
     level_b = gather_cols(level_own)
 
     hidden_pre = dot(level_b, up_full)

time: 127 us -> 127 us (level)
  local copies, waits for them, and re-layouts: 5.36 us -> 8.36 us
  waiting for transfers between devices: 48.8 us -> 46.3 us
    slice x1, local copies, waits for them, and re-layouts: 0.19 us -> 1.81 us  [whole_step(): down_full = weights[:, :, 1].reshape(wide, -1)]
    unnamed x20 -> x18, local copies, waits for them, and re-layouts: 0.69 us -> 2.06 us
    ppermute x5, waiting for transfers between devices: 12.2 us -> 10.8 us  [swap_xl(): return lax.ppermute(array, 'xl', [(0, 1), (1, 0)])]
  transfers between devices with their start and end apart: 37 -> 37, of which waited for: 20 -> 20; matrix products, arithmetic and copies ran while one was open for 5% -> 7% of each run, Pallas kernels for 9% -> 9%
where the time goes in v2:
time: 127 us; the launch traced here: 126 us
  starting transfers between devices  48.1 us (38%)
  waiting for transfers between devices  46.3 us (36%)
  Pallas kernels  11.1 us (9%)
  local copies, waits for them, and re-layouts  8.36 us (7%)
  other arithmetic  5.74 us (5%)
  matrix products  5.06 us (4%)
    ppermute x16, waiting for transfers between devices, along_z(): return lax.ppermute(array, 'z', [(i, (i + step) % NZ) for i in range(NZ)])  23 us
    ppermute x16, starting transfers between devices, along_z(): return lax.ppermute(array, 'z', [(i, (i + step) % NZ) for i in range(NZ)])  20.3 us
    ppermute x6, starting transfers between devices, to_grid(): return lax.ppermute(array, GRID, pairs)  11 us
    ppermute x5, waiting for transfers between devices, swap_xl(): return lax.ppermute(array, 'xl', [(0, 1), (1, 0)])  10.8 us
    ppermute x6, starting transfers between devices, swap_core(): return lax.ppermute(array, 'core', [(0, 1), (1, 0)])  8.91 us
    ppermute x6, waiting for transfers between devices, to_grid(): return lax.ppermute(array, GRID, pairs)  7.27 us
    pallas_call x1, Pallas kernels, whole_step(): pl.pallas_call(window_kernel, out_shape=[jax.ShapeDtypeStruct((own, 4 * c...  6.34 us
    ppermute x2, starting transfers between devices, swap_half(): return lax.ppermute(array, 'xh', [(0, 1), (1, 0)])  4.23 us
  transfers between devices with their start and end apart: 37, of which 20 were waited for; matrix products, arithmetic and copies ran while one was open for 7% of the time, Pallas kernels for 9%

profile of v2, /device:TPU:1, one launch (start us, length us, event | category | flops | bytes accessed | tf_op | source)
XLA Modules:
  0.0 125.9 jit_solution(242156233467305089)
XLA Ops:
  0.7 1.1 pad_maximum_fusion.12
  1.7 3.6 %collective-permute-start.8 = (bf16[2,48,768]{2,1,0:T(8,128)(2,1)S(1)}, bf16[2,48,768]{2,1,0:T(8,128)(2,1)S(1)}, u32[]{:S(2)}, u32[]{:S(2)}) collective-permute-start(bf16[2,48,768]{2,1,0:T(8,128)(2,1)S(1)} %pad_maximum_fusion.12), channel_id=1, source_target_pairs={{0,128},{128,0},{1,129},{129,1},{2,130},{130,2},{3,131},{131,3},{4... | collective-permute-start | bytes 442376 | tf_op jit(solution)/shard_map/ppermute | solution.py:70
  5.4 2.0 %order.1 = (bf16[96,384]{1,0:T(8,128)(2,1)}, bf16[96,384]{1,0:T(8,128)(2,1)}, bf16[96,384]{1,0:T(8,128)(2,1)}, bf16[96,384]{1,0:T(8,128)(2,1)}) custom-call(f32[256,384]{1,0:T(8,128)} %bitcast.112, bf16[64,768]{1,0:T(8,128)(2,1)} %bitcast.119), custom_call_target="tpu_custom_call" | custom-call | tf_op jit(solution)/shard_map/order/pallas_call | solution.py:231
  7.4 1.0 collective-permute-start
  8.3 5.5 %collective-permute-start.1 = (bf16[96,384]{1,0:T(8,128)(2,1)}, bf16[96,384]{1,0:T(8,128)(2,1)}, u32[]{:S(2)}, u32[]{:S(2)}) collective-permute-start(bf16[96,384]{1,0:T(8,128)(2,1)} %get-tuple-element.14), channel_id=1, source_target_pairs={{0,240},{4,244},{8,248},{12,252},{16,0},{20,4},{24,8},{28,12},{32,... | collective-permute-start | bytes 221192 | tf_op jit(solution)/shard_map/ppermute | solution.py:58
  13.8 2.1 %collective-permute-start.2 = (bf16[96,384]{1,0:T(8,128)(2,1)}, bf16[96,384]{1,0:T(8,128)(2,1)}, u32[]{:S(2)}, u32[]{:S(2)}) collective-permute-start(bf16[96,384]{1,0:T(8,128)(2,1)} %get-tuple-element.15), channel_id=1, source_target_pairs={{0,252},{4,240},{8,244},{12,248},{16,12},{20,0},{24,4},{28,8},{32,... | collective-permute-start | bytes 221192 | tf_op jit(solution)/shard_map/ppermute | solution.py:58
  16.0 0.9 select_bitcast_fusion.6
  17.1 1.5 %collective-permute-start.10 = (bf16[2,2,48,768]{3,2,1,0:T(8,128)(2,1)S(1)}, bf16[2,2,48,768]{3,2,1,0:T(8,128)(2,1)}, u32[]{:S(2)}, u32[]{:S(2)}) collective-permute-start(bf16[2,2,48,768]{3,2,1,0:T(8,128)(2,1)S(1)} %get-tuple-element.54), channel_id=1, source_target_pairs={{0,16},{16,32},{32,48},{48,64},{64,80},{80,96},{96,112},{112,0},{1... | collective-permute-start | bytes 884744 | tf_op jit(solution)/shard_map/ppermute | solution.py:74
  19.4 6.3 %window.1 = (bf16[64,1536]{1,0:T(8,128)(2,1)}, bf16[64,768]{1,0:T(8,128)(2,1)}) custom-call(f32[6]{0:T(128)} %scale_ref.1, bf16[96,384]{1,0:T(8,128)(2,1)} %get-tuple-element.12.x0, bf16[96,384]{1,0:T(8,128)(2,1)} %copy-done.7, bf16[96,384]{1,0:T(8,128)(2,1)} %collective-permute-done.1.x2, bf16[96,384]{1,0:T(8,128)(2,1)} %collective-permute-done.2.x3, ...), custom_call_target="tpu_custom_call" | custom-call | flops 402653184 | bytes 2000000 | tf_op jit(solution)/shard_map/window/pallas_call | solution.py:266
  26.1 4.3 %collective-permute-start.11 = (bf16[2,2,48,768]{3,2,1,0:T(8,128)(2,1)}, bf16[2,2,48,768]{3,2,1,0:T(8,128)(2,1)S(1)}, u32[]{:S(2)}, u32[]{:S(2)}) collective-permute-start(bf16[2,2,48,768]{3,2,1,0:T(8,128)(2,1)} %collective-permute-done.9), channel_id=1, source_target_pairs={{0,112},{16,0},{32,16},{48,32},{64,48},{80,64},{96,80},{112,96},{1... | collective-permute-start | bytes 884744 | tf_op jit(solution)/shard_map/ppermute | solution.py:74
  30.4 1.0 copy_dynamic-update-slice_fusion.5
  31.4 1.0 copy_dynamic-update-slice_fusion.4
  32.4 1.5 %collective-permute-done.4.near_ref = bf16[192,1536]{1,0:T(8,128)(2,1)S(1)} collective-permute-done((bf16[192,1536]{1,0:T(8,128)(2,1)S(1)}, bf16[192,1536]{1,0:T(8,128)(2,1)S(1)}, u32[]{:S(2)}, u32[]{:S(2)}) %collective-permute-start.4) | collective-permute-done | bytes 589856 | tf_op jit(solution)/shard_map/ppermute | solution.py:66
  33.9 1.2 collective-permute-start.5
  35.1 1.6 %collective-permute-done.11 = bf16[2,2,48,768]{3,2,1,0:T(8,128)(2,1)S(1)} collective-permute-done((bf16[2,2,48,768]{3,2,1,0:T(8,128)(2,1)}, bf16[2,2,48,768]{3,2,1,0:T(8,128)(2,1)S(1)}, u32[]{:S(2)}, u32[]{:S(2)}) %collective-permute-start.11) | collective-permute-done | bytes 294944 | tf_op jit(solution)/shard_map/ppermute | solution.py:74
  36.7 3.3 %collective-permute-start.13 = (bf16[2,2,48,768]{3,2,1,0:T(8,128)(2,1)S(1)}, bf16[2,2,48,768]{3,2,1,0:T(8,128)(2,1)S(1)}, u32[]{:S(2)}, u32[]{:S(2)}) collective-permute-start(bf16[2,2,48,768]{3,2,1,0:T(8,128)(2,1)S(1)} %collective-permute-done.11), channel_id=1, source_target_pairs={{0,112},{16,0},{32,16},{48,32},{64,48},{80,64},{96,80},{112,96},{1... | collective-permute-start | bytes 884744 | tf_op jit(solution)/shard_map/ppermute | solution.py:74
  40.1 8.2 %collective-permute-done.14 = bf16[2,2,48,768]{3,2,1,0:T(8,128)(2,1)S(1)} collective-permute-done((bf16[2,2,48,768]{3,2,1,0:T(8,128)(2,1)S(1)}, bf16[2,2,48,768]{3,2,1,0:T(8,128)(2,1)S(1)}, u32[]{:S(2)}, u32[]{:S(2)}) %collective-permute-start.14) | collective-permute-done | bytes 294944 | tf_op jit(solution)/shard_map/ppermute | solution.py:74
  48.4 2.7 %collective-permute-start.15 = (bf16[2,48,768]{2,1,0:T(8,128)(2,1)S(1)}, bf16[2,48,768]{2,1,0:T(8,128)(2,1)S(1)}, u32[]{:S(2)}, u32[]{:S(2)}) collective-permute-start(bf16[2,48,768]{2,1,0:T(8,128)(2,1)S(1)} %slice_bitcast_fusion.3), channel_id=1, source_target_pairs={{0,112},{16,0},{32,16},{48,32},{64,48},{80,64},{96,80},{112,96},{1... | collective-permute-start | bytes 442376 | tf_op jit(solution)/shard_map/ppermute | solution.py:74
  51.2 1.4 %copy-done.3 = bf16[2,8,2,48,768]{4,3,1,0,2:T(8,128)(2,1)} copy-done((bf16[2,8,2,48,768]{4,3,1,0,2:T(8,128)(2,1)}, bf16[2,8,2,48,768]{4,3,1,0,2:T(8,128)(2,1)S(1)}, u32[]{:S(2)}) %copy-start.3) | copy-done | bytes 2359320
  52.6 2.8 %level.1 = (f32[64,768]{1,0:T(8,128)}, bf16[64,768]{1,0:T(8,128)(2,1)}) custom-call(bf16[64,1536]{1,0:T(8,128)(2,1)} %get-tuple-element.16.merged_ref, bf16[192,1536]{1,0:T(8,128)(2,1)S(1)} %bitcast.104, bf16[192,1536]{1,0:T(8,128)(2,1)S(1)} %collective-permute-done.3.core_ref, bf16[192,1536]{1,0:T(8,128)(2,1)S(1)} %collective-permute-done.4.near_ref, ...), custom_call_target="tpu_custom_call" | custom-call | flops 150994944 | bytes 3000000 | tf_op jit(solution)/shard_map/level/pallas_call | solution.py:286
  55.4 0.8 fusion.10
  56.2 1.8 %fusion.42 = (bf16[2,8,1,48,768]{4,3,1,0,2:T(8,128)(2,1)S(1)}, bf16[2,8,1,48,768]{4,3,1,0,2:T(8,128)(2,1)S(1)}) fusion(bf16[2,8,2,48,768]{4,3,1,0,2:T(8,128)(2,1)} %fusion.10), kind=kLoop, calls=%fused_computation.142 | loop fusion | bytes 4718592 | tf_op jit(solution)/shard_map/slice | solution.py:259
  58.0 1.1 collective-permute-done.6
  59.1 4.2 %collective-permute-start.7 = (bf16[128,768]{1,0:T(8,128)(2,1)S(1)}, bf16[128,768]{1,0:T(8,128)(2,1)S(1)}, u32[]{:S(2)}, u32[]{:S(2)}) collective-permute-start(bf16[128,768]{1,0:T(8,128)(2,1)S(1)} %pad_maximum_fusion.3), channel_id=1, source_target_pairs={{0,4},{4,0},{1,5},{5,1},{2,6},{6,2},{3,7},{7,3},{8,12},{12,8},{9,1... | collective-permute-start | bytes 589832 | tf_op jit(solution)/shard_map/ppermute | solution.py:62
  63.3 1.1 collective-permute-done.7
  64.3 2.4 %multiply_convert_fusion = (bf16[256,768]{1,0:T(8,128)(2,1)S(1)}, f32[256,768]{1,0:T(8,128)S(1)}, f32[256,768]{1,0:T(8,128)S(1)}) fusion(bf16[256,768]{1,0:T(8,128)(2,1)S(1)} %constant_dynamic-update-slice_fusion, bf16[768,768]{1,0:T(8,128)(2,1)S(1)} %bitcast.105), kind=kOutput, calls=%fused_computation.7 | convolution fusion | flops 314769408 | bytes 3538944 | tf_op jit(solution)/shard_map/dot_general | solution.py:23
  67.8 1.1 collective-permute-done.17
  69.0 4.0 %collective-permute-done.18 = bf16[64,768]{1,0:T(8,128)(2,1)S(1)} collective-permute-done((bf16[64,768]{1,0:T(8,128)(2,1)S(1)}, bf16[64,768]{1,0:T(8,128)(2,1)S(1)}, u32[]{:S(2)}, u32[]{:S(2)}) %collective-permute-start.18) | collective-permute-done | bytes 98336 | tf_op jit(solution)/shard_map/ppermute | solution.py:66
  74.1 3.2 %collective-permute-done.19 = bf16[64,768]{1,0:T(8,128)(2,1)S(1)} collective-permute-done((bf16[64,768]{1,0:T(8,128)(2,1)S(1)}, bf16[64,768]{1,0:T(8,128)(2,1)S(1)}, u32[]{:S(2)}, u32[]{:S(2)}) %collective-permute-start.19) | collective-permute-done | bytes 98336 | tf_op jit(solution)/shard_map/ppermute | solution.py:66
  77.3 2.5 %collective-permute-start.20 = (bf16[128,768]{1,0:T(8,128)(2,1)S(1)}, bf16[128,768]{1,0:T(8,128)(2,1)S(1)}, u32[]{:S(2)}, u32[]{:S(2)}) collective-permute-start(bf16[128,768]{1,0:T(8,128)(2,1)S(1)} %pad_maximum_fusion.4), channel_id=1, source_target_pairs={{0,4},{4,0},{1,5},{5,1},{2,6},{6,2},{3,7},{7,3},{8,12},{12,8},{9,1... | collective-permute-start | bytes 589832 | tf_op jit(solution)/shard_map/ppermute | solution.py:62
  79.7 1.1 collective-permute-done.20
  83.9 2.7 %collective-permute-start.27 = (bf16[2,48,768]{2,1,0:T(8,128)(2,1)S(1)}, bf16[2,48,768]{2,1,0:T(8,128)(2,1)S(1)}, u32[]{:S(2)}, u32[]{:S(2)}) collective-permute-start(bf16[2,48,768]{2,1,0:T(8,128)(2,1)S(1)} %get-tuple-element.52), channel_id=1, source_target_pairs={{0,112},{16,0},{32,16},{48,32},{64,48},{80,64},{96,80},{112,96},{1... | collective-permute-start | bytes 442376 | tf_op jit(solution)/shard_map/ppermute | solution.py:74
  87.9 2.5 %collective-permute-done.31 = bf16[2,48,768]{2,1,0:T(8,128)(2,1)S(1)} collective-permute-done((bf16[2,48,768]{2,1,0:T(8,128)(2,1)S(1)}, bf16[2,48,768]{2,1,0:T(8,128)(2,1)S(1)}, u32[]{:S(2)}, u32[]{:S(2)}) %collective-permute-start.31) | collective-permute-done | bytes 147488 | tf_op jit(solution)/shard_map/ppermute | solution.py:74
  90.8 2.7 %collective-permute-start.28 = (bf16[2,2,48,768]{3,2,1,0:T(8,128)(2,1)S(1)}, bf16[2,2,48,768]{3,2,1,0:T(8,128)(2,1)S(1)}, u32[]{:S(2)}, u32[]{:S(2)}) collective-permute-start(bf16[2,2,48,768]{3,2,1,0:T(8,128)(2,1)S(1)} %fusion.9), channel_id=1, source_target_pairs={{0,112},{16,0},{32,16},{48,32},{64,48},{80,64},{96,80},{112,96},{1... | collective-permute-start | bytes 884744 | tf_op jit(solution)/shard_map/ppermute | solution.py:74
  93.5 1.1 collective-permute-done.22
  94.7 2.2 %collective-permute-start.25 = (bf16[16,1536]{1,0:T(8,128)(2,1)S(1)}, bf16[16,1536]{1,0:T(8,128)(2,1)S(1)}, u32[]{:S(2)}, u32[]{:S(2)}) collective-permute-start(bf16[16,1536]{1,0:T(8,128)(2,1)S(1)} %get-tuple-element.61), channel_id=1, source_target_pairs={{0,4},{4,8},{8,12},{12,0},{16,20},{20,24},{24,28},{28,16},{32,36},... | collective-permute-start | bytes 147464 | tf_op jit(solution)/shard_map/ppermute | solution.py:58
  96.8 2.5 %collective-permute-done.32 = bf16[2,2,48,768]{3,2,1,0:T(8,128)(2,1)S(1)} collective-permute-done((bf16[2,2,48,768]{3,2,1,0:T(8,128)(2,1)S(1)}, bf16[2,2,48,768]{3,2,1,0:T(8,128)(2,1)S(1)}, u32[]{:S(2)}, u32[]{:S(2)}) %collective-permute-start.32) | collective-permute-done | bytes 294944 | tf_op jit(solution)/shard_map/ppermute | solution.py:74
  99.7 4.3 %collective-permute-done.24 = bf16[16,1536]{1,0:T(8,128)(2,1)S(1)} collective-permute-done((bf16[16,1536]{1,0:T(8,128)(2,1)S(1)}, bf16[16,1536]{1,0:T(8,128)(2,1)S(1)}, u32[]{:S(2)}, u32[]{:S(2)}) %collective-permute-start.24) | collective-permute-done | bytes 49184 | tf_op jit(solution)/shard_map/ppermute | solution.py:58
  104.0 3.0 %collective-permute-done.23 = bf16[16,1536]{1,0:T(8,128)(2,1)S(1)} collective-permute-done((bf16[16,1536]{1,0:T(8,128)(2,1)S(1)}, bf16[16,1536]{1,0:T(8,128)(2,1)S(1)}, u32[]{:S(2)}, u32[]{:S(2)}) %collective-permute-start.23) | collective-permute-done | bytes 49184 | tf_op jit(solution)/shard_map/ppermute | solution.py:58
  107.4 4.6 %collective-permute-done.33 = bf16[2,2,48,768]{3,2,1,0:T(8,128)(2,1)S(1)} collective-permute-done((bf16[2,2,48,768]{3,2,1,0:T(8,128)(2,1)S(1)}, bf16[2,2,48,768]{3,2,1,0:T(8,128)(2,1)S(1)}, u32[]{:S(2)}, u32[]{:S(2)}) %collective-permute-start.33) | collective-permute-done | bytes 294944 | tf_op jit(solution)/shard_map/ppermute | solution.py:74
  112.2 2.2 %collective-permute-done.29 = bf16[2,2,48,768]{3,2,1,0:T(8,128)(2,1)S(1)} collective-permute-done((bf16[2,2,48,768]{3,2,1,0:T(8,128)(2,1)S(1)}, bf16[2,2,48,768]{3,2,1,0:T(8,128)(2,1)S(1)}, u32[]{:S(2)}, u32[]{:S(2)}) %collective-permute-start.29) | collective-permute-done | bytes 294944 | tf_op jit(solution)/shard_map/ppermute | solution.py:74
  114.5 3.0 %collective-permute-start.35 = (bf16[2,48,768]{2,1,0:T(8,128)(2,1)S(1)}, bf16[2,48,768]{2,1,0:T(8,128)(2,1)S(1)}, u32[]{:S(2)}, u32[]{:S(2)}) collective-permute-start(bf16[2,48,768]{2,1,0:T(8,128)(2,1)S(1)} %get-tuple-element.49), channel_id=1, source_target_pairs={{0,240},{16,128},{32,144},{48,160},{64,176},{80,192},{96,208},{112... | collective-permute-start | bytes 442376 | tf_op jit(solution)/shard_map/ppermute | solution.py:82
  117.5 2.7 %collective-permute-start.30 = (bf16[2,48,768]{2,1,0:T(8,128)(2,1)S(1)}, bf16[2,48,768]{2,1,0:T(8,128)(2,1)S(1)}, u32[]{:S(2)}, u32[]{:S(2)}) collective-permute-start(bf16[2,48,768]{2,1,0:T(8,128)(2,1)S(1)} %get-tuple-element.48), channel_id=1, source_target_pairs={{0,112},{16,0},{32,16},{48,32},{64,48},{80,64},{96,80},{112,96},{1... | collective-permute-start | bytes 442376 | tf_op jit(solution)/shard_map/ppermute | solution.py:74
  120.1 0.8 fusion.43
  120.9 0.9 collective-permute-done.36
  121.8 1.2 collective-permute-done.35
  123.0 1.1 collective-permute-done.30
  124.1 1.0 fusion.14
  (108 shorter events, 10.3 us)
Async XLA Ops:
  0.6 18.5 %copy-start = (bf16[1536,192]{0,1:T(8,128)(2,1)S(1)}, bf16[1536,192]{0,1:T(8,128)(2,1)}, u32[]{:S(2)}) copy-start(bf16[1536,192]{0,1:T(8,128)(2,1)} %param.12) | copy-start | bytes 1769476
  0.6 18.7 %copy-start.1 = (bf16[384,1152]{1,0:T(8,128)(2,1)S(1)}, bf16[384,1152]{1,0:T(8,128)(2,1)}, u32[]{:S(2)}) copy-start(bf16[384,1152]{1,0:T(8,128)(2,1)} %qkv_ref.1) | copy-start | bytes 2654212
  0.7 18.7 %copy-start.2 = (bf16[384,384]{1,0:T(8,128)(2,1)S(1)}, bf16[384,384]{1,0:T(8,128)(2,1)}, u32[]{:S(2)}) copy-start(bf16[384,384]{1,0:T(8,128)(2,1)} %proj_ref.1) | copy-start | bytes 884740
  1.7 14.3 %collective-permute-start.8 = (bf16[2,48,768]{2,1,0:T(8,128)(2,1)S(1)}, bf16[2,48,768]{2,1,0:T(8,128)(2,1)S(1)}, u32[]{:S(2)}, u32[]{:S(2)}) collective-permute-start(bf16[2,48,768]{2,1,0:T(8,128)(2,1)S(1)} %pad_maximum_fusion.12), channel_id=1, source_target_pairs={{0,128},{128,0},{1,129},{129,1},{2,130},{130,2},{3,131},{131,3},{4... | collective-permute-start | bytes 442376 | tf_op jit(solution)/shard_map/ppermute | solution.py:70
  7.4 11.2 %collective-permute-start = (bf16[96,384]{1,0:T(8,128)(2,1)}, bf16[96,384]{1,0:T(8,128)(2,1)S(1)}, u32[]{:S(2)}, u32[]{:S(2)}) collective-permute-start(bf16[96,384]{1,0:T(8,128)(2,1)} %get-tuple-element.13), channel_id=1, source_target_pairs={{0,12},{4,0},{8,4},{12,8},{16,28},{20,16},{24,20},{28,24},{32,44},... | collective-permute-start | bytes 221192 | tf_op jit(solution)/shard_map/ppermute | solution.py:58
  8.3 11.0 %collective-permute-start.1 = (bf16[96,384]{1,0:T(8,128)(2,1)}, bf16[96,384]{1,0:T(8,128)(2,1)}, u32[]{:S(2)}, u32[]{:S(2)}) collective-permute-start(bf16[96,384]{1,0:T(8,128)(2,1)} %get-tuple-element.14), channel_id=1, source_target_pairs={{0,240},{4,244},{8,248},{12,252},{16,0},{20,4},{24,8},{28,12},{32,... | collective-permute-start | bytes 221192 | tf_op jit(solution)/shard_map/ppermute | solution.py:58
  13.8 5.5 %collective-permute-start.2 = (bf16[96,384]{1,0:T(8,128)(2,1)}, bf16[96,384]{1,0:T(8,128)(2,1)}, u32[]{:S(2)}, u32[]{:S(2)}) collective-permute-start(bf16[96,384]{1,0:T(8,128)(2,1)} %get-tuple-element.15), channel_id=1, source_target_pairs={{0,252},{4,240},{8,244},{12,248},{16,12},{20,0},{24,4},{28,8},{32,... | collective-permute-start | bytes 221192 | tf_op jit(solution)/shard_map/ppermute | solution.py:58
  17.0 9.1 %collective-permute-start.9 = (bf16[2,2,48,768]{3,2,1,0:T(8,128)(2,1)S(1)}, bf16[2,2,48,768]{3,2,1,0:T(8,128)(2,1)}, u32[]{:S(2)}, u32[]{:S(2)}) collective-permute-start(bf16[2,2,48,768]{3,2,1,0:T(8,128)(2,1)S(1)} %get-tuple-element.54), channel_id=1, source_target_pairs={{0,112},{16,0},{32,16},{48,32},{64,48},{80,64},{96,80},{112,96},{1... | collective-permute-start | bytes 884744 | tf_op jit(solution)/shard_map/ppermute | solution.py:74
  17.1 13.3 %collective-permute-start.10 = (bf16[2,2,48,768]{3,2,1,0:T(8,128)(2,1)S(1)}, bf16[2,2,48,768]{3,2,1,0:T(8,128)(2,1)}, u32[]{:S(2)}, u32[]{:S(2)}) collective-permute-start(bf16[2,2,48,768]{3,2,1,0:T(8,128)(2,1)S(1)} %get-tuple-element.54), channel_id=1, source_target_pairs={{0,16},{16,32},{32,48},{48,64},{64,80},{80,96},{96,112},{112,0},{1... | collective-permute-start | bytes 884744 | tf_op jit(solution)/shard_map/ppermute | solution.py:74
  18.5 0.6 copy-start.7
  19.2 32.1 %collective-permute-start.3 = (bf16[192,1536]{1,0:T(8,128)(2,1)S(1)}, bf16[192,1536]{1,0:T(8,128)(2,1)S(1)}, u32[]{:S(2)}, u32[]{:S(2)}) collective-permute-start(bf16[192,1536]{1,0:T(8,128)(2,1)S(1)} %bitcast.102), channel_id=1, source_target_pairs={{0,4},{4,0},{1,5},{5,1},{2,6},{6,2},{3,7},{7,3},{8,12},{12,8},{9,1... | collective-permute-start | bytes 1769480 | tf_op jit(solution)/shard_map/ppermute | solution.py:62
  19.3 14.5 %collective-permute-start.4 = (bf16[192,1536]{1,0:T(8,128)(2,1)S(1)}, bf16[192,1536]{1,0:T(8,128)(2,1)S(1)}, u32[]{:S(2)}, u32[]{:S(2)}) collective-permute-start(bf16[192,1536]{1,0:T(8,128)(2,1)S(1)} %bitcast.103), channel_id=1, source_target_pairs={{0,8},{8,0},{1,9},{9,1},{2,10},{10,2},{3,11},{11,3},{4,12},{12,4},... | collective-permute-start | bytes 1769480 | tf_op jit(solution)/shard_map/ppermute | solution.py:66
  26.1 10.6 %collective-permute-start.11 = (bf16[2,2,48,768]{3,2,1,0:T(8,128)(2,1)}, bf16[2,2,48,768]{3,2,1,0:T(8,128)(2,1)S(1)}, u32[]{:S(2)}, u32[]{:S(2)}) collective-permute-start(bf16[2,2,48,768]{3,2,1,0:T(8,128)(2,1)} %collective-permute-done.9), channel_id=1, source_target_pairs={{0,112},{16,0},{32,16},{48,32},{64,48},{80,64},{96,80},{112,96},{1... | collective-permute-start | bytes 884744 | tf_op jit(solution)/shard_map/ppermute | solution.py:74
  30.4 9.6 %collective-permute-start.12 = (bf16[2,2,48,768]{3,2,1,0:T(8,128)(2,1)}, bf16[2,2,48,768]{3,2,1,0:T(8,128)(2,1)S(1)}, u32[]{:S(2)}, u32[]{:S(2)}) collective-permute-start(bf16[2,2,48,768]{3,2,1,0:T(8,128)(2,1)} %collective-permute-done.10), channel_id=1, source_target_pairs={{0,16},{16,32},{32,48},{48,64},{64,80},{80,96},{96,112},{112,0},{1... | collective-permute-start | bytes 884744 | tf_op jit(solution)/shard_map/ppermute | solution.py:74
  33.9 17.4 %collective-permute-start.5 = (bf16[192,1536]{1,0:T(8,128)(2,1)S(1)}, bf16[192,1536]{1,0:T(8,128)(2,1)S(1)}, u32[]{:S(2)}, u32[]{:S(2)}) collective-permute-start(bf16[192,1536]{1,0:T(8,128)(2,1)S(1)} %collective-permute-done.4.near_ref), channel_id=1, source_target_pairs={{0,4},{4,0},{1,5},{5,1},{2,6},{6,2},{3,7},{7,3},{8,12},{12,8},{9,1... | collective-permute-start | bytes 1769480 | tf_op jit(solution)/shard_map/ppermute | solution.py:62
  36.7 11.7 %collective-permute-start.13 = (bf16[2,2,48,768]{3,2,1,0:T(8,128)(2,1)S(1)}, bf16[2,2,48,768]{3,2,1,0:T(8,128)(2,1)S(1)}, u32[]{:S(2)}, u32[]{:S(2)}) collective-permute-start(bf16[2,2,48,768]{3,2,1,0:T(8,128)(2,1)S(1)} %collective-permute-done.11), channel_id=1, source_target_pairs={{0,112},{16,0},{32,16},{48,32},{64,48},{80,64},{96,80},{112,96},{1... | collective-permute-start | bytes 884744 | tf_op jit(solution)/shard_map/ppermute | solution.py:74
  40.0 8.3 %collective-permute-start.14 = (bf16[2,2,48,768]{3,2,1,0:T(8,128)(2,1)S(1)}, bf16[2,2,48,768]{3,2,1,0:T(8,128)(2,1)S(1)}, u32[]{:S(2)}, u32[]{:S(2)}) collective-permute-start(bf16[2,2,48,768]{3,2,1,0:T(8,128)(2,1)S(1)} %collective-permute-done.12), channel_id=1, source_target_pairs={{0,16},{16,32},{32,48},{48,64},{64,80},{80,96},{96,112},{112,0},{1... | collective-permute-start | bytes 884744 | tf_op jit(solution)/shard_map/ppermute | solution.py:74
  48.3 7.1 %collective-permute-start.16 = (bf16[2,48,768]{2,1,0:T(8,128)(2,1)S(1)}, bf16[2,48,768]{2,1,0:T(8,128)(2,1)S(1)}, u32[]{:S(2)}, u32[]{:S(2)}) collective-permute-start(bf16[2,48,768]{2,1,0:T(8,128)(2,1)S(1)} %slice_bitcast_fusion.2), channel_id=1, source_target_pairs={{0,16},{16,32},{32,48},{48,64},{64,80},{80,96},{96,112},{112,0},{1... | collective-permute-start | bytes 442376 | tf_op jit(solution)/shard_map/ppermute | solution.py:74
  48.4 7.0 %collective-permute-start.15 = (bf16[2,48,768]{2,1,0:T(8,128)(2,1)S(1)}, bf16[2,48,768]{2,1,0:T(8,128)(2,1)S(1)}, u32[]{:S(2)}, u32[]{:S(2)}) collective-permute-start(bf16[2,48,768]{2,1,0:T(8,128)(2,1)S(1)} %slice_bitcast_fusion.3), channel_id=1, source_target_pairs={{0,112},{16,0},{32,16},{48,32},{64,48},{80,64},{96,80},{112,96},{1... | collective-permute-start | bytes 442376 | tf_op jit(solution)/shard_map/ppermute | solution.py:74
  51.2 1.4 %copy-start.3 = (bf16[2,8,2,48,768]{4,3,1,0,2:T(8,128)(2,1)}, bf16[2,8,2,48,768]{4,3,1,0,2:T(8,128)(2,1)S(1)}, u32[]{:S(2)}) copy-start(bf16[2,8,2,48,768]{4,3,1,0,2:T(8,128)(2,1)S(1)} %copy_dynamic-update-slice_fusion) | copy-start | bytes 7077892
  55.4 3.7 %collective-permute-start.6 = (bf16[64,768]{1,0:T(8,128)(2,1)}, bf16[64,768]{1,0:T(8,128)(2,1)S(1)}, u32[]{:S(2)}, u32[]{:S(2)}) collective-permute-start(bf16[64,768]{1,0:T(8,128)(2,1)} %get-tuple-element.18), channel_id=1, source_target_pairs={{0,8},{8,0},{1,9},{9,1},{2,10},{10,2},{3,11},{11,3},{4,12},{12,4},... | collective-permute-start | bytes 294920 | tf_op jit(solution)/shard_map/ppermute | solution.py:66
  56.2 2.9 %copy-start.5 = (bf16[64,768]{1,0:T(8,128)(2,1)S(1)}, bf16[64,768]{1,0:T(8,128)(2,1)}, u32[]{:S(2)}) copy-start(bf16[64,768]{1,0:T(8,128)(2,1)} %get-tuple-element.18) | copy-start | bytes 294916
  59.1 5.2 %collective-permute-start.7 = (bf16[128,768]{1,0:T(8,128)(2,1)S(1)}, bf16[128,768]{1,0:T(8,128)(2,1)S(1)}, u32[]{:S(2)}, u32[]{:S(2)}) collective-permute-start(bf16[128,768]{1,0:T(8,128)(2,1)S(1)} %pad_maximum_fusion.3), channel_id=1, source_target_pairs={{0,4},{4,0},{1,5},{5,1},{2,6},{6,2},{3,7},{7,3},{8,12},{12,8},{9,1... | collective-permute-start | bytes 589832 | tf_op jit(solution)/shard_map/ppermute | solution.py:62
  66.8 6.6 %copy-start.4 = (bf16[64,768]{1,0:T(8,128)(2,1)S(1)}, bf16[64,768]{1,0:T(8,128)(2,1)}, u32[]{:S(2)}) copy-start(bf16[64,768]{1,0:T(8,128)(2,1)} %get-tuple-element.19) | copy-start | bytes 294916
  66.8 6.8 %copy-start.6 = (f32[64,768]{1,0:T(8,128)S(1)}, f32[64,768]{1,0:T(8,128)}, u32[]{:S(2)}) copy-start(f32[64,768]{1,0:T(8,128)} %get-tuple-element.17) | copy-start | bytes 589828
  67.3 1.5 %collective-permute-start.17 = (bf16[128,768]{1,0:T(8,128)(2,1)S(1)}, bf16[128,768]{1,0:T(8,128)(2,1)S(1)}, u32[]{:S(2)}, u32[]{:S(2)}) collective-permute-start(bf16[128,768]{1,0:T(8,128)(2,1)S(1)} %slice.141), channel_id=1, source_target_pairs={{0,4},{4,0},{1,5},{5,1},{2,6},{6,2},{3,7},{7,3},{8,12},{12,8},{9,1... | collective-permute-start | bytes 589832 | tf_op jit(solution)/shard_map/ppermute | solution.py:62
  68.9 4.1 %collective-permute-start.18 = (bf16[64,768]{1,0:T(8,128)(2,1)S(1)}, bf16[64,768]{1,0:T(8,128)(2,1)S(1)}, u32[]{:S(2)}, u32[]{:S(2)}) collective-permute-start(bf16[64,768]{1,0:T(8,128)(2,1)S(1)} %slice.259), channel_id=1, source_target_pairs={{0,8},{8,0},{1,9},{9,1},{2,10},{10,2},{3,11},{11,3},{4,12},{12,4},... | collective-permute-start | bytes 294920 | tf_op jit(solution)/shard_map/ppermute | solution.py:66
  73.7 3.6 %collective-permute-start.19 = (bf16[64,768]{1,0:T(8,128)(2,1)S(1)}, bf16[64,768]{1,0:T(8,128)(2,1)S(1)}, u32[]{:S(2)}, u32[]{:S(2)}) collective-permute-start(bf16[64,768]{1,0:T(8,128)(2,1)S(1)} %get-tuple-element.43), channel_id=1, source_target_pairs={{0,8},{8,0},{1,9},{9,1},{2,10},{10,2},{3,11},{11,3},{4,12},{12,4},... | collective-permute-start | bytes 294920 | tf_op jit(solution)/shard_map/ppermute | solution.py:66
  77.3 3.5 %collective-permute-start.20 = (bf16[128,768]{1,0:T(8,128)(2,1)S(1)}, bf16[128,768]{1,0:T(8,128)(2,1)S(1)}, u32[]{:S(2)}, u32[]{:S(2)}) collective-permute-start(bf16[128,768]{1,0:T(8,128)(2,1)S(1)} %pad_maximum_fusion.4), channel_id=1, source_target_pairs={{0,4},{4,0},{1,5},{5,1},{2,6},{6,2},{3,7},{7,3},{8,12},{12,8},{9,1... | collective-permute-start | bytes 589832 | tf_op jit(solution)/shard_map/ppermute | solution.py:62
  82.5 8.1 %collective-permute-start.21 = (bf16[128,768]{1,0:T(8,128)(2,1)S(1)}, bf16[128,768]{1,0:T(8,128)(2,1)S(1)}, u32[]{:S(2)}, u32[]{:S(2)}) collective-permute-start(bf16[128,768]{1,0:T(8,128)(2,1)S(1)} %slice.145), channel_id=1, source_target_pairs={{0,4},{4,0},{1,5},{5,1},{2,6},{6,2},{3,7},{7,3},{8,12},{12,8},{9,1... | collective-permute-start | bytes 589832 | tf_op jit(solution)/shard_map/ppermute | solution.py:62
  83.8 6.6 %collective-permute-start.31 = (bf16[2,48,768]{2,1,0:T(8,128)(2,1)S(1)}, bf16[2,48,768]{2,1,0:T(8,128)(2,1)S(1)}, u32[]{:S(2)}, u32[]{:S(2)}) collective-permute-start(bf16[2,48,768]{2,1,0:T(8,128)(2,1)S(1)} %get-tuple-element.53), channel_id=1, source_target_pairs={{0,16},{16,32},{32,48},{48,64},{64,80},{80,96},{96,112},{112,0},{1... | collective-permute-start | bytes 442376 | tf_op jit(solution)/shard_map/ppermute | solution.py:74
  83.9 6.6 %collective-permute-start.27 = (bf16[2,48,768]{2,1,0:T(8,128)(2,1)S(1)}, bf16[2,48,768]{2,1,0:T(8,128)(2,1)S(1)}, u32[]{:S(2)}, u32[]{:S(2)}) collective-permute-start(bf16[2,48,768]{2,1,0:T(8,128)(2,1)S(1)} %get-tuple-element.52), channel_id=1, source_target_pairs={{0,112},{16,0},{32,16},{48,32},{64,48},{80,64},{96,80},{112,96},{1... | collective-permute-start | bytes 442376 | tf_op jit(solution)/shard_map/ppermute | solution.py:74
  87.3 33.7 %collective-permute-start.26 = (bf16[2,48,768]{2,1,0:T(8,128)(2,1)}, bf16[2,48,768]{2,1,0:T(8,128)(2,1)}, u32[]{:S(2)}, u32[]{:S(2)}) collective-permute-start(bf16[2,48,768]{2,1,0:T(8,128)(2,1)} %select_bitcast_fusion.4), channel_id=1, source_target_pairs={{0,128},{128,0},{1,129},{129,1},{2,130},{130,2},{3,131},{131,3},{4... | collective-permute-start | bytes 442376 | tf_op jit(solution)/shard_map/ppermute | solution.py:70
  90.4 8.9 %collective-permute-start.32 = (bf16[2,2,48,768]{3,2,1,0:T(8,128)(2,1)S(1)}, bf16[2,2,48,768]{3,2,1,0:T(8,128)(2,1)S(1)}, u32[]{:S(2)}, u32[]{:S(2)}) collective-permute-start(bf16[2,2,48,768]{3,2,1,0:T(8,128)(2,1)S(1)} %pad_maximum_fusion.2), channel_id=1, source_target_pairs={{0,16},{16,32},{32,48},{48,64},{64,80},{80,96},{96,112},{112,0},{1... | collective-permute-start | bytes 884744 | tf_op jit(solution)/shard_map/ppermute | solution.py:74
  90.6 4.0 %collective-permute-start.22 = (bf16[64,768]{1,0:T(8,128)(2,1)S(1)}, bf16[64,768]{1,0:T(8,128)(2,1)S(1)}, u32[]{:S(2)}, u32[]{:S(2)}) collective-permute-start(bf16[64,768]{1,0:T(8,128)(2,1)S(1)} %slice.258), channel_id=1, source_target_pairs={{0,8},{8,0},{1,9},{9,1},{2,10},{10,2},{3,11},{11,3},{4,12},{12,4},... | collective-permute-start | bytes 294920 | tf_op jit(solution)/shard_map/ppermute | solution.py:66
  90.8 16.5 %collective-permute-start.28 = (bf16[2,2,48,768]{3,2,1,0:T(8,128)(2,1)S(1)}, bf16[2,2,48,768]{3,2,1,0:T(8,128)(2,1)S(1)}, u32[]{:S(2)}, u32[]{:S(2)}) collective-permute-start(bf16[2,2,48,768]{3,2,1,0:T(8,128)(2,1)S(1)} %fusion.9), channel_id=1, source_target_pairs={{0,112},{16,0},{32,16},{48,32},{64,48},{80,64},{96,80},{112,96},{1... | collective-permute-start | bytes 884744 | tf_op jit(solution)/shard_map/ppermute | solution.py:74
  94.7 4.9 %collective-permute-start.25 = (bf16[16,1536]{1,0:T(8,128)(2,1)S(1)}, bf16[16,1536]{1,0:T(8,128)(2,1)S(1)}, u32[]{:S(2)}, u32[]{:S(2)}) collective-permute-start(bf16[16,1536]{1,0:T(8,128)(2,1)S(1)} %get-tuple-element.61), channel_id=1, source_target_pairs={{0,4},{4,8},{8,12},{12,0},{16,20},{20,24},{24,28},{28,16},{32,36},... | collective-permute-start | bytes 147464 | tf_op jit(solution)/shard_map/ppermute | solution.py:58
  96.8 7.2 %collective-permute-start.24 = (bf16[16,1536]{1,0:T(8,128)(2,1)S(1)}, bf16[16,1536]{1,0:T(8,128)(2,1)S(1)}, u32[]{:S(2)}, u32[]{:S(2)}) collective-permute-start(bf16[16,1536]{1,0:T(8,128)(2,1)S(1)} %get-tuple-element.59), channel_id=1, source_target_pairs={{0,16},{4,20},{8,24},{12,28},{16,32},{20,36},{24,40},{28,44},{32,4... | collective-permute-start | bytes 147464 | tf_op jit(solution)/shard_map/ppermute | solution.py:58
  99.3 7.7 %collective-permute-start.23 = (bf16[16,1536]{1,0:T(8,128)(2,1)S(1)}, bf16[16,1536]{1,0:T(8,128)(2,1)S(1)}, u32[]{:S(2)}, u32[]{:S(2)}) collective-permute-start(bf16[16,1536]{1,0:T(8,128)(2,1)S(1)} %get-tuple-element.58), channel_id=1, source_target_pairs={{0,20},{4,24},{8,28},{12,16},{16,36},{20,40},{24,44},{28,32},{32,5... | collective-permute-start | bytes 147464 | tf_op jit(solution)/shard_map/ppermute | solution.py:58
  99.6 12.5 %collective-permute-start.33 = (bf16[2,2,48,768]{3,2,1,0:T(8,128)(2,1)S(1)}, bf16[2,2,48,768]{3,2,1,0:T(8,128)(2,1)S(1)}, u32[]{:S(2)}, u32[]{:S(2)}) collective-permute-start(bf16[2,2,48,768]{3,2,1,0:T(8,128)(2,1)S(1)} %maximum_add_fusion.2), channel_id=1, source_target_pairs={{0,16},{16,32},{32,48},{48,64},{64,80},{80,96},{96,112},{112,0},{1... | collective-permute-start | bytes 884744 | tf_op jit(solution)/shard_map/ppermute | solution.py:74
  107.3 7.1 %collective-permute-start.29 = (bf16[2,2,48,768]{3,2,1,0:T(8,128)(2,1)S(1)}, bf16[2,2,48,768]{3,2,1,0:T(8,128)(2,1)S(1)}, u32[]{:S(2)}, u32[]{:S(2)}) collective-permute-start(bf16[2,2,48,768]{3,2,1,0:T(8,128)(2,1)S(1)} %maximum_add_fusion), channel_id=1, source_target_pairs={{0,112},{16,0},{32,16},{48,32},{64,48},{80,64},{96,80},{112,96},{1... | collective-permute-start | bytes 884744 | tf_op jit(solution)/shard_map/ppermute | solution.py:74
  112.2 9.7 %collective-permute-start.36 = (bf16[2,48,768]{2,1,0:T(8,128)(2,1)S(1)}, bf16[2,48,768]{2,1,0:T(8,128)(2,1)S(1)}, u32[]{:S(2)}, u32[]{:S(2)}) collective-permute-start(bf16[2,48,768]{2,1,0:T(8,128)(2,1)S(1)} %get-tuple-element.51), channel_id=1, source_target_pairs={{0,144},{16,160},{32,176},{48,192},{64,208},{80,224},{96,240},{112... | collective-permute-start | bytes 442376 | tf_op jit(solution)/shard_map/ppermute | solution.py:82
  114.5 8.5 %collective-permute-start.35 = (bf16[2,48,768]{2,1,0:T(8,128)(2,1)S(1)}, bf16[2,48,768]{2,1,0:T(8,128)(2,1)S(1)}, u32[]{:S(2)}, u32[]{:S(2)}) collective-permute-start(bf16[2,48,768]{2,1,0:T(8,128)(2,1)S(1)} %get-tuple-element.49), channel_id=1, source_target_pairs={{0,240},{16,128},{32,144},{48,160},{64,176},{80,192},{96,208},{112... | collective-permute-start | bytes 442376 | tf_op jit(solution)/shard_map/ppermute | solution.py:82
  117.5 5.5 %collective-permute-start.34 = (bf16[2,48,768]{2,1,0:T(8,128)(2,1)S(1)}, bf16[2,48,768]{2,1,0:T(8,128)(2,1)S(1)}, u32[]{:S(2)}, u32[]{:S(2)}) collective-permute-start(bf16[2,48,768]{2,1,0:T(8,128)(2,1)S(1)} %get-tuple-element.50), channel_id=1, source_target_pairs={{0,16},{16,32},{32,48},{48,64},{64,80},{80,96},{96,112},{112,0},{1... | collective-permute-start | bytes 442376 | tf_op jit(solution)/shard_map/ppermute | solution.py:74
  117.5 6.6 %collective-permute-start.30 = (bf16[2,48,768]{2,1,0:T(8,128)(2,1)S(1)}, bf16[2,48,768]{2,1,0:T(8,128)(2,1)S(1)}, u32[]{:S(2)}, u32[]{:S(2)}) collective-permute-start(bf16[2,48,768]{2,1,0:T(8,128)(2,1)S(1)} %get-tuple-element.48), channel_id=1, source_target_pairs={{0,112},{16,0},{32,16},{48,32},{64,48},{80,64},{96,80},{112,96},{1... | collective-permute-start | bytes 442376 | tf_op jit(solution)/shard_map/ppermute | solution.py:74

commit v3 on v2

--- a/solution.py
+++ b/solution.py
@@ -16,6 +16,7 @@
 eps_norm = 1e-05
 eps_unit = 1e-06
 BF = jnp.bfloat16
+LIMIT = 24 * 2**20
 F32 = jnp.float32
 
 
@@ -45,8 +46,12 @@
     return inverse * (upstream - first_mean - normed * second_mean)
 
 
-def exact_gelu(value):
-    return jax.nn.gelu(value, approximate=False)
+def in_vmem(array):
+    return pltpu.with_memory_space_constraint(array, pltpu.VMEM)
+
+
+def vmem(shape, dtype):
+    return pltpu.VMEM(shape, dtype)
 
 
 def to_grid(array, dr, dc):
@@ -83,38 +88,33 @@
 
 
 def gather_cols(rows):
-    other = swap_xl(rows)
-    near = jnp.concatenate([rows, other], axis=0)
-    across = swap_core(near)
-    return jnp.concatenate([near, across], axis=0)
-
-
-def scatter_cols(rows):
-    rows = rows.astype(BF)
-    half, quarter = rows.shape[0] // 2, rows.shape[0] // 4
-    near = rows[:half].astype(F32) + swap_core(rows[half:]).astype(F32)
+    near = jnp.concatenate([rows, swap_xl(rows)], axis=0)
+    return jnp.concatenate([near, swap_core(near)], axis=0)
+
+
+def scatter_cols(low, high):
+    quarter = low.shape[0] // 2
+    near = low.astype(F32) + swap_core(high).astype(F32)
     return near[:quarter] + swap_xl(near[quarter:].astype(BF)).astype(F32)
 
 
 def gather_rows(shard):
     other = swap_half(shard)
-    first = lax.axis_index("xh") == 0
-    own = jnp.stack([jnp.where(first, shard, other), jnp.where(first, other, shard)])
-    z = lax.axis_index("z")
-    full = jnp.zeros((NX, NZ, *shard.shape), shard.dtype)
-
-    def put(full, block, k):
-        return lax.dynamic_update_slice_in_dim(full, block[:, None], (z + k) % NZ, 1)
-
-    full = put(full, own, 0)
+    own = pl.pallas_call(
+        pair_kernel,
+        out_shape=vmem((NX, *shard.shape), shard.dtype),
+        in_specs=whole(2),
+        out_specs=whole(1)[0],
+        compiler_params=pltpu.CompilerParams(vmem_limit_bytes=LIMIT),
+        name="pair",
+    )(in_vmem(shard), in_vmem(other))
+    pieces = [own]
     left = right = own
-    for k in (1, 2, 3):
+    for _ in range(3):
         left, right = along_z(left, -1), along_z(right, 1)
-        full = put(full, left, k)
-        full = put(full, right, NZ - k)
+        pieces += [left, right]
     far = [along_z(left[0], -1), along_z(right[1], 1)]
-    far = jnp.stack(far)
-    return put(full, far, 4)
+    return pieces + far
 
 
 def scatter_rows(terms):
@@ -148,6 +148,44 @@
     for part in near + cross:
         total = total + part.astype(F32)
     return total
+
+
+def pair_kernel(own_ref, other_ref, out_ref):
+    first = lax.axis_index("xh") == 0
+    out_ref[0] = jnp.where(first, own_ref[...], other_ref[...])
+    out_ref[1] = jnp.where(first, other_ref[...], own_ref[...])
+
+
+def forward_kernel(*refs):
+    level, near, across = refs[:3]
+    pieces = refs[3:10]
+    far = refs[10:12]
+    level_b, up, down, hidden_ref, slope_ref, low_ref, high_ref = refs[12:]
+    own = level.shape[0]
+    level_b[:own] = level[...]
+    level_b[own : 2 * own] = near[...]
+    level_b[2 * own :] = across[...]
+    z = lax.axis_index("z")
+    rows = pieces[0].shape[2]
+
+    def put(piece, half, k):
+        start = pl.multiple_of((half * NZ + lax.rem(z + k, NZ)) * rows, 16)
+        up[pl.ds(start, rows), :] = piece[0]
+        down[pl.ds(start, rows), :] = piece[1]
+
+    for piece, k in zip(pieces, (0, 1, 7, 2, 6, 3, 5)):
+        for half in (0, 1):
+            put(piece[half], half, k)
+    put(far[0][...], 0, 4)
+    put(far[1][...], 1, 4)
+    pre = dot(level_b[...], up[...])
+    share = 0.5 + 0.5 * lax.erf(pre * 0.7071067811865476)
+    slope_ref[...] = share + pre * (0.3989422804014327 * jnp.exp(-0.5 * pre * pre))
+    hidden = (pre * share).astype(BF)
+    hidden_ref[...] = hidden
+    sums = dot_nt(hidden, down[...]).astype(BF)
+    low_ref[...] = sums[: 2 * own]
+    high_ref[...] = sums[2 * own :]
 
 
 def order_kernel(fields_ref, cot_ref, *outs):
@@ -214,10 +252,6 @@
     bf_ref[...] = level.astype(BF)
 
 
-def in_vmem(array):
-    return pltpu.with_memory_space_constraint(array, pltpu.VMEM)
-
-
 def whole(count):
     return [pl.BlockSpec(memory_space=pltpu.VMEM)] * count
 
@@ -230,9 +264,10 @@
 
     tile_quads = pl.pallas_call(
         order_kernel,
-        out_shape=[jax.ShapeDtypeStruct((96, channels), BF)] * 4,
+        out_shape=[vmem((96, channels), BF)] * 4,
         in_specs=whole(2),
         out_specs=whole(4),
+        compiler_params=pltpu.CompilerParams(vmem_limit_bytes=LIMIT),
         name="order",
     )(fields.reshape(tokens, channels), cotangent.reshape(own, wide))
 
@@ -255,9 +290,6 @@
     x = to_window(tile_quads)
 
     weights = gather_rows(jnp.stack([w_up, w_down.T]))
-    up_full = weights[:, :, 0].reshape(wide, -1)
-    down_full = weights[:, :, 1].reshape(wide, -1)
-
     merge_own = w_merge.T
     merge_near = swap_xl(merge_own)
     merge_core = swap_core(merge_own)
@@ -266,8 +298,8 @@
     merged, cot = pl.pallas_call(
         window_kernel,
         out_shape=[
-            jax.ShapeDtypeStruct((own, 4 * channels), BF),
-            jax.ShapeDtypeStruct((own, wide), BF),
+            vmem((own, 4 * channels), BF),
+            vmem((own, wide), BF),
         ],
         in_specs=[pl.BlockSpec(memory_space=pltpu.SMEM)] + whole(6),
         out_specs=whole(2),
@@ -276,40 +308,59 @@
             transcendentals=tokens * tokens * 6,
             bytes_accessed=2_000_000,
         ),
+        compiler_params=pltpu.CompilerParams(vmem_limit_bytes=LIMIT),
         name="window",
     )(
         logit_scale,
-        *x,
+        *(in_vmem(q) for q in x),
         in_vmem(w_qkv),
         in_vmem(w_proj),
     )
     level, level_own = pl.pallas_call(
         level_kernel,
-        out_shape=[jax.ShapeDtypeStruct((own, wide), F32), jax.ShapeDtypeStruct((own, wide), BF)],
+        out_shape=[vmem((own, wide), F32), vmem((own, wide), BF)],
         in_specs=whole(5),
         out_specs=whole(2),
         cost_estimate=pl.CostEstimate(
             flops=8 * own * channels * wide, transcendentals=own, bytes_accessed=3_000_000
         ),
+        compiler_params=pltpu.CompilerParams(vmem_limit_bytes=LIMIT),
         name="level",
-    )(merged, *(in_vmem(w) for w in (merge_own, merge_core, merge_near, merge_far)))
-    level_b = gather_cols(level_own)
-
-    hidden_pre = dot(level_b, up_full)
-    hidden = exact_gelu(hidden_pre).astype(BF)
-
-    branch_norm, branch_inv = layer_norm(scatter_cols(dot_nt(hidden, down_full)))
+    )(in_vmem(merged), *(in_vmem(w) for w in (merge_own, merge_core, merge_near, merge_far)))
+    level_near = swap_xl(level_own)
+    level_across = swap_core(jnp.concatenate([level_own, level_near], axis=0))
+    hid = w_up.shape[1]
+    level_b, up_full, down_full, hidden, gelu_slope, low, high = pl.pallas_call(
+        forward_kernel,
+        out_shape=[
+            vmem((tokens, wide), BF),
+            vmem((wide, hid), BF),
+            vmem((wide, hid), BF),
+            vmem((tokens, hid), BF),
+            vmem((tokens, hid), F32),
+            vmem((2 * own, wide), BF),
+            vmem((2 * own, wide), BF),
+        ],
+        in_specs=whole(12),
+        out_specs=whole(7),
+        cost_estimate=pl.CostEstimate(
+            flops=4 * tokens * wide * hid, transcendentals=2 * tokens * hid, bytes_accessed=6_000_000
+        ),
+        compiler_params=pltpu.CompilerParams(vmem_limit_bytes=LIMIT),
+        name="forward",
+    )(*(in_vmem(v) for v in (level_own, level_near, level_across, *weights)))
+
+    branch_norm, branch_inv = layer_norm(scatter_cols(low, high))
     coarse = level + branch_norm
     upstream = cot.astype(F32)
     slope_own = norm_slope(upstream, branch_norm, branch_inv).astype(BF)
     slope_out = gather_cols(slope_own)
-    slope_hidden = dot(slope_out, down_full)
-    _, pullback = jax.vjp(exact_gelu, hidden_pre)
-    slope_pre = pullback(slope_hidden)[0].astype(BF)
+    slope_pre = (gelu_slope * dot(slope_out, down_full)).astype(BF)
     term_down = dot_tn(slope_out, hidden).astype(BF)
     term_up = dot_tn(level_b, slope_pre).astype(BF)
     grads = scatter_rows((term_down, term_up))
-    grad_coarse = upstream + scatter_cols(dot_nt(slope_pre, up_full))
+    sums = dot_nt(slope_pre, up_full).astype(BF)
+    grad_coarse = upstream + scatter_cols(sums[: 2 * own], sums[2 * own :])
 
     both = jnp.concatenate([coarse, grad_coarse], axis=1).astype(BF)
     quads = to_tile([both[k * 16 : (k + 1) * 16] for k in range(4)])

time: 127 us -> 148 us (1.17)
  waiting for transfers between devices: 46.3 us -> 68.3 us
  starting transfers between devices: 48.1 us -> 56.8 us
  Pallas kernels: 11.1 us -> 7.74 us
  local copies, waits for them, and re-layouts: 8.36 us -> 5.11 us
  matrix products: 5.06 us -> 3.27 us
    ppermute x2, waiting for transfers between devices: 0.01 us -> 15.1 us  [swap_half(): return lax.ppermute(array, 'xh', [(0, 1), (1, 0)])]
    ppermute x6, waiting for transfers between devices: 7.27 us -> 13.4 us  [to_grid(): return lax.ppermute(array, GRID, pairs)]
    ppermute x16, starting transfers between devices: 20.3 us -> 26.3 us  [along_z(): return lax.ppermute(array, 'z', [(i, (i + step) % NZ) for i in range(NZ)])]
    ppermute x16, waiting for transfers between devices: 23 us -> 27.7 us  [along_z(): return lax.ppermute(array, 'z', [(i, (i + step) % NZ) for i in range(NZ)])]
    pallas_call x3 -> x5, Pallas kernels: 11.1 us -> 7.74 us  [the longest x1 5.21 us: whole_step(): pl.pallas_call(window_kernel, out_shape=[vmem((own, 4 * channels), BF), v...]
    ppermute x5, waiting for transfers between devices: 10.8 us -> 7.9 us  [swap_xl(): return lax.ppermute(array, 'xl', [(0, 1), (1, 0)])]
    ppermute x5, starting transfers between devices: 0.56 us -> 2.82 us  [swap_xl(): return lax.ppermute(array, 'xl', [(0, 1), (1, 0)])]
    dynamic_update_slice x7 -> x0, local copies, waits for them, and re-layouts: 2.12 us -> none  [put(): lax.dynamic_update_slice_in_dim(full, block[:, None], (z + k) % NZ, 1)]
  transfers between devices with their start and end apart: 37 -> 37, of which waited for: 20 -> 22; matrix products, arithmetic and copies ran while one was open for 7% -> 3% of each run, Pallas kernels for 9% -> 5%
where the time goes in v3:
time: 148 us; the launch traced here: 147 us
  waiting for transfers between devices  68.3 us (46%)
  starting transfers between devices  56.8 us (38%)
  Pallas kernels  7.74 us (5%)
  local copies, waits for them, and re-layouts  5.11 us (3%)
  other arithmetic  4.69 us (3%)
  matrix products  3.27 us (2%)
    ppermute x16, waiting for transfers between devices, along_z(): return lax.ppermute(array, 'z', [(i, (i + step) % NZ) for i in range(NZ)])  27.7 us
    ppermute x16, starting transfers between devices, along_z(): return lax.ppermute(array, 'z', [(i, (i + step) % NZ) for i in range(NZ)])  26.3 us
    ppermute x2, waiting for transfers between devices, swap_half(): return lax.ppermute(array, 'xh', [(0, 1), (1, 0)])  15.1 us
    ppermute x6, waiting for transfers between devices, to_grid(): return lax.ppermute(array, GRID, pairs)  13.4 us
    ppermute x6, starting transfers between devices, to_grid(): return lax.ppermute(array, GRID, pairs)  12.2 us
    ppermute x6, starting transfers between devices, swap_core(): return lax.ppermute(array, 'core', [(0, 1), (1, 0)])  9.38 us
    ppermute x5, waiting for transfers between devices, swap_xl(): return lax.ppermute(array, 'xl', [(0, 1), (1, 0)])  7.9 us
    pallas_call x1, Pallas kernels, whole_step(): pl.pallas_call(window_kernel, out_shape=[vmem((own, 4 * channels), BF), v...  5.21 us
  transfers between devices with their start and end apart: 37, of which 22 were waited for; matrix products, arithmetic and copies ran while one was open for 3% of the time, Pallas kernels for 5%

profile of v3, /device:TPU:1, one launch (start us, length us, event | category | flops | bytes accessed | tf_op | source)
XLA Modules:
  0.0 147.0 jit_solution(16535715601762451024)
XLA Ops:
  0.7 2.1 %collective-permute-start.4 = (bf16[192,1536]{1,0:T(8,128)(2,1)}, bf16[192,1536]{1,0:T(8,128)(2,1)S(1)}, u32[]{:S(2)}, u32[]{:S(2)}) collective-permute-start(bf16[192,1536]{1,0:T(8,128)(2,1)} %bitcast.64), channel_id=1, source_target_pairs={{0,8},{8,0},{1,9},{9,1},{2,10},{10,2},{3,11},{11,3},{4,12},{12,4},... | collective-permute-start | bytes 1769480 | tf_op jit(solution)/shard_map/ppermute | solution.py:71
  2.8 0.9 pad_maximum_fusion.9.own_ref
  3.7 2.5 %collective-permute-start.8 = (bf16[2,48,768]{2,1,0:T(8,128)(2,1)S(1)}, bf16[2,48,768]{2,1,0:T(8,128)(2,1)S(1)}, u32[]{:S(2)}, u32[]{:S(2)}) collective-permute-start(bf16[2,48,768]{2,1,0:T(8,128)(2,1)S(1)} %pad_maximum_fusion.9.own_ref), channel_id=1, source_target_pairs={{0,128},{128,0},{1,129},{129,1},{2,130},{130,2},{3,131},{131,3},{4... | collective-permute-start | bytes 442376 | tf_op jit(solution)/shard_map/ppermute | solution.py:75
  6.3 15.1 %collective-permute-done.8.other_ref = bf16[2,48,768]{2,1,0:T(8,128)(2,1)S(1)} collective-permute-done((bf16[2,48,768]{2,1,0:T(8,128)(2,1)S(1)}, bf16[2,48,768]{2,1,0:T(8,128)(2,1)S(1)}, u32[]{:S(2)}, u32[]{:S(2)}) %collective-permute-start.8) | collective-permute-done | bytes 147488 | tf_op jit(solution)/shard_map/ppermute | solution.py:75
  21.4 5.7 %collective-permute-start.9 = (bf16[2,2,48,768]{3,2,1,0:T(8,128)(2,1)S(1)}, bf16[2,2,48,768]{3,2,1,0:T(8,128)(2,1)S(1)}, u32[]{:S(2)}, u32[]{:S(2)}) collective-permute-start(bf16[2,2,48,768]{3,2,1,0:T(8,128)(2,1)S(1)} %pair.1.refs_3_), channel_id=1, source_target_pairs={{0,112},{16,0},{32,16},{48,32},{64,48},{80,64},{96,80},{112,96},{1... | collective-permute-start | bytes 884744 | tf_op jit(solution)/shard_map/ppermute | solution.py:79
  27.0 1.8 %collective-permute-start.3 = (bf16[192,1536]{1,0:T(8,128)(2,1)}, bf16[192,1536]{1,0:T(8,128)(2,1)S(1)}, u32[]{:S(2)}, u32[]{:S(2)}) collective-permute-start(bf16[192,1536]{1,0:T(8,128)(2,1)} %bitcast.65), channel_id=1, source_target_pairs={{0,4},{4,0},{1,5},{5,1},{2,6},{6,2},{3,7},{7,3},{8,12},{12,8},{9,1... | collective-permute-start | bytes 1769480 | tf_op jit(solution)/shard_map/ppermute | solution.py:67
  28.9 2.9 %collective-permute-done.9.refs_4_ = bf16[2,2,48,768]{3,2,1,0:T(8,128)(2,1)S(1)} collective-permute-done((bf16[2,2,48,768]{3,2,1,0:T(8,128)(2,1)S(1)}, bf16[2,2,48,768]{3,2,1,0:T(8,128)(2,1)S(1)}, u32[]{:S(2)}, u32[]{:S(2)}) %collective-permute-start.9) | collective-permute-done | bytes 294944 | tf_op jit(solution)/shard_map/ppermute | solution.py:79
  31.9 3.4 %collective-permute-start.11 = (bf16[2,2,48,768]{3,2,1,0:T(8,128)(2,1)S(1)}, bf16[2,2,48,768]{3,2,1,0:T(8,128)(2,1)S(1)}, u32[]{:S(2)}, u32[]{:S(2)}) collective-permute-start(bf16[2,2,48,768]{3,2,1,0:T(8,128)(2,1)S(1)} %collective-permute-done.9.refs_4_), channel_id=1, source_target_pairs={{0,112},{16,0},{32,16},{48,32},{64,48},{80,64},{96,80},{112,96},{1... | collective-permute-start | bytes 884744 | tf_op jit(solution)/shard_map/ppermute | solution.py:79
  35.3 4.0 %collective-permute-done.11.refs_6_ = bf16[2,2,48,768]{3,2,1,0:T(8,128)(2,1)S(1)} collective-permute-done((bf16[2,2,48,768]{3,2,1,0:T(8,128)(2,1)S(1)}, bf16[2,2,48,768]{3,2,1,0:T(8,128)(2,1)S(1)}, u32[]{:S(2)}, u32[]{:S(2)}) %collective-permute-start.11) | collective-permute-done | bytes 294944 | tf_op jit(solution)/shard_map/ppermute | solution.py:79
  39.3 3.4 %collective-permute-start.13 = (bf16[2,2,48,768]{3,2,1,0:T(8,128)(2,1)S(1)}, bf16[2,2,48,768]{3,2,1,0:T(8,128)(2,1)S(1)}, u32[]{:S(2)}, u32[]{:S(2)}) collective-permute-start(bf16[2,2,48,768]{3,2,1,0:T(8,128)(2,1)S(1)} %collective-permute-done.11.refs_6_), channel_id=1, source_target_pairs={{0,112},{16,0},{32,16},{48,32},{64,48},{80,64},{96,80},{112,96},{1... | collective-permute-start | bytes 884744 | tf_op jit(solution)/shard_map/ppermute | solution.py:79
  42.7 1.0 copy-done.1
  43.7 0.9 copy-done.2
  44.8 3.6 %collective-permute-start = (bf16[96,384]{1,0:T(8,128)(2,1)S(1)}, bf16[96,384]{1,0:T(8,128)(2,1)S(1)}, u32[]{:S(2)}, u32[]{:S(2)}) collective-permute-start(bf16[96,384]{1,0:T(8,128)(2,1)S(1)} %get-tuple-element.20), channel_id=1, source_target_pairs={{0,12},{4,0},{8,4},{12,8},{16,28},{20,16},{24,20},{28,24},{32,44},... | collective-permute-start | bytes 221192 | tf_op jit(solution)/shard_map/ppermute | solution.py:63
  48.4 1.9 %collective-permute-done.x1 = bf16[96,384]{1,0:T(8,128)(2,1)S(1)} collective-permute-done((bf16[96,384]{1,0:T(8,128)(2,1)S(1)}, bf16[96,384]{1,0:T(8,128)(2,1)S(1)}, u32[]{:S(2)}, u32[]{:S(2)}) %collective-permute-start) | collective-permute-done | bytes 73760 | tf_op jit(solution)/shard_map/ppermute | solution.py:63
  50.3 1.2 collective-permute-start.1
  51.5 2.5 %collective-permute-done.1.x2 = bf16[96,384]{1,0:T(8,128)(2,1)S(1)} collective-permute-done((bf16[96,384]{1,0:T(8,128)(2,1)S(1)}, bf16[96,384]{1,0:T(8,128)(2,1)S(1)}, u32[]{:S(2)}, u32[]{:S(2)}) %collective-permute-start.1) | collective-permute-done | bytes 73760 | tf_op jit(solution)/shard_map/ppermute | solution.py:63
  54.0 4.4 %collective-permute-start.2 = (bf16[96,384]{1,0:T(8,128)(2,1)S(1)}, bf16[96,384]{1,0:T(8,128)(2,1)S(1)}, u32[]{:S(2)}, u32[]{:S(2)}) collective-permute-start(bf16[96,384]{1,0:T(8,128)(2,1)S(1)} %get-tuple-element.22), channel_id=1, source_target_pairs={{0,252},{4,240},{8,244},{12,248},{16,12},{20,0},{24,4},{28,8},{32,... | collective-permute-start | bytes 221192 | tf_op jit(solution)/shard_map/ppermute | solution.py:63
  58.4 1.8 %collective-permute-done.2.x3 = bf16[96,384]{1,0:T(8,128)(2,1)S(1)} collective-permute-done((bf16[96,384]{1,0:T(8,128)(2,1)S(1)}, bf16[96,384]{1,0:T(8,128)(2,1)S(1)}, u32[]{:S(2)}, u32[]{:S(2)}) %collective-permute-start.2) | collective-permute-done | bytes 73760 | tf_op jit(solution)/shard_map/ppermute | solution.py:63
  60.2 1.2 copy-done.4
  61.3 5.2 %window.1 = (bf16[64,1536]{1,0:T(8,128)(2,1)S(1)}, bf16[64,768]{1,0:T(8,128)(2,1)S(1)}) custom-call(f32[6]{0:T(128)S(1)} %copy-done.6, bf16[96,384]{1,0:T(8,128)(2,1)S(1)} %get-tuple-element.19.x0, bf16[96,384]{1,0:T(8,128)(2,1)S(1)} %collective-permute-done.x1, bf16[96,384]{1,0:T(8,128)(2,1)S(1)} %collective-permute-done.1.x2, ...), custom_call_target="tpu_custom_call" | custom-call | flops 402653184 | bytes 2000000 | tf_op jit(solution)/shard_map/window/pallas_call | solution.py:298
  66.9 1.1 level.1
  68.4 4.9 %collective-permute-start.15 = (bf16[2,48,768]{2,1,0:T(8,128)(2,1)S(1)}, bf16[2,48,768]{2,1,0:T(8,128)(2,1)S(1)}, u32[]{:S(2)}, u32[]{:S(2)}) collective-permute-start(bf16[2,48,768]{2,1,0:T(8,128)(2,1)S(1)} %slice_bitcast_fusion.3), channel_id=1, source_target_pairs={{0,112},{16,0},{32,16},{48,32},{64,48},{80,64},{96,80},{112,96},{1... | collective-permute-start | bytes 442376 | tf_op jit(solution)/shard_map/ppermute | solution.py:79
  73.4 1.6 %collective-permute-start.7 = (bf16[128,768]{1,0:T(8,128)(2,1)S(1)}, bf16[128,768]{1,0:T(8,128)(2,1)S(1)}, u32[]{:S(2)}, u32[]{:S(2)}) collective-permute-start(bf16[128,768]{1,0:T(8,128)(2,1)S(1)} %pad_maximum_fusion.2), channel_id=1, source_target_pairs={{0,4},{4,0},{1,5},{5,1},{2,6},{6,2},{3,7},{7,3},{8,12},{12,8},{9,1... | collective-permute-start | bytes 589832 | tf_op jit(solution)/shard_map/ppermute | solution.py:67
  74.9 3.2 %collective-permute-done.14.refs_9_ = bf16[2,2,48,768]{3,2,1,0:T(8,128)(2,1)S(1)} collective-permute-done((bf16[2,2,48,768]{3,2,1,0:T(8,128)(2,1)S(1)}, bf16[2,2,48,768]{3,2,1,0:T(8,128)(2,1)S(1)}, u32[]{:S(2)}, u32[]{:S(2)}) %collective-permute-start.14) | collective-permute-done | bytes 294944 | tf_op jit(solution)/shard_map/ppermute | solution.py:79
  78.3 5.2 %collective-permute-done.16.refs_11_ = bf16[2,48,768]{2,1,0:T(8,128)(2,1)S(1)} collective-permute-done((bf16[2,48,768]{2,1,0:T(8,128)(2,1)S(1)}, bf16[2,48,768]{2,1,0:T(8,128)(2,1)S(1)}, u32[]{:S(2)}, u32[]{:S(2)}) %collective-permute-start.16) | collective-permute-done | bytes 147488 | tf_op jit(solution)/shard_map/ppermute | solution.py:79
  83.5 1.1 forward.1
  84.6 3.0 %collective-permute-start.17 = (bf16[128,768]{1,0:T(8,128)(2,1)S(1)}, bf16[128,768]{1,0:T(8,128)(2,1)S(1)}, u32[]{:S(2)}, u32[]{:S(2)}) collective-permute-start(bf16[128,768]{1,0:T(8,128)(2,1)S(1)} %get-tuple-element.27), channel_id=1, source_target_pairs={{0,4},{4,0},{1,5},{5,1},{2,6},{6,2},{3,7},{7,3},{8,12},{12,8},{9,1... | collective-permute-start | bytes 589832 | tf_op jit(solution)/shard_map/ppermute | solution.py:67
  87.6 1.1 collective-permute-done.17
  88.8 4.0 %collective-permute-done.18 = bf16[64,768]{1,0:T(8,128)(2,1)S(1)} collective-permute-done((bf16[64,768]{1,0:T(8,128)(2,1)S(1)}, bf16[64,768]{1,0:T(8,128)(2,1)S(1)}, u32[]{:S(2)}, u32[]{:S(2)}) %collective-permute-start.18) | collective-permute-done | bytes 98336 | tf_op jit(solution)/shard_map/ppermute | solution.py:71
  93.6 3.5 %collective-permute-done.19 = bf16[64,768]{1,0:T(8,128)(2,1)S(1)} collective-permute-done((bf16[64,768]{1,0:T(8,128)(2,1)S(1)}, bf16[64,768]{1,0:T(8,128)(2,1)S(1)}, u32[]{:S(2)}, u32[]{:S(2)}) %collective-permute-start.19) | collective-permute-done | bytes 98336 | tf_op jit(solution)/shard_map/ppermute | solution.py:71
  97.1 2.5 %collective-permute-start.20 = (bf16[128,768]{1,0:T(8,128)(2,1)S(1)}, bf16[128,768]{1,0:T(8,128)(2,1)S(1)}, u32[]{:S(2)}, u32[]{:S(2)}) collective-permute-start(bf16[128,768]{1,0:T(8,128)(2,1)S(1)} %pad_maximum_fusion.3), channel_id=1, source_target_pairs={{0,4},{4,0},{1,5},{5,1},{2,6},{6,2},{3,7},{7,3},{8,12},{12,8},{9,1... | collective-permute-start | bytes 589832 | tf_op jit(solution)/shard_map/ppermute | solution.py:67
  99.6 1.1 collective-permute-done.20
  100.6 1.7 %fusion.13 = f32[256,768]{1,0:T(8,128)S(1)} fusion(bf16[768,768]{1,0:T(8,128)(2,1)} %copy-done.3, bf16[128,768]{1,0:T(8,128)(2,1)S(1)} %collective-permute-done.20, bf16[64,768]{1,0:T(8,128)(2,1)S(1)} %collective-permute-done.19, bf16[64,768]{1,0:T(8,128)(2,1)S(1)} %get-tuple-element.53), kind=kOutput, calls=%fused_computation.55 | convolution fusion | flops 303169536 | bytes 2359296 | tf_op jit(solution)/shard_map/dot_general | solution.py:24
  104.9 2.7 %collective-permute-start.27 = (bf16[2,48,768]{2,1,0:T(8,128)(2,1)S(1)}, bf16[2,48,768]{2,1,0:T(8,128)(2,1)S(1)}, u32[]{:S(2)}, u32[]{:S(2)}) collective-permute-start(bf16[2,48,768]{2,1,0:T(8,128)(2,1)S(1)} %get-tuple-element.62), channel_id=1, source_target_pairs={{0,112},{16,0},{32,16},{48,32},{64,48},{80,64},{96,80},{112,96},{1... | collective-permute-start | bytes 442376 | tf_op jit(solution)/shard_map/ppermute | solution.py:79
  108.8 2.5 %collective-permute-done.31 = bf16[2,48,768]{2,1,0:T(8,128)(2,1)S(1)} collective-permute-done((bf16[2,48,768]{2,1,0:T(8,128)(2,1)S(1)}, bf16[2,48,768]{2,1,0:T(8,128)(2,1)S(1)}, u32[]{:S(2)}, u32[]{:S(2)}) %collective-permute-start.31) | collective-permute-done | bytes 147488 | tf_op jit(solution)/shard_map/ppermute | solution.py:79
  112.6 2.6 %collective-permute-start.28 = (bf16[2,2,48,768]{3,2,1,0:T(8,128)(2,1)}, bf16[2,2,48,768]{3,2,1,0:T(8,128)(2,1)S(1)}, u32[]{:S(2)}, u32[]{:S(2)}) collective-permute-start(bf16[2,2,48,768]{3,2,1,0:T(8,128)(2,1)} %fusion.3), channel_id=1, source_target_pairs={{0,112},{16,0},{32,16},{48,32},{64,48},{80,64},{96,80},{112,96},{1... | collective-permute-start | bytes 884744 | tf_op jit(solution)/shard_map/ppermute | solution.py:79
  115.8 2.8 %collective-permute-start.25 = (bf16[16,1536]{1,0:T(8,128)(2,1)S(1)}, bf16[16,1536]{1,0:T(8,128)(2,1)S(1)}, u32[]{:S(2)}, u32[]{:S(2)}) collective-permute-start(bf16[16,1536]{1,0:T(8,128)(2,1)S(1)} %get-tuple-element.67), channel_id=1, source_target_pairs={{0,4},{4,8},{8,12},{12,0},{16,20},{20,24},{24,28},{28,16},{32,36},... | collective-permute-start | bytes 147464 | tf_op jit(solution)/shard_map/ppermute | solution.py:63
  118.6 1.8 %collective-permute-done.32 = bf16[2,2,48,768]{3,2,1,0:T(8,128)(2,1)S(1)} collective-permute-done((bf16[2,2,48,768]{3,2,1,0:T(8,128)(2,1)S(1)}, bf16[2,2,48,768]{3,2,1,0:T(8,128)(2,1)S(1)}, u32[]{:S(2)}, u32[]{:S(2)}) %collective-permute-start.32) | collective-permute-done | bytes 294944 | tf_op jit(solution)/shard_map/ppermute | solution.py:79
  120.9 4.4 %collective-permute-done.24 = bf16[16,1536]{1,0:T(8,128)(2,1)S(1)} collective-permute-done((bf16[16,1536]{1,0:T(8,128)(2,1)S(1)}, bf16[16,1536]{1,0:T(8,128)(2,1)S(1)}, u32[]{:S(2)}, u32[]{:S(2)}) %collective-permute-start.24) | collective-permute-done | bytes 49184 | tf_op jit(solution)/shard_map/ppermute | solution.py:63
  125.3 2.8 %collective-permute-done.23 = bf16[16,1536]{1,0:T(8,128)(2,1)S(1)} collective-permute-done((bf16[16,1536]{1,0:T(8,128)(2,1)S(1)}, bf16[16,1536]{1,0:T(8,128)(2,1)S(1)}, u32[]{:S(2)}, u32[]{:S(2)}) %collective-permute-start.23) | collective-permute-done | bytes 49184 | tf_op jit(solution)/shard_map/ppermute | solution.py:63
  128.6 4.6 %collective-permute-done.33 = bf16[2,2,48,768]{3,2,1,0:T(8,128)(2,1)S(1)} collective-permute-done((bf16[2,2,48,768]{3,2,1,0:T(8,128)(2,1)S(1)}, bf16[2,2,48,768]{3,2,1,0:T(8,128)(2,1)S(1)}, u32[]{:S(2)}, u32[]{:S(2)}) %collective-permute-start.33) | collective-permute-done | bytes 294944 | tf_op jit(solution)/shard_map/ppermute | solution.py:79
  133.4 2.2 %collective-permute-done.29 = bf16[2,2,48,768]{3,2,1,0:T(8,128)(2,1)S(1)} collective-permute-done((bf16[2,2,48,768]{3,2,1,0:T(8,128)(2,1)S(1)}, bf16[2,2,48,768]{3,2,1,0:T(8,128)(2,1)S(1)}, u32[]{:S(2)}, u32[]{:S(2)}) %collective-permute-start.29) | collective-permute-done | bytes 294944 | tf_op jit(solution)/shard_map/ppermute | solution.py:79
  135.7 2.9 %collective-permute-start.35 = (bf16[2,48,768]{2,1,0:T(8,128)(2,1)S(1)}, bf16[2,48,768]{2,1,0:T(8,128)(2,1)S(1)}, u32[]{:S(2)}, u32[]{:S(2)}) collective-permute-start(bf16[2,48,768]{2,1,0:T(8,128)(2,1)S(1)} %get-tuple-element.59), channel_id=1, source_target_pairs={{0,240},{16,128},{32,144},{48,160},{64,176},{80,192},{96,208},{112... | collective-permute-start | bytes 442376 | tf_op jit(solution)/shard_map/ppermute | solution.py:87
  138.6 2.7 %collective-permute-start.30 = (bf16[2,48,768]{2,1,0:T(8,128)(2,1)S(1)}, bf16[2,48,768]{2,1,0:T(8,128)(2,1)S(1)}, u32[]{:S(2)}, u32[]{:S(2)}) collective-permute-start(bf16[2,48,768]{2,1,0:T(8,128)(2,1)S(1)} %get-tuple-element.58), channel_id=1, source_target_pairs={{0,112},{16,0},{32,16},{48,32},{64,48},{80,64},{96,80},{112,96},{1... | collective-permute-start | bytes 442376 | tf_op jit(solution)/shard_map/ppermute | solution.py:79
  142.0 0.8 collective-permute-done.36
  142.9 1.3 collective-permute-done.35
  144.2 1.1 collective-permute-done.30
  145.3 1.0 fusion.7
  (91 shorter events, 10.2 us)
Async XLA Ops:
  0.6 59.5 %copy-start.6 = (f32[6]{0:T(128)S(1)}, f32[6]{0:T(128)}, u32[]{:S(2)}) copy-start(f32[6]{0:T(128)} %scale_ref.1) | copy-start | bytes 76
  0.6 59.5 %copy-start.5 = (bf16[384,384]{1,0:T(8,128)(2,1)S(1)}, bf16[384,384]{1,0:T(8,128)(2,1)}, u32[]{:S(2)}) copy-start(bf16[384,384]{1,0:T(8,128)(2,1)} %proj_ref.1) | copy-start | bytes 884740
  0.7 28.2 %collective-permute-start.4 = (bf16[192,1536]{1,0:T(8,128)(2,1)}, bf16[192,1536]{1,0:T(8,128)(2,1)S(1)}, u32[]{:S(2)}, u32[]{:S(2)}) collective-permute-start(bf16[192,1536]{1,0:T(8,128)(2,1)} %bitcast.64), channel_id=1, source_target_pairs={{0,8},{8,0},{1,9},{9,1},{2,10},{10,2},{3,11},{11,3},{4,12},{12,4},... | collective-permute-start | bytes 1769480 | tf_op jit(solution)/shard_map/ppermute | solution.py:71
  3.7 63.2 %copy-start = (bf16[1536,192]{0,1:T(8,128)(2,1)S(1)}, bf16[1536,192]{0,1:T(8,128)(2,1)}, u32[]{:S(2)}) copy-start(bf16[1536,192]{0,1:T(8,128)(2,1)} %param.12) | copy-start | bytes 1769476
  3.7 17.6 %collective-permute-start.8 = (bf16[2,48,768]{2,1,0:T(8,128)(2,1)S(1)}, bf16[2,48,768]{2,1,0:T(8,128)(2,1)S(1)}, u32[]{:S(2)}, u32[]{:S(2)}) collective-permute-start(bf16[2,48,768]{2,1,0:T(8,128)(2,1)S(1)} %pad_maximum_fusion.9.own_ref), channel_id=1, source_target_pairs={{0,128},{128,0},{1,129},{129,1},{2,130},{130,2},{3,131},{131,3},{4... | collective-permute-start | bytes 442376 | tf_op jit(solution)/shard_map/ppermute | solution.py:75
  21.4 10.5 %collective-permute-start.9 = (bf16[2,2,48,768]{3,2,1,0:T(8,128)(2,1)S(1)}, bf16[2,2,48,768]{3,2,1,0:T(8,128)(2,1)S(1)}, u32[]{:S(2)}, u32[]{:S(2)}) collective-permute-start(bf16[2,2,48,768]{3,2,1,0:T(8,128)(2,1)S(1)} %pair.1.refs_3_), channel_id=1, source_target_pairs={{0,112},{16,0},{32,16},{48,32},{64,48},{80,64},{96,80},{112,96},{1... | collective-permute-start | bytes 884744 | tf_op jit(solution)/shard_map/ppermute | solution.py:79
  27.0 8.3 %collective-permute-start.10 = (bf16[2,2,48,768]{3,2,1,0:T(8,128)(2,1)S(1)}, bf16[2,2,48,768]{3,2,1,0:T(8,128)(2,1)S(1)}, u32[]{:S(2)}, u32[]{:S(2)}) collective-permute-start(bf16[2,2,48,768]{3,2,1,0:T(8,128)(2,1)S(1)} %pair.1.refs_3_), channel_id=1, source_target_pairs={{0,16},{16,32},{32,48},{48,64},{64,80},{80,96},{96,112},{112,0},{1... | collective-permute-start | bytes 884744 | tf_op jit(solution)/shard_map/ppermute | solution.py:79
  27.0 39.8 %collective-permute-start.3 = (bf16[192,1536]{1,0:T(8,128)(2,1)}, bf16[192,1536]{1,0:T(8,128)(2,1)S(1)}, u32[]{:S(2)}, u32[]{:S(2)}) collective-permute-start(bf16[192,1536]{1,0:T(8,128)(2,1)} %bitcast.65), channel_id=1, source_target_pairs={{0,4},{4,0},{1,5},{5,1},{2,6},{6,2},{3,7},{7,3},{8,12},{12,8},{9,1... | collective-permute-start | bytes 1769480 | tf_op jit(solution)/shard_map/ppermute | solution.py:67
  28.8 38.0 %collective-permute-start.5 = (bf16[192,1536]{1,0:T(8,128)(2,1)S(1)}, bf16[192,1536]{1,0:T(8,128)(2,1)S(1)}, u32[]{:S(2)}, u32[]{:S(2)}) collective-permute-start(bf16[192,1536]{1,0:T(8,128)(2,1)S(1)} %collective-permute-done.4.near_ref), channel_id=1, source_target_pairs={{0,4},{4,0},{1,5},{5,1},{2,6},{6,2},{3,7},{7,3},{8,12},{12,8},{9,1... | collective-permute-start | bytes 1769480 | tf_op jit(solution)/shard_map/ppermute | solution.py:67
  31.9 7.4 %collective-permute-start.11 = (bf16[2,2,48,768]{3,2,1,0:T(8,128)(2,1)S(1)}, bf16[2,2,48,768]{3,2,1,0:T(8,128)(2,1)S(1)}, u32[]{:S(2)}, u32[]{:S(2)}) collective-permute-start(bf16[2,2,48,768]{3,2,1,0:T(8,128)(2,1)S(1)} %collective-permute-done.9.refs_4_), channel_id=1, source_target_pairs={{0,112},{16,0},{32,16},{48,32},{64,48},{80,64},{96,80},{112,96},{1... | collective-permute-start | bytes 884744 | tf_op jit(solution)/shard_map/ppermute | solution.py:79
  35.3 31.3 %collective-permute-start.12 = (bf16[2,2,48,768]{3,2,1,0:T(8,128)(2,1)S(1)}, bf16[2,2,48,768]{3,2,1,0:T(8,128)(2,1)S(1)}, u32[]{:S(2)}, u32[]{:S(2)}) collective-permute-start(bf16[2,2,48,768]{3,2,1,0:T(8,128)(2,1)S(1)} %collective-permute-done.10.refs_5_), channel_id=1, source_target_pairs={{0,16},{16,32},{32,48},{48,64},{64,80},{80,96},{96,112},{112,0},{1... | collective-permute-start | bytes 884744 | tf_op jit(solution)/shard_map/ppermute | solution.py:79
  39.3 29.2 %collective-permute-start.13 = (bf16[2,2,48,768]{3,2,1,0:T(8,128)(2,1)S(1)}, bf16[2,2,48,768]{3,2,1,0:T(8,128)(2,1)S(1)}, u32[]{:S(2)}, u32[]{:S(2)}) collective-permute-start(bf16[2,2,48,768]{3,2,1,0:T(8,128)(2,1)S(1)} %collective-permute-done.11.refs_6_), channel_id=1, source_target_pairs={{0,112},{16,0},{32,16},{48,32},{64,48},{80,64},{96,80},{112,96},{1... | collective-permute-start | bytes 884744 | tf_op jit(solution)/shard_map/ppermute | solution.py:79
  42.7 1.0 copy-start.1
  43.7 0.9 copy-start.2
  44.8 5.5 %collective-permute-start = (bf16[96,384]{1,0:T(8,128)(2,1)S(1)}, bf16[96,384]{1,0:T(8,128)(2,1)S(1)}, u32[]{:S(2)}, u32[]{:S(2)}) collective-permute-start(bf16[96,384]{1,0:T(8,128)(2,1)S(1)} %get-tuple-element.20), channel_id=1, source_target_pairs={{0,12},{4,0},{8,4},{12,8},{16,28},{20,16},{24,20},{28,24},{32,44},... | collective-permute-start | bytes 221192 | tf_op jit(solution)/shard_map/ppermute | solution.py:63
  50.3 3.7 %collective-permute-start.1 = (bf16[96,384]{1,0:T(8,128)(2,1)S(1)}, bf16[96,384]{1,0:T(8,128)(2,1)S(1)}, u32[]{:S(2)}, u32[]{:S(2)}) collective-permute-start(bf16[96,384]{1,0:T(8,128)(2,1)S(1)} %get-tuple-element.21), channel_id=1, source_target_pairs={{0,240},{4,244},{8,248},{12,252},{16,0},{20,4},{24,8},{28,12},{32,... | collective-permute-start | bytes 221192 | tf_op jit(solution)/shard_map/ppermute | solution.py:63
  54.0 6.2 %collective-permute-start.2 = (bf16[96,384]{1,0:T(8,128)(2,1)S(1)}, bf16[96,384]{1,0:T(8,128)(2,1)S(1)}, u32[]{:S(2)}, u32[]{:S(2)}) collective-permute-start(bf16[96,384]{1,0:T(8,128)(2,1)S(1)} %get-tuple-element.22), channel_id=1, source_target_pairs={{0,252},{4,240},{8,244},{12,248},{16,12},{20,0},{24,4},{28,8},{32,... | collective-permute-start | bytes 221192 | tf_op jit(solution)/shard_map/ppermute | solution.py:63
  60.2 1.2 copy-start.4
  66.6 11.6 %collective-permute-start.14 = (bf16[2,2,48,768]{3,2,1,0:T(8,128)(2,1)S(1)}, bf16[2,2,48,768]{3,2,1,0:T(8,128)(2,1)S(1)}, u32[]{:S(2)}, u32[]{:S(2)}) collective-permute-start(bf16[2,2,48,768]{3,2,1,0:T(8,128)(2,1)S(1)} %collective-permute-done.12.refs_7_), channel_id=1, source_target_pairs={{0,16},{16,32},{32,48},{48,64},{64,80},{80,96},{96,112},{112,0},{1... | collective-permute-start | bytes 884744 | tf_op jit(solution)/shard_map/ppermute | solution.py:79
  68.0 5.4 %collective-permute-start.6 = (bf16[64,768]{1,0:T(8,128)(2,1)S(1)}, bf16[64,768]{1,0:T(8,128)(2,1)S(1)}, u32[]{:S(2)}, u32[]{:S(2)}) collective-permute-start(bf16[64,768]{1,0:T(8,128)(2,1)S(1)} %get-tuple-element.25.refs_0_), channel_id=1, source_target_pairs={{0,8},{8,0},{1,9},{9,1},{2,10},{10,2},{3,11},{11,3},{4,12},{12,4},... | collective-permute-start | bytes 294920 | tf_op jit(solution)/shard_map/ppermute | solution.py:71
  68.4 9.9 %collective-permute-start.15 = (bf16[2,48,768]{2,1,0:T(8,128)(2,1)S(1)}, bf16[2,48,768]{2,1,0:T(8,128)(2,1)S(1)}, u32[]{:S(2)}, u32[]{:S(2)}) collective-permute-start(bf16[2,48,768]{2,1,0:T(8,128)(2,1)S(1)} %slice_bitcast_fusion.3), channel_id=1, source_target_pairs={{0,112},{16,0},{32,16},{48,32},{64,48},{80,64},{96,80},{112,96},{1... | collective-permute-start | bytes 442376 | tf_op jit(solution)/shard_map/ppermute | solution.py:79
  73.4 10.1 %collective-permute-start.7 = (bf16[128,768]{1,0:T(8,128)(2,1)S(1)}, bf16[128,768]{1,0:T(8,128)(2,1)S(1)}, u32[]{:S(2)}, u32[]{:S(2)}) collective-permute-start(bf16[128,768]{1,0:T(8,128)(2,1)S(1)} %pad_maximum_fusion.2), channel_id=1, source_target_pairs={{0,4},{4,0},{1,5},{5,1},{2,6},{6,2},{3,7},{7,3},{8,12},{12,8},{9,1... | collective-permute-start | bytes 589832 | tf_op jit(solution)/shard_map/ppermute | solution.py:67
  78.2 5.3 %collective-permute-start.16 = (bf16[2,48,768]{2,1,0:T(8,128)(2,1)S(1)}, bf16[2,48,768]{2,1,0:T(8,128)(2,1)S(1)}, u32[]{:S(2)}, u32[]{:S(2)}) collective-permute-start(bf16[2,48,768]{2,1,0:T(8,128)(2,1)S(1)} %slice_bitcast_fusion.2), channel_id=1, source_target_pairs={{0,16},{16,32},{32,48},{48,64},{64,80},{80,96},{96,112},{112,0},{1... | collective-permute-start | bytes 442376 | tf_op jit(solution)/shard_map/ppermute | solution.py:79
  84.6 8.9 %copy-start.3 = (bf16[768,768]{1,0:T(8,128)(2,1)}, bf16[768,768]{1,0:T(8,128)(2,1)S(1)}, u32[]{:S(2)}) copy-start(bf16[768,768]{1,0:T(8,128)(2,1)S(1)} %get-tuple-element.30) | copy-start | bytes 3538948
  84.6 4.1 %collective-permute-start.17 = (bf16[128,768]{1,0:T(8,128)(2,1)S(1)}, bf16[128,768]{1,0:T(8,128)(2,1)S(1)}, u32[]{:S(2)}, u32[]{:S(2)}) collective-permute-start(bf16[128,768]{1,0:T(8,128)(2,1)S(1)} %get-tuple-element.27), channel_id=1, source_target_pairs={{0,4},{4,0},{1,5},{5,1},{2,6},{6,2},{3,7},{7,3},{8,12},{12,8},{9,1... | collective-permute-start | bytes 589832 | tf_op jit(solution)/shard_map/ppermute | solution.py:67
  88.7 4.1 %collective-permute-start.18 = (bf16[64,768]{1,0:T(8,128)(2,1)S(1)}, bf16[64,768]{1,0:T(8,128)(2,1)S(1)}, u32[]{:S(2)}, u32[]{:S(2)}) collective-permute-start(bf16[64,768]{1,0:T(8,128)(2,1)S(1)} %slice.238), channel_id=1, source_target_pairs={{0,8},{8,0},{1,9},{9,1},{2,10},{10,2},{3,11},{11,3},{4,12},{12,4},... | collective-permute-start | bytes 294920 | tf_op jit(solution)/shard_map/ppermute | solution.py:71
  93.5 3.6 %collective-permute-start.19 = (bf16[64,768]{1,0:T(8,128)(2,1)S(1)}, bf16[64,768]{1,0:T(8,128)(2,1)S(1)}, u32[]{:S(2)}, u32[]{:S(2)}) collective-permute-start(bf16[64,768]{1,0:T(8,128)(2,1)S(1)} %get-tuple-element.53), channel_id=1, source_target_pairs={{0,8},{8,0},{1,9},{9,1},{2,10},{10,2},{3,11},{11,3},{4,12},{12,4},... | collective-permute-start | bytes 294920 | tf_op jit(solution)/shard_map/ppermute | solution.py:71
  97.1 3.5 %collective-permute-start.20 = (bf16[128,768]{1,0:T(8,128)(2,1)S(1)}, bf16[128,768]{1,0:T(8,128)(2,1)S(1)}, u32[]{:S(2)}, u32[]{:S(2)}) collective-permute-start(bf16[128,768]{1,0:T(8,128)(2,1)S(1)} %pad_maximum_fusion.3), channel_id=1, source_target_pairs={{0,4},{4,0},{1,5},{5,1},{2,6},{6,2},{3,7},{7,3},{8,12},{12,8},{9,1... | collective-permute-start | bytes 589832 | tf_op jit(solution)/shard_map/ppermute | solution.py:67
  103.0 8.7 %collective-permute-start.21 = (bf16[128,768]{1,0:T(8,128)(2,1)S(1)}, bf16[128,768]{1,0:T(8,128)(2,1)S(1)}, u32[]{:S(2)}, u32[]{:S(2)}) collective-permute-start(bf16[128,768]{1,0:T(8,128)(2,1)S(1)} %slice.125), channel_id=1, source_target_pairs={{0,4},{4,0},{1,5},{5,1},{2,6},{6,2},{3,7},{7,3},{8,12},{12,8},{9,1... | collective-permute-start | bytes 589832 | tf_op jit(solution)/shard_map/ppermute | solution.py:67
  104.8 6.6 %collective-permute-start.31 = (bf16[2,48,768]{2,1,0:T(8,128)(2,1)S(1)}, bf16[2,48,768]{2,1,0:T(8,128)(2,1)S(1)}, u32[]{:S(2)}, u32[]{:S(2)}) collective-permute-start(bf16[2,48,768]{2,1,0:T(8,128)(2,1)S(1)} %get-tuple-element.63), channel_id=1, source_target_pairs={{0,16},{16,32},{32,48},{48,64},{64,80},{80,96},{96,112},{112,0},{1... | collective-permute-start | bytes 442376 | tf_op jit(solution)/shard_map/ppermute | solution.py:79
  104.9 6.8 %collective-permute-start.27 = (bf16[2,48,768]{2,1,0:T(8,128)(2,1)S(1)}, bf16[2,48,768]{2,1,0:T(8,128)(2,1)S(1)}, u32[]{:S(2)}, u32[]{:S(2)}) collective-permute-start(bf16[2,48,768]{2,1,0:T(8,128)(2,1)S(1)} %get-tuple-element.62), channel_id=1, source_target_pairs={{0,112},{16,0},{32,16},{48,32},{64,48},{80,64},{96,80},{112,96},{1... | collective-permute-start | bytes 442376 | tf_op jit(solution)/shard_map/ppermute | solution.py:79
  108.2 33.8 %collective-permute-start.26 = (bf16[2,48,768]{2,1,0:T(8,128)(2,1)}, bf16[2,48,768]{2,1,0:T(8,128)(2,1)}, u32[]{:S(2)}, u32[]{:S(2)}) collective-permute-start(bf16[2,48,768]{2,1,0:T(8,128)(2,1)} %select_bitcast_fusion.4), channel_id=1, source_target_pairs={{0,128},{128,0},{1,129},{129,1},{2,130},{130,2},{3,131},{131,3},{4... | collective-permute-start | bytes 442376 | tf_op jit(solution)/shard_map/ppermute | solution.py:75
  111.4 9.1 %collective-permute-start.32 = (bf16[2,2,48,768]{3,2,1,0:T(8,128)(2,1)S(1)}, bf16[2,2,48,768]{3,2,1,0:T(8,128)(2,1)S(1)}, u32[]{:S(2)}, u32[]{:S(2)}) collective-permute-start(bf16[2,2,48,768]{3,2,1,0:T(8,128)(2,1)S(1)} %pad_maximum_fusion.1), channel_id=1, source_target_pairs={{0,16},{16,32},{32,48},{48,64},{64,80},{80,96},{96,112},{112,0},{1... | collective-permute-start | bytes 884744 | tf_op jit(solution)/shard_map/ppermute | solution.py:79
  111.8 4.0 %collective-permute-start.22 = (bf16[64,768]{1,0:T(8,128)(2,1)S(1)}, bf16[64,768]{1,0:T(8,128)(2,1)S(1)}, u32[]{:S(2)}, u32[]{:S(2)}) collective-permute-start(bf16[64,768]{1,0:T(8,128)(2,1)S(1)} %slice.237), channel_id=1, source_target_pairs={{0,8},{8,0},{1,9},{9,1},{2,10},{10,2},{3,11},{11,3},{4,12},{12,4},... | collective-permute-start | bytes 294920 | tf_op jit(solution)/shard_map/ppermute | solution.py:71
  112.6 15.8 %collective-permute-start.28 = (bf16[2,2,48,768]{3,2,1,0:T(8,128)(2,1)}, bf16[2,2,48,768]{3,2,1,0:T(8,128)(2,1)S(1)}, u32[]{:S(2)}, u32[]{:S(2)}) collective-permute-start(bf16[2,2,48,768]{3,2,1,0:T(8,128)(2,1)} %fusion.3), channel_id=1, source_target_pairs={{0,112},{16,0},{32,16},{48,32},{64,48},{80,64},{96,80},{112,96},{1... | collective-permute-start | bytes 884744 | tf_op jit(solution)/shard_map/ppermute | solution.py:79
  115.8 4.9 %collective-permute-start.25 = (bf16[16,1536]{1,0:T(8,128)(2,1)S(1)}, bf16[16,1536]{1,0:T(8,128)(2,1)S(1)}, u32[]{:S(2)}, u32[]{:S(2)}) collective-permute-start(bf16[16,1536]{1,0:T(8,128)(2,1)S(1)} %get-tuple-element.67), channel_id=1, source_target_pairs={{0,4},{4,8},{8,12},{12,0},{16,20},{20,24},{24,28},{28,16},{32,36},... | collective-permute-start | bytes 147464 | tf_op jit(solution)/shard_map/ppermute | solution.py:63
  118.6 6.7 %collective-permute-start.24 = (bf16[16,1536]{1,0:T(8,128)(2,1)S(1)}, bf16[16,1536]{1,0:T(8,128)(2,1)S(1)}, u32[]{:S(2)}, u32[]{:S(2)}) collective-permute-start(bf16[16,1536]{1,0:T(8,128)(2,1)S(1)} %get-tuple-element.65), channel_id=1, source_target_pairs={{0,16},{4,20},{8,24},{12,28},{16,32},{20,36},{24,40},{28,44},{32,4... | collective-permute-start | bytes 147464 | tf_op jit(solution)/shard_map/ppermute | solution.py:63
  120.5 7.7 %collective-permute-start.23 = (bf16[16,1536]{1,0:T(8,128)(2,1)S(1)}, bf16[16,1536]{1,0:T(8,128)(2,1)S(1)}, u32[]{:S(2)}, u32[]{:S(2)}) collective-permute-start(bf16[16,1536]{1,0:T(8,128)(2,1)S(1)} %get-tuple-element.64), channel_id=1, source_target_pairs={{0,20},{4,24},{8,28},{12,16},{16,36},{20,40},{24,44},{28,32},{32,5... | collective-permute-start | bytes 147464 | tf_op jit(solution)/shard_map/ppermute | solution.py:63
  120.8 12.4 %collective-permute-start.33 = (bf16[2,2,48,768]{3,2,1,0:T(8,128)(2,1)S(1)}, bf16[2,2,48,768]{3,2,1,0:T(8,128)(2,1)S(1)}, u32[]{:S(2)}, u32[]{:S(2)}) collective-permute-start(bf16[2,2,48,768]{3,2,1,0:T(8,128)(2,1)S(1)} %maximum_add_fusion.2), channel_id=1, source_target_pairs={{0,16},{16,32},{32,48},{48,64},{64,80},{80,96},{96,112},{112,0},{1... | collective-permute-start | bytes 884744 | tf_op jit(solution)/shard_map/ppermute | solution.py:79
  128.5 7.1 %collective-permute-start.29 = (bf16[2,2,48,768]{3,2,1,0:T(8,128)(2,1)S(1)}, bf16[2,2,48,768]{3,2,1,0:T(8,128)(2,1)S(1)}, u32[]{:S(2)}, u32[]{:S(2)}) collective-permute-start(bf16[2,2,48,768]{3,2,1,0:T(8,128)(2,1)S(1)} %maximum_add_fusion), channel_id=1, source_target_pairs={{0,112},{16,0},{32,16},{48,32},{64,48},{80,64},{96,80},{112,96},{1... | collective-permute-start | bytes 884744 | tf_op jit(solution)/shard_map/ppermute | solution.py:79
  133.3 9.6 %collective-permute-start.36 = (bf16[2,48,768]{2,1,0:T(8,128)(2,1)S(1)}, bf16[2,48,768]{2,1,0:T(8,128)(2,1)S(1)}, u32[]{:S(2)}, u32[]{:S(2)}) collective-permute-start(bf16[2,48,768]{2,1,0:T(8,128)(2,1)S(1)} %get-tuple-element.61), channel_id=1, source_target_pairs={{0,144},{16,160},{32,176},{48,192},{64,208},{80,224},{96,240},{112... | collective-permute-start | bytes 442376 | tf_op jit(solution)/shard_map/ppermute | solution.py:87
  135.7 8.5 %collective-permute-start.35 = (bf16[2,48,768]{2,1,0:T(8,128)(2,1)S(1)}, bf16[2,48,768]{2,1,0:T(8,128)(2,1)S(1)}, u32[]{:S(2)}, u32[]{:S(2)}) collective-permute-start(bf16[2,48,768]{2,1,0:T(8,128)(2,1)S(1)} %get-tuple-element.59), channel_id=1, source_target_pairs={{0,240},{16,128},{32,144},{48,160},{64,176},{80,192},{96,208},{112... | collective-permute-start | bytes 442376 | tf_op jit(solution)/shard_map/ppermute | solution.py:87
  138.6 5.6 %collective-permute-start.34 = (bf16[2,48,768]{2,1,0:T(8,128)(2,1)S(1)}, bf16[2,48,768]{2,1,0:T(8,128)(2,1)S(1)}, u32[]{:S(2)}, u32[]{:S(2)}) collective-permute-start(bf16[2,48,768]{2,1,0:T(8,128)(2,1)S(1)} %get-tuple-element.60), channel_id=1, source_target_pairs={{0,16},{16,32},{32,48},{48,64},{64,80},{80,96},{96,112},{112,0},{1... | collective-permute-start | bytes 442376 | tf_op jit(solution)/shard_map/ppermute | solution.py:79
  138.6 6.6 %collective-permute-start.30 = (bf16[2,48,768]{2,1,0:T(8,128)(2,1)S(1)}, bf16[2,48,768]{2,1,0:T(8,128)(2,1)S(1)}, u32[]{:S(2)}, u32[]{:S(2)}) collective-permute-start(bf16[2,48,768]{2,1,0:T(8,128)(2,1)S(1)} %get-tuple-element.58), channel_id=1, source_target_pairs={{0,112},{16,0},{32,16},{48,32},{64,48},{80,64},{96,80},{112,96},{1... | collective-permute-start | bytes 442376 | tf_op jit(solution)/shard_map/ppermute | solution.py:79

commit v4 on v3

--- a/solution.py
+++ b/solution.py
@@ -85,11 +85,6 @@
         for i in range(NZ):
             pairs.append((h * NZ + i, (1 - h) * NZ + (i + step) % NZ))
     return lax.ppermute(array, ROWS, pairs)
-
-
-def gather_cols(rows):
-    near = jnp.concatenate([rows, swap_xl(rows)], axis=0)
-    return jnp.concatenate([near, swap_core(near)], axis=0)
 
 
 def scatter_cols(low, high):
@@ -144,10 +139,15 @@
 
     near = [along_z(mine(left), -1), along_z(mine(right), 1)]
     cross = [across_z(theirs(left), -1), across_z(theirs(right), 1)]
-    total = mine(own).astype(F32) + own_other.astype(F32)
-    for part in near + cross:
-        total = total + part.astype(F32)
-    return total
+    shape = jax.ShapeDtypeStruct(own.shape[2:], F32)
+    return pl.pallas_call(
+        finish_kernel,
+        out_shape=[shape] * 2,
+        in_specs=whole(6),
+        out_specs=whole(2),
+        compiler_params=pltpu.CompilerParams(vmem_limit_bytes=LIMIT),
+        name="finish",
+    )(*(in_vmem(v) for v in (mine(own), own_other, *near, *cross)))
 
 
 def pair_kernel(own_ref, other_ref, out_ref):
@@ -186,6 +186,29 @@
     sums = dot_nt(hidden, down[...]).astype(BF)
     low_ref[...] = sums[: 2 * own]
     high_ref[...] = sums[2 * own :]
+
+
+def backward_kernel(*refs):
+    own_ref, near, across, level_b, up, down, hidden, gelu_slope = refs[:8]
+    down_term, up_term, low_ref, high_ref, slope = refs[8:]
+    own = own_ref.shape[0]
+    slope[:own] = own_ref[...]
+    slope[own : 2 * own] = near[...]
+    slope[2 * own :] = across[...]
+    down_term[...] = dot_tn(slope[...], hidden[...]).astype(BF)
+    pre = (gelu_slope[...] * dot(slope[...], down[...])).astype(BF)
+    up_term[...] = dot_tn(level_b[...], pre).astype(BF)
+    sums = dot_nt(pre, up[...]).astype(BF)
+    low_ref[...] = sums[: 2 * own]
+    high_ref[...] = sums[2 * own :]
+
+
+def finish_kernel(*refs):
+    total = refs[0][...].astype(F32)
+    for part in refs[1:-2]:
+        total = total + part[...].astype(F32)
+    refs[-2][...] = total[0]
+    refs[-1][...] = total[1]
 
 
 def order_kernel(fields_ref, cot_ref, *outs):
@@ -354,19 +377,47 @@
     coarse = level + branch_norm
     upstream = cot.astype(F32)
     slope_own = norm_slope(upstream, branch_norm, branch_inv).astype(BF)
-    slope_out = gather_cols(slope_own)
-    slope_pre = (gelu_slope * dot(slope_out, down_full)).astype(BF)
-    term_down = dot_tn(slope_out, hidden).astype(BF)
-    term_up = dot_tn(level_b, slope_pre).astype(BF)
-    grads = scatter_rows((term_down, term_up))
-    sums = dot_nt(slope_pre, up_full).astype(BF)
-    grad_coarse = upstream + scatter_cols(sums[: 2 * own], sums[2 * own :])
+    slope_near = swap_xl(slope_own)
+    slope_across = swap_core(jnp.concatenate([slope_own, slope_near], axis=0))
+    term_down, term_up, low, high = pl.pallas_call(
+        backward_kernel,
+        out_shape=[
+            vmem((wide, hid), BF),
+            vmem((wide, hid), BF),
+            vmem((2 * own, wide), BF),
+            vmem((2 * own, wide), BF),
+        ],
+        in_specs=whole(8),
+        out_specs=whole(4),
+        scratch_shapes=[pltpu.VMEM((tokens, wide), BF)],
+        cost_estimate=pl.CostEstimate(
+            flops=8 * tokens * wide * hid, transcendentals=0, bytes_accessed=6_000_000
+        ),
+        compiler_params=pltpu.CompilerParams(vmem_limit_bytes=LIMIT),
+        name="backward",
+    )(
+        *(
+            in_vmem(v)
+            for v in (
+                slope_own,
+                slope_near,
+                slope_across,
+                level_b,
+                up_full,
+                down_full,
+                hidden,
+                gelu_slope,
+            )
+        )
+    )
+    grad_down, grad_up = scatter_rows((term_down, term_up))
+    grad_coarse = upstream + scatter_cols(low, high)
 
     both = jnp.concatenate([coarse, grad_coarse], axis=1).astype(BF)
     quads = to_tile([both[k * 16 : (k + 1) * 16] for k in range(4)])
     both = jnp.stack(quads).reshape(2, 2, 4, 4, 2 * wide).transpose(0, 2, 1, 3, 4)
     both = both.reshape(tile_rows // 2, tile_cols // 2, 2 * wide).astype(F32)
-    return (both[..., :wide], both[..., wide:], grads[1], grads[0].T)
+    return (both[..., :wide], both[..., wide:], grad_up, grad_down.T)
 
 
 def solution(mesh):

time: 148 us -> 155 us (1.047)
  starting transfers between devices: 56.8 us -> 61.2 us
  matrix products: 3.27 us -> 0 us
  Pallas kernels: 7.74 us -> 11 us
    ppermute x2, waiting for transfers between devices: 2.08 us -> 6.02 us  [across_z(): return lax.ppermute(array, ROWS, pairs)]
    dot_general x4 -> x0, matrix products: 3.27 us -> none  [the longest x1 1.74 us: dot(): return jnp.dot(a, b, preferred_element_type=F32)]
    pallas_call x0 -> x2, Pallas kernels: none -> 3.23 us  [the longest x1 2.46 us: whole_step(): pl.pallas_call(backward_kernel, out_shape=[vmem((wide, hid), BF), vmem((w...]
    ppermute x16, waiting for transfers between devices: 27.7 us -> 25.2 us  [along_z(): return lax.ppermute(array, 'z', [(i, (i + step) % NZ) for i in range(NZ)])]
    ppermute x6, waiting for transfers between devices: 13.4 us -> 11.1 us  [to_grid(): return lax.ppermute(array, GRID, pairs)]
    ppermute x16, starting transfers between devices: 26.3 us -> 28.5 us  [along_z(): return lax.ppermute(array, 'z', [(i, (i + step) % NZ) for i in range(NZ)])]
    unnamed x14 -> x20, local copies, waits for them, and re-layouts: 3.07 us -> 5.07 us
    ppermute x5, waiting for transfers between devices: 7.9 us -> 9.45 us  [swap_xl(): return lax.ppermute(array, 'xl', [(0, 1), (1, 0)])]
  transfers between devices with their start and end apart: 37 -> 37, of which waited for: 22 -> 23; matrix products, arithmetic and copies ran while one was open for 3% -> 3% of each run, Pallas kernels for 5% -> 4%
where the time goes in v4:
time: 155 us; the launch traced here: 153 us
  waiting for transfers between devices  69.3 us (45%)
  starting transfers between devices  61.2 us (39%)
  Pallas kernels  11 us (7%)
  local copies, waits for them, and re-layouts  6.34 us (4%)
  other arithmetic  4.22 us (3%)
    ppermute x16, starting transfers between devices, along_z(): return lax.ppermute(array, 'z', [(i, (i + step) % NZ) for i in range(NZ)])  28.5 us
    ppermute x16, waiting for transfers between devices, along_z(): return lax.ppermute(array, 'z', [(i, (i + step) % NZ) for i in range(NZ)])  25.2 us
    ppermute x2, waiting for transfers between devices, swap_half(): return lax.ppermute(array, 'xh', [(0, 1), (1, 0)])  15.1 us
    ppermute x6, starting transfers between devices, to_grid(): return lax.ppermute(array, GRID, pairs)  12.6 us
    ppermute x6, waiting for transfers between devices, to_grid(): return lax.ppermute(array, GRID, pairs)  11.1 us
    ppermute x5, waiting for transfers between devices, swap_xl(): return lax.ppermute(array, 'xl', [(0, 1), (1, 0)])  9.45 us
    ppermute x6, starting transfers between devices, swap_core(): return lax.ppermute(array, 'core', [(0, 1), (1, 0)])  9.28 us
    ppermute x2, waiting for transfers between devices, across_z(): return lax.ppermute(array, ROWS, pairs)  6.02 us
  transfers between devices with their start and end apart: 37, of which 23 were waited for; matrix products, arithmetic and copies ran while one was open for 3% of the time, Pallas kernels for 4%

profile of v4, /device:TPU:1, one launch (start us, length us, event | category | flops | bytes accessed | tf_op | source)
XLA Modules:
  0.0 153.0 jit_solution(4407284875779418245)
XLA Ops:
  0.7 2.1 %collective-permute-start.4 = (bf16[192,1536]{1,0:T(8,128)(2,1)}, bf16[192,1536]{1,0:T(8,128)(2,1)S(1)}, u32[]{:S(2)}, u32[]{:S(2)}) collective-permute-start(bf16[192,1536]{1,0:T(8,128)(2,1)} %bitcast.54), channel_id=1, source_target_pairs={{0,8},{8,0},{1,9},{9,1},{2,10},{10,2},{3,11},{11,3},{4,12},{12,4},... | collective-permute-start | bytes 1769480 | tf_op jit(solution)/shard_map/ppermute | solution.py:71
  3.7 2.5 %collective-permute-start.8 = (bf16[2,48,768]{2,1,0:T(8,128)(2,1)S(1)}, bf16[2,48,768]{2,1,0:T(8,128)(2,1)S(1)}, u32[]{:S(2)}, u32[]{:S(2)}) collective-permute-start(bf16[2,48,768]{2,1,0:T(8,128)(2,1)S(1)} %pad_maximum_fusion.6.own_ref), channel_id=1, source_target_pairs={{0,128},{128,0},{1,129},{129,1},{2,130},{130,2},{3,131},{131,3},{4... | collective-permute-start | bytes 442376 | tf_op jit(solution)/shard_map/ppermute | solution.py:75
  6.3 15.1 %collective-permute-done.8.other_ref = bf16[2,48,768]{2,1,0:T(8,128)(2,1)S(1)} collective-permute-done((bf16[2,48,768]{2,1,0:T(8,128)(2,1)S(1)}, bf16[2,48,768]{2,1,0:T(8,128)(2,1)S(1)}, u32[]{:S(2)}, u32[]{:S(2)}) %collective-permute-start.8) | collective-permute-done | bytes 147488 | tf_op jit(solution)/shard_map/ppermute | solution.py:75
  21.4 5.7 %collective-permute-start.9 = (bf16[2,2,48,768]{3,2,1,0:T(8,128)(2,1)S(1)}, bf16[2,2,48,768]{3,2,1,0:T(8,128)(2,1)S(1)}, u32[]{:S(2)}, u32[]{:S(2)}) collective-permute-start(bf16[2,2,48,768]{3,2,1,0:T(8,128)(2,1)S(1)} %pair.1.refs_3_), channel_id=1, source_target_pairs={{0,112},{16,0},{32,16},{48,32},{64,48},{80,64},{96,80},{112,96},{1... | collective-permute-start | bytes 884744 | tf_op jit(solution)/shard_map/ppermute | solution.py:79
  27.0 1.8 %collective-permute-start.3 = (bf16[192,1536]{1,0:T(8,128)(2,1)}, bf16[192,1536]{1,0:T(8,128)(2,1)S(1)}, u32[]{:S(2)}, u32[]{:S(2)}) collective-permute-start(bf16[192,1536]{1,0:T(8,128)(2,1)} %bitcast.55), channel_id=1, source_target_pairs={{0,4},{4,0},{1,5},{5,1},{2,6},{6,2},{3,7},{7,3},{8,12},{12,8},{9,1... | collective-permute-start | bytes 1769480 | tf_op jit(solution)/shard_map/ppermute | solution.py:67
  28.9 2.9 %collective-permute-done.9.refs_4_ = bf16[2,2,48,768]{3,2,1,0:T(8,128)(2,1)S(1)} collective-permute-done((bf16[2,2,48,768]{3,2,1,0:T(8,128)(2,1)S(1)}, bf16[2,2,48,768]{3,2,1,0:T(8,128)(2,1)S(1)}, u32[]{:S(2)}, u32[]{:S(2)}) %collective-permute-start.9) | collective-permute-done | bytes 294944 | tf_op jit(solution)/shard_map/ppermute | solution.py:79
  31.9 3.4 %collective-permute-start.11 = (bf16[2,2,48,768]{3,2,1,0:T(8,128)(2,1)S(1)}, bf16[2,2,48,768]{3,2,1,0:T(8,128)(2,1)S(1)}, u32[]{:S(2)}, u32[]{:S(2)}) collective-permute-start(bf16[2,2,48,768]{3,2,1,0:T(8,128)(2,1)S(1)} %collective-permute-done.9.refs_4_), channel_id=1, source_target_pairs={{0,112},{16,0},{32,16},{48,32},{64,48},{80,64},{96,80},{112,96},{1... | collective-permute-start | bytes 884744 | tf_op jit(solution)/shard_map/ppermute | solution.py:79
  35.3 4.0 %collective-permute-done.11.refs_6_ = bf16[2,2,48,768]{3,2,1,0:T(8,128)(2,1)S(1)} collective-permute-done((bf16[2,2,48,768]{3,2,1,0:T(8,128)(2,1)S(1)}, bf16[2,2,48,768]{3,2,1,0:T(8,128)(2,1)S(1)}, u32[]{:S(2)}, u32[]{:S(2)}) %collective-permute-start.11) | collective-permute-done | bytes 294944 | tf_op jit(solution)/shard_map/ppermute | solution.py:79
  39.3 3.4 %collective-permute-start.13 = (bf16[2,2,48,768]{3,2,1,0:T(8,128)(2,1)S(1)}, bf16[2,2,48,768]{3,2,1,0:T(8,128)(2,1)S(1)}, u32[]{:S(2)}, u32[]{:S(2)}) collective-permute-start(bf16[2,2,48,768]{3,2,1,0:T(8,128)(2,1)S(1)} %collective-permute-done.11.refs_6_), channel_id=1, source_target_pairs={{0,112},{16,0},{32,16},{48,32},{64,48},{80,64},{96,80},{112,96},{1... | collective-permute-start | bytes 884744 | tf_op jit(solution)/shard_map/ppermute | solution.py:79
  42.7 1.0 copy-done.1
  44.8 3.6 %collective-permute-start = (bf16[96,384]{1,0:T(8,128)(2,1)S(1)}, bf16[96,384]{1,0:T(8,128)(2,1)S(1)}, u32[]{:S(2)}, u32[]{:S(2)}) collective-permute-start(bf16[96,384]{1,0:T(8,128)(2,1)S(1)} %get-tuple-element.26), channel_id=1, source_target_pairs={{0,12},{4,0},{8,4},{12,8},{16,28},{20,16},{24,20},{28,24},{32,44},... | collective-permute-start | bytes 221192 | tf_op jit(solution)/shard_map/ppermute | solution.py:63
  48.4 1.9 %collective-permute-done.x1 = bf16[96,384]{1,0:T(8,128)(2,1)S(1)} collective-permute-done((bf16[96,384]{1,0:T(8,128)(2,1)S(1)}, bf16[96,384]{1,0:T(8,128)(2,1)S(1)}, u32[]{:S(2)}, u32[]{:S(2)}) %collective-permute-start) | collective-permute-done | bytes 73760 | tf_op jit(solution)/shard_map/ppermute | solution.py:63
  50.3 1.2 collective-permute-start.1
  51.5 2.5 %collective-permute-done.1.x2 = bf16[96,384]{1,0:T(8,128)(2,1)S(1)} collective-permute-done((bf16[96,384]{1,0:T(8,128)(2,1)S(1)}, bf16[96,384]{1,0:T(8,128)(2,1)S(1)}, u32[]{:S(2)}, u32[]{:S(2)}) %collective-permute-start.1) | collective-permute-done | bytes 73760 | tf_op jit(solution)/shard_map/ppermute | solution.py:63
  54.0 4.4 %collective-permute-start.2 = (bf16[96,384]{1,0:T(8,128)(2,1)S(1)}, bf16[96,384]{1,0:T(8,128)(2,1)S(1)}, u32[]{:S(2)}, u32[]{:S(2)}) collective-permute-start(bf16[96,384]{1,0:T(8,128)(2,1)S(1)} %get-tuple-element.28), channel_id=1, source_target_pairs={{0,252},{4,240},{8,244},{12,248},{16,12},{20,0},{24,4},{28,8},{32,... | collective-permute-start | bytes 221192 | tf_op jit(solution)/shard_map/ppermute | solution.py:63
  58.4 1.8 %collective-permute-done.2.x3 = bf16[96,384]{1,0:T(8,128)(2,1)S(1)} collective-permute-done((bf16[96,384]{1,0:T(8,128)(2,1)S(1)}, bf16[96,384]{1,0:T(8,128)(2,1)S(1)}, u32[]{:S(2)}, u32[]{:S(2)}) %collective-permute-start.2) | collective-permute-done | bytes 73760 | tf_op jit(solution)/shard_map/ppermute | solution.py:63
  60.2 1.2 copy-done.3
  61.3 5.2 %window.1 = (bf16[64,1536]{1,0:T(8,128)(2,1)S(1)}, bf16[64,768]{1,0:T(8,128)(2,1)S(1)}) custom-call(f32[6]{0:T(128)S(1)} %copy-done.9, bf16[96,384]{1,0:T(8,128)(2,1)S(1)} %get-tuple-element.25.x0, bf16[96,384]{1,0:T(8,128)(2,1)S(1)} %collective-permute-done.x1, bf16[96,384]{1,0:T(8,128)(2,1)S(1)} %collective-permute-done.1.x2, ...), custom_call_target="tpu_custom_call" | custom-call | flops 402653184 | bytes 2000000 | tf_op jit(solution)/shard_map/window/pallas_call | solution.py:321
  66.9 1.1 level.1
  68.4 4.9 %collective-permute-start.15 = (bf16[2,48,768]{2,1,0:T(8,128)(2,1)S(1)}, bf16[2,48,768]{2,1,0:T(8,128)(2,1)S(1)}, u32[]{:S(2)}, u32[]{:S(2)}) collective-permute-start(bf16[2,48,768]{2,1,0:T(8,128)(2,1)S(1)} %slice_bitcast_fusion.1), channel_id=1, source_target_pairs={{0,112},{16,0},{32,16},{48,32},{64,48},{80,64},{96,80},{112,96},{1... | collective-permute-start | bytes 442376 | tf_op jit(solution)/shard_map/ppermute | solution.py:79
  73.4 1.5 %collective-permute-start.7 = (bf16[128,768]{1,0:T(8,128)(2,1)S(1)}, bf16[128,768]{1,0:T(8,128)(2,1)S(1)}, u32[]{:S(2)}, u32[]{:S(2)}) collective-permute-start(bf16[128,768]{1,0:T(8,128)(2,1)S(1)} %pad_maximum_fusion.1), channel_id=1, source_target_pairs={{0,4},{4,0},{1,5},{5,1},{2,6},{6,2},{3,7},{7,3},{8,12},{12,8},{9,1... | collective-permute-start | bytes 589832 | tf_op jit(solution)/shard_map/ppermute | solution.py:67
  74.9 3.3 %collective-permute-done.14.refs_9_ = bf16[2,2,48,768]{3,2,1,0:T(8,128)(2,1)S(1)} collective-permute-done((bf16[2,2,48,768]{3,2,1,0:T(8,128)(2,1)S(1)}, bf16[2,2,48,768]{3,2,1,0:T(8,128)(2,1)S(1)}, u32[]{:S(2)}, u32[]{:S(2)}) %collective-permute-start.14) | collective-permute-done | bytes 294944 | tf_op jit(solution)/shard_map/ppermute | solution.py:79
  78.3 5.2 %collective-permute-done.16.refs_11_ = bf16[2,48,768]{2,1,0:T(8,128)(2,1)S(1)} collective-permute-done((bf16[2,48,768]{2,1,0:T(8,128)(2,1)S(1)}, bf16[2,48,768]{2,1,0:T(8,128)(2,1)S(1)}, u32[]{:S(2)}, u32[]{:S(2)}) %collective-permute-start.16) | collective-permute-done | bytes 147488 | tf_op jit(solution)/shard_map/ppermute | solution.py:79
  83.5 1.1 forward.1
  84.6 3.0 %collective-permute-start.17 = (bf16[128,768]{1,0:T(8,128)(2,1)S(1)}, bf16[128,768]{1,0:T(8,128)(2,1)S(1)}, u32[]{:S(2)}, u32[]{:S(2)}) collective-permute-start(bf16[128,768]{1,0:T(8,128)(2,1)S(1)} %get-tuple-element.33), channel_id=1, source_target_pairs={{0,4},{4,0},{1,5},{5,1},{2,6},{6,2},{3,7},{7,3},{8,12},{12,8},{9,1... | collective-permute-start | bytes 589832 | tf_op jit(solution)/shard_map/ppermute | solution.py:67
  87.6 1.1 collective-permute-done.17
  88.8 4.0 %collective-permute-done.18 = bf16[64,768]{1,0:T(8,128)(2,1)S(1)} collective-permute-done((bf16[64,768]{1,0:T(8,128)(2,1)S(1)}, bf16[64,768]{1,0:T(8,128)(2,1)S(1)}, u32[]{:S(2)}, u32[]{:S(2)}) %collective-permute-start.18) | collective-permute-done | bytes 98336 | tf_op jit(solution)/shard_map/ppermute | solution.py:71
  93.6 3.5 %collective-permute-done.19.refs_1_ = bf16[64,768]{1,0:T(8,128)(2,1)S(1)} collective-permute-done((bf16[64,768]{1,0:T(8,128)(2,1)S(1)}, bf16[64,768]{1,0:T(8,128)(2,1)S(1)}, u32[]{:S(2)}, u32[]{:S(2)}) %collective-permute-start.19) | collective-permute-done | bytes 98336 | tf_op jit(solution)/shard_map/ppermute | solution.py:71
  97.8 2.4 %collective-permute-start.20 = (bf16[128,768]{1,0:T(8,128)(2,1)}, bf16[128,768]{1,0:T(8,128)(2,1)}, u32[]{:S(2)}, u32[]{:S(2)}) collective-permute-start(bf16[128,768]{1,0:T(8,128)(2,1)} %pad_maximum_fusion.2), channel_id=1, source_target_pairs={{0,4},{4,0},{1,5},{5,1},{2,6},{6,2},{3,7},{7,3},{8,12},{12,8},{9,1... | collective-permute-start | bytes 589832 | tf_op jit(solution)/shard_map/ppermute | solution.py:67
  100.1 1.4 collective-permute-done.20.refs_2_
  101.6 1.0 copy-done.5
  102.6 1.0 copy-done.7
  103.6 2.5 %backward.1 = (bf16[768,768]{1,0:T(8,128)(2,1)S(1)}, bf16[768,768]{1,0:T(8,128)(2,1)S(1)}, bf16[128,768]{1,0:T(8,128)(2,1)S(1)}, bf16[128,768]{1,0:T(8,128)(2,1)S(1)}) custom-call(bf16[64,768]{1,0:T(8,128)(2,1)S(1)} %get-tuple-element.65.refs_0_, bf16[64,768]{1,0:T(8,128)(2,1)S(1)} %collective-permute-done.19.refs_1_, ...), custom_call_target="tpu_custom_call" | custom-call | flops 1207959552 | bytes 6000000 | tf_op jit(solution)/shard_map/backward/pallas_call | solution.py:382
  108.1 1.4 collective-permute-start.31
  109.5 2.5 %collective-permute-done.27 = bf16[2,48,768]{2,1,0:T(8,128)(2,1)S(1)} collective-permute-done((bf16[2,48,768]{2,1,0:T(8,128)(2,1)S(1)}, bf16[2,48,768]{2,1,0:T(8,128)(2,1)S(1)}, u32[]{:S(2)}, u32[]{:S(2)}) %collective-permute-start.27) | collective-permute-done | bytes 147488 | tf_op jit(solution)/shard_map/ppermute | solution.py:79
  112.1 1.5 collective-permute-start.28
  114.2 1.2 collective-permute-start.22
  116.2 2.0 %collective-permute-done.22 = bf16[64,768]{1,0:T(8,128)(2,1)S(1)} collective-permute-done((bf16[64,768]{1,0:T(8,128)(2,1)S(1)}, bf16[64,768]{1,0:T(8,128)(2,1)S(1)}, u32[]{:S(2)}, u32[]{:S(2)}) %collective-permute-start.22) | collective-permute-done | bytes 98336 | tf_op jit(solution)/shard_map/ppermute | solution.py:71
  118.3 3.2 %collective-permute-start.25 = (bf16[16,1536]{1,0:T(8,128)(2,1)S(1)}, bf16[16,1536]{1,0:T(8,128)(2,1)S(1)}, u32[]{:S(2)}, u32[]{:S(2)}) collective-permute-start(bf16[16,1536]{1,0:T(8,128)(2,1)S(1)} %get-tuple-element.79), channel_id=1, source_target_pairs={{0,4},{4,8},{8,12},{12,0},{16,20},{20,24},{24,28},{28,16},{32,36},... | collective-permute-start | bytes 147464 | tf_op jit(solution)/shard_map/ppermute | solution.py:63
  122.7 3.7 %collective-permute-start.29 = (bf16[2,2,48,768]{3,2,1,0:T(8,128)(2,1)S(1)}, bf16[2,2,48,768]{3,2,1,0:T(8,128)(2,1)S(1)}, u32[]{:S(2)}, u32[]{:S(2)}) collective-permute-start(bf16[2,2,48,768]{3,2,1,0:T(8,128)(2,1)S(1)} %maximum_add_fusion), channel_id=1, source_target_pairs={{0,112},{16,0},{32,16},{48,32},{64,48},{80,64},{96,80},{112,96},{1... | collective-permute-start | bytes 884744 | tf_op jit(solution)/shard_map/ppermute | solution.py:79
  126.4 2.2 %collective-permute-done.24 = bf16[16,1536]{1,0:T(8,128)(2,1)S(1)} collective-permute-done((bf16[16,1536]{1,0:T(8,128)(2,1)S(1)}, bf16[16,1536]{1,0:T(8,128)(2,1)S(1)}, u32[]{:S(2)}, u32[]{:S(2)}) %collective-permute-start.24) | collective-permute-done | bytes 49184 | tf_op jit(solution)/shard_map/ppermute | solution.py:63
  128.6 1.8 %collective-permute-done.23 = bf16[16,1536]{1,0:T(8,128)(2,1)S(1)} collective-permute-done((bf16[16,1536]{1,0:T(8,128)(2,1)S(1)}, bf16[16,1536]{1,0:T(8,128)(2,1)S(1)}, u32[]{:S(2)}, u32[]{:S(2)}) %collective-permute-start.23) | collective-permute-done | bytes 49184 | tf_op jit(solution)/shard_map/ppermute | solution.py:63
  130.9 1.5 collective-permute-done.29
  132.4 3.5 %collective-permute-start.30 = (bf16[2,48,768]{2,1,0:T(8,128)(2,1)S(1)}, bf16[2,48,768]{2,1,0:T(8,128)(2,1)S(1)}, u32[]{:S(2)}, u32[]{:S(2)}) collective-permute-start(bf16[2,48,768]{2,1,0:T(8,128)(2,1)S(1)} %get-tuple-element.71), channel_id=1, source_target_pairs={{0,112},{16,0},{32,16},{48,32},{64,48},{80,64},{96,80},{112,96},{1... | collective-permute-start | bytes 442376 | tf_op jit(solution)/shard_map/ppermute | solution.py:79
  135.9 4.6 %collective-permute-done.33 = bf16[2,2,48,768]{3,2,1,0:T(8,128)(2,1)S(1)} collective-permute-done((bf16[2,2,48,768]{3,2,1,0:T(8,128)(2,1)S(1)}, bf16[2,2,48,768]{3,2,1,0:T(8,128)(2,1)S(1)}, u32[]{:S(2)}, u32[]{:S(2)}) %collective-permute-start.33) | collective-permute-done | bytes 294944 | tf_op jit(solution)/shard_map/ppermute | solution.py:79
  140.6 4.0 %collective-permute-start.35 = (bf16[2,48,768]{2,1,0:T(8,128)(2,1)S(1)}, bf16[2,48,768]{2,1,0:T(8,128)(2,1)S(1)}, u32[]{:S(2)}, u32[]{:S(2)}) collective-permute-start(bf16[2,48,768]{2,1,0:T(8,128)(2,1)S(1)} %get-tuple-element.70), channel_id=1, source_target_pairs={{0,240},{16,128},{32,144},{48,160},{64,176},{80,192},{96,208},{112... | collective-permute-start | bytes 442376 | tf_op jit(solution)/shard_map/ppermute | solution.py:87
  146.2 1.3 collective-permute-done.35.refs_4_
  147.5 4.7 %collective-permute-done.36.refs_5_ = bf16[2,48,768]{2,1,0:T(8,128)(2,1)S(1)} collective-permute-done((bf16[2,48,768]{2,1,0:T(8,128)(2,1)S(1)}, bf16[2,48,768]{2,1,0:T(8,128)(2,1)S(1)}, u32[]{:S(2)}, u32[]{:S(2)}) %collective-permute-start.36) | collective-permute-done | bytes 147488 | tf_op jit(solution)/shard_map/ppermute | solution.py:87
  (91 shorter events, 12.4 us)
Async XLA Ops:
  0.6 59.5 %copy-start.9 = (f32[6]{0:T(128)S(1)}, f32[6]{0:T(128)}, u32[]{:S(2)}) copy-start(f32[6]{0:T(128)} %scale_ref.1) | copy-start | bytes 76
  0.6 59.5 %copy-start.8 = (bf16[384,384]{1,0:T(8,128)(2,1)S(1)}, bf16[384,384]{1,0:T(8,128)(2,1)}, u32[]{:S(2)}) copy-start(bf16[384,384]{1,0:T(8,128)(2,1)} %proj_ref.1) | copy-start | bytes 884740
  0.7 28.2 %collective-permute-start.4 = (bf16[192,1536]{1,0:T(8,128)(2,1)}, bf16[192,1536]{1,0:T(8,128)(2,1)S(1)}, u32[]{:S(2)}, u32[]{:S(2)}) collective-permute-start(bf16[192,1536]{1,0:T(8,128)(2,1)} %bitcast.54), channel_id=1, source_target_pairs={{0,8},{8,0},{1,9},{9,1},{2,10},{10,2},{3,11},{11,3},{4,12},{12,4},... | collective-permute-start | bytes 1769480 | tf_op jit(solution)/shard_map/ppermute | solution.py:71
  3.7 63.2 %copy-start = (bf16[1536,192]{0,1:T(8,128)(2,1)S(1)}, bf16[1536,192]{0,1:T(8,128)(2,1)}, u32[]{:S(2)}) copy-start(bf16[1536,192]{0,1:T(8,128)(2,1)} %param.12) | copy-start | bytes 1769476
  3.7 17.6 %collective-permute-start.8 = (bf16[2,48,768]{2,1,0:T(8,128)(2,1)S(1)}, bf16[2,48,768]{2,1,0:T(8,128)(2,1)S(1)}, u32[]{:S(2)}, u32[]{:S(2)}) collective-permute-start(bf16[2,48,768]{2,1,0:T(8,128)(2,1)S(1)} %pad_maximum_fusion.6.own_ref), channel_id=1, source_target_pairs={{0,128},{128,0},{1,129},{129,1},{2,130},{130,2},{3,131},{131,3},{4... | collective-permute-start | bytes 442376 | tf_op jit(solution)/shard_map/ppermute | solution.py:75
  21.4 10.5 %collective-permute-start.9 = (bf16[2,2,48,768]{3,2,1,0:T(8,128)(2,1)S(1)}, bf16[2,2,48,768]{3,2,1,0:T(8,128)(2,1)S(1)}, u32[]{:S(2)}, u32[]{:S(2)}) collective-permute-start(bf16[2,2,48,768]{3,2,1,0:T(8,128)(2,1)S(1)} %pair.1.refs_3_), channel_id=1, source_target_pairs={{0,112},{16,0},{32,16},{48,32},{64,48},{80,64},{96,80},{112,96},{1... | collective-permute-start | bytes 884744 | tf_op jit(solution)/shard_map/ppermute | solution.py:79
  27.0 8.3 %collective-permute-start.10 = (bf16[2,2,48,768]{3,2,1,0:T(8,128)(2,1)S(1)}, bf16[2,2,48,768]{3,2,1,0:T(8,128)(2,1)S(1)}, u32[]{:S(2)}, u32[]{:S(2)}) collective-permute-start(bf16[2,2,48,768]{3,2,1,0:T(8,128)(2,1)S(1)} %pair.1.refs_3_), channel_id=1, source_target_pairs={{0,16},{16,32},{32,48},{48,64},{64,80},{80,96},{96,112},{112,0},{1... | collective-permute-start | bytes 884744 | tf_op jit(solution)/shard_map/ppermute | solution.py:79
  27.0 39.8 %collective-permute-start.3 = (bf16[192,1536]{1,0:T(8,128)(2,1)}, bf16[192,1536]{1,0:T(8,128)(2,1)S(1)}, u32[]{:S(2)}, u32[]{:S(2)}) collective-permute-start(bf16[192,1536]{1,0:T(8,128)(2,1)} %bitcast.55), channel_id=1, source_target_pairs={{0,4},{4,0},{1,5},{5,1},{2,6},{6,2},{3,7},{7,3},{8,12},{12,8},{9,1... | collective-permute-start | bytes 1769480 | tf_op jit(solution)/shard_map/ppermute | solution.py:67
  28.8 38.0 %collective-permute-start.5 = (bf16[192,1536]{1,0:T(8,128)(2,1)S(1)}, bf16[192,1536]{1,0:T(8,128)(2,1)S(1)}, u32[]{:S(2)}, u32[]{:S(2)}) collective-permute-start(bf16[192,1536]{1,0:T(8,128)(2,1)S(1)} %collective-permute-done.4.near_ref), channel_id=1, source_target_pairs={{0,4},{4,0},{1,5},{5,1},{2,6},{6,2},{3,7},{7,3},{8,12},{12,8},{9,1... | collective-permute-start | bytes 1769480 | tf_op jit(solution)/shard_map/ppermute | solution.py:67
  31.9 7.4 %collective-permute-start.11 = (bf16[2,2,48,768]{3,2,1,0:T(8,128)(2,1)S(1)}, bf16[2,2,48,768]{3,2,1,0:T(8,128)(2,1)S(1)}, u32[]{:S(2)}, u32[]{:S(2)}) collective-permute-start(bf16[2,2,48,768]{3,2,1,0:T(8,128)(2,1)S(1)} %collective-permute-done.9.refs_4_), channel_id=1, source_target_pairs={{0,112},{16,0},{32,16},{48,32},{64,48},{80,64},{96,80},{112,96},{1... | collective-permute-start | bytes 884744 | tf_op jit(solution)/shard_map/ppermute | solution.py:79
  35.3 31.3 %collective-permute-start.12 = (bf16[2,2,48,768]{3,2,1,0:T(8,128)(2,1)S(1)}, bf16[2,2,48,768]{3,2,1,0:T(8,128)(2,1)S(1)}, u32[]{:S(2)}, u32[]{:S(2)}) collective-permute-start(bf16[2,2,48,768]{3,2,1,0:T(8,128)(2,1)S(1)} %collective-permute-done.10.refs_5_), channel_id=1, source_target_pairs={{0,16},{16,32},{32,48},{48,64},{64,80},{80,96},{96,112},{112,0},{1... | collective-permute-start | bytes 884744 | tf_op jit(solution)/shard_map/ppermute | solution.py:79
  39.3 29.2 %collective-permute-start.13 = (bf16[2,2,48,768]{3,2,1,0:T(8,128)(2,1)S(1)}, bf16[2,2,48,768]{3,2,1,0:T(8,128)(2,1)S(1)}, u32[]{:S(2)}, u32[]{:S(2)}) collective-permute-start(bf16[2,2,48,768]{3,2,1,0:T(8,128)(2,1)S(1)} %collective-permute-done.11.refs_6_), channel_id=1, source_target_pairs={{0,112},{16,0},{32,16},{48,32},{64,48},{80,64},{96,80},{112,96},{1... | collective-permute-start | bytes 884744 | tf_op jit(solution)/shard_map/ppermute | solution.py:79
  42.7 1.0 copy-start.1
  43.7 0.9 copy-start.2
  44.8 5.5 %collective-permute-start = (bf16[96,384]{1,0:T(8,128)(2,1)S(1)}, bf16[96,384]{1,0:T(8,128)(2,1)S(1)}, u32[]{:S(2)}, u32[]{:S(2)}) collective-permute-start(bf16[96,384]{1,0:T(8,128)(2,1)S(1)} %get-tuple-element.26), channel_id=1, source_target_pairs={{0,12},{4,0},{8,4},{12,8},{16,28},{20,16},{24,20},{28,24},{32,44},... | collective-permute-start | bytes 221192 | tf_op jit(solution)/shard_map/ppermute | solution.py:63
  50.3 3.7 %collective-permute-start.1 = (bf16[96,384]{1,0:T(8,128)(2,1)S(1)}, bf16[96,384]{1,0:T(8,128)(2,1)S(1)}, u32[]{:S(2)}, u32[]{:S(2)}) collective-permute-start(bf16[96,384]{1,0:T(8,128)(2,1)S(1)} %get-tuple-element.27), channel_id=1, source_target_pairs={{0,240},{4,244},{8,248},{12,252},{16,0},{20,4},{24,8},{28,12},{32,... | collective-permute-start | bytes 221192 | tf_op jit(solution)/shard_map/ppermute | solution.py:63
  54.0 6.2 %collective-permute-start.2 = (bf16[96,384]{1,0:T(8,128)(2,1)S(1)}, bf16[96,384]{1,0:T(8,128)(2,1)S(1)}, u32[]{:S(2)}, u32[]{:S(2)}) collective-permute-start(bf16[96,384]{1,0:T(8,128)(2,1)S(1)} %get-tuple-element.28), channel_id=1, source_target_pairs={{0,252},{4,240},{8,244},{12,248},{16,12},{20,0},{24,4},{28,8},{32,... | collective-permute-start | bytes 221192 | tf_op jit(solution)/shard_map/ppermute | solution.py:63
  60.2 1.2 copy-start.3
  66.6 11.6 %collective-permute-start.14 = (bf16[2,2,48,768]{3,2,1,0:T(8,128)(2,1)S(1)}, bf16[2,2,48,768]{3,2,1,0:T(8,128)(2,1)S(1)}, u32[]{:S(2)}, u32[]{:S(2)}) collective-permute-start(bf16[2,2,48,768]{3,2,1,0:T(8,128)(2,1)S(1)} %collective-permute-done.12.refs_7_), channel_id=1, source_target_pairs={{0,16},{16,32},{32,48},{48,64},{64,80},{80,96},{96,112},{112,0},{1... | collective-permute-start | bytes 884744 | tf_op jit(solution)/shard_map/ppermute | solution.py:79
  68.0 5.4 %collective-permute-start.6 = (bf16[64,768]{1,0:T(8,128)(2,1)S(1)}, bf16[64,768]{1,0:T(8,128)(2,1)S(1)}, u32[]{:S(2)}, u32[]{:S(2)}) collective-permute-start(bf16[64,768]{1,0:T(8,128)(2,1)S(1)} %get-tuple-element.31.refs_0_), channel_id=1, source_target_pairs={{0,8},{8,0},{1,9},{9,1},{2,10},{10,2},{3,11},{11,3},{4,12},{12,4},... | collective-permute-start | bytes 294920 | tf_op jit(solution)/shard_map/ppermute | solution.py:71
  68.4 9.9 %collective-permute-start.15 = (bf16[2,48,768]{2,1,0:T(8,128)(2,1)S(1)}, bf16[2,48,768]{2,1,0:T(8,128)(2,1)S(1)}, u32[]{:S(2)}, u32[]{:S(2)}) collective-permute-start(bf16[2,48,768]{2,1,0:T(8,128)(2,1)S(1)} %slice_bitcast_fusion.1), channel_id=1, source_target_pairs={{0,112},{16,0},{32,16},{48,32},{64,48},{80,64},{96,80},{112,96},{1... | collective-permute-start | bytes 442376 | tf_op jit(solution)/shard_map/ppermute | solution.py:79
  73.4 10.1 %collective-permute-start.7 = (bf16[128,768]{1,0:T(8,128)(2,1)S(1)}, bf16[128,768]{1,0:T(8,128)(2,1)S(1)}, u32[]{:S(2)}, u32[]{:S(2)}) collective-permute-start(bf16[128,768]{1,0:T(8,128)(2,1)S(1)} %pad_maximum_fusion.1), channel_id=1, source_target_pairs={{0,4},{4,0},{1,5},{5,1},{2,6},{6,2},{3,7},{7,3},{8,12},{12,8},{9,1... | collective-permute-start | bytes 589832 | tf_op jit(solution)/shard_map/ppermute | solution.py:67
  78.2 5.3 %collective-permute-start.16 = (bf16[2,48,768]{2,1,0:T(8,128)(2,1)S(1)}, bf16[2,48,768]{2,1,0:T(8,128)(2,1)S(1)}, u32[]{:S(2)}, u32[]{:S(2)}) collective-permute-start(bf16[2,48,768]{2,1,0:T(8,128)(2,1)S(1)} %slice_bitcast_fusion), channel_id=1, source_target_pairs={{0,16},{16,32},{32,48},{48,64},{64,80},{80,96},{96,112},{112,0},{1... | collective-permute-start | bytes 442376 | tf_op jit(solution)/shard_map/ppermute | solution.py:79
  84.6 8.9 %copy-start.4 = (bf16[256,768]{1,0:T(8,128)(2,1)}, bf16[256,768]{1,0:T(8,128)(2,1)S(1)}, u32[]{:S(2)}) copy-start(bf16[256,768]{1,0:T(8,128)(2,1)S(1)} %get-tuple-element.35.refs_3_) | copy-start | bytes 1179652
  84.6 8.9 %copy-start.6 = (bf16[256,768]{1,0:T(8,128)(2,1)}, bf16[256,768]{1,0:T(8,128)(2,1)S(1)}, u32[]{:S(2)}) copy-start(bf16[256,768]{1,0:T(8,128)(2,1)S(1)} %get-tuple-element.38.refs_6_) | copy-start | bytes 1179652
  84.6 4.1 %collective-permute-start.17 = (bf16[128,768]{1,0:T(8,128)(2,1)S(1)}, bf16[128,768]{1,0:T(8,128)(2,1)S(1)}, u32[]{:S(2)}, u32[]{:S(2)}) collective-permute-start(bf16[128,768]{1,0:T(8,128)(2,1)S(1)} %get-tuple-element.33), channel_id=1, source_target_pairs={{0,4},{4,0},{1,5},{5,1},{2,6},{6,2},{3,7},{7,3},{8,12},{12,8},{9,1... | collective-permute-start | bytes 589832 | tf_op jit(solution)/shard_map/ppermute | solution.py:67
  88.7 4.1 %collective-permute-start.18 = (bf16[64,768]{1,0:T(8,128)(2,1)S(1)}, bf16[64,768]{1,0:T(8,128)(2,1)S(1)}, u32[]{:S(2)}, u32[]{:S(2)}) collective-permute-start(bf16[64,768]{1,0:T(8,128)(2,1)S(1)} %slice.215), channel_id=1, source_target_pairs={{0,8},{8,0},{1,9},{9,1},{2,10},{10,2},{3,11},{11,3},{4,12},{12,4},... | collective-permute-start | bytes 294920 | tf_op jit(solution)/shard_map/ppermute | solution.py:71
  93.5 3.6 %collective-permute-start.19 = (bf16[64,768]{1,0:T(8,128)(2,1)S(1)}, bf16[64,768]{1,0:T(8,128)(2,1)S(1)}, u32[]{:S(2)}, u32[]{:S(2)}) collective-permute-start(bf16[64,768]{1,0:T(8,128)(2,1)S(1)} %get-tuple-element.65.refs_0_), channel_id=1, source_target_pairs={{0,8},{8,0},{1,9},{9,1},{2,10},{10,2},{3,11},{11,3},{4,12},{12,4},... | collective-permute-start | bytes 294920 | tf_op jit(solution)/shard_map/ppermute | solution.py:71
  97.8 3.8 %collective-permute-start.20 = (bf16[128,768]{1,0:T(8,128)(2,1)}, bf16[128,768]{1,0:T(8,128)(2,1)}, u32[]{:S(2)}, u32[]{:S(2)}) collective-permute-start(bf16[128,768]{1,0:T(8,128)(2,1)} %pad_maximum_fusion.2), channel_id=1, source_target_pairs={{0,4},{4,0},{1,5},{5,1},{2,6},{6,2},{3,7},{7,3},{8,12},{12,8},{9,1... | collective-permute-start | bytes 589832 | tf_op jit(solution)/shard_map/ppermute | solution.py:67
  101.6 1.0 copy-start.5
  102.6 1.0 copy-start.7
  106.0 8.1 %collective-permute-start.21 = (bf16[128,768]{1,0:T(8,128)(2,1)S(1)}, bf16[128,768]{1,0:T(8,128)(2,1)S(1)}, u32[]{:S(2)}, u32[]{:S(2)}) collective-permute-start(bf16[128,768]{1,0:T(8,128)(2,1)S(1)} %get-tuple-element.41), channel_id=1, source_target_pairs={{0,4},{4,0},{1,5},{5,1},{2,6},{6,2},{3,7},{7,3},{8,12},{12,8},{9,1... | collective-permute-start | bytes 589832 | tf_op jit(solution)/shard_map/ppermute | solution.py:67
  106.7 5.3 %collective-permute-start.27 = (bf16[2,48,768]{2,1,0:T(8,128)(2,1)S(1)}, bf16[2,48,768]{2,1,0:T(8,128)(2,1)S(1)}, u32[]{:S(2)}, u32[]{:S(2)}) collective-permute-start(bf16[2,48,768]{2,1,0:T(8,128)(2,1)S(1)} %get-tuple-element.73), channel_id=1, source_target_pairs={{0,112},{16,0},{32,16},{48,32},{64,48},{80,64},{96,80},{112,96},{1... | collective-permute-start | bytes 442376 | tf_op jit(solution)/shard_map/ppermute | solution.py:79
  107.7 37.7 %collective-permute-start.26 = (bf16[2,48,768]{2,1,0:T(8,128)(2,1)}, bf16[2,48,768]{2,1,0:T(8,128)(2,1)S(1)}, u32[]{:S(2)}, u32[]{:S(2)}) collective-permute-start(bf16[2,48,768]{2,1,0:T(8,128)(2,1)} %get-tuple-element.74), channel_id=1, source_target_pairs={{0,128},{128,0},{1,129},{129,1},{2,130},{130,2},{3,131},{131,3},{4... | collective-permute-start | bytes 442376 | tf_op jit(solution)/shard_map/ppermute | solution.py:75
  108.1 5.9 %collective-permute-start.31 = (bf16[2,48,768]{2,1,0:T(8,128)(2,1)S(1)}, bf16[2,48,768]{2,1,0:T(8,128)(2,1)S(1)}, u32[]{:S(2)}, u32[]{:S(2)}) collective-permute-start(bf16[2,48,768]{2,1,0:T(8,128)(2,1)S(1)} %get-tuple-element.72), channel_id=1, source_target_pairs={{0,16},{16,32},{32,48},{48,64},{64,80},{80,96},{96,112},{112,0},{1... | collective-permute-start | bytes 442376 | tf_op jit(solution)/shard_map/ppermute | solution.py:79
  112.1 9.6 %collective-permute-start.28 = (bf16[2,2,48,768]{3,2,1,0:T(8,128)(2,1)S(1)}, bf16[2,2,48,768]{3,2,1,0:T(8,128)(2,1)S(1)}, u32[]{:S(2)}, u32[]{:S(2)}) collective-permute-start(bf16[2,2,48,768]{3,2,1,0:T(8,128)(2,1)S(1)} %fusion.3), channel_id=1, source_target_pairs={{0,112},{16,0},{32,16},{48,32},{64,48},{80,64},{96,80},{112,96},{1... | collective-permute-start | bytes 884744 | tf_op jit(solution)/shard_map/ppermute | solution.py:79
  114.2 4.1 %collective-permute-start.22 = (bf16[64,768]{1,0:T(8,128)(2,1)S(1)}, bf16[64,768]{1,0:T(8,128)(2,1)S(1)}, u32[]{:S(2)}, u32[]{:S(2)}) collective-permute-start(bf16[64,768]{1,0:T(8,128)(2,1)S(1)} %slice.214), channel_id=1, source_target_pairs={{0,8},{8,0},{1,9},{9,1},{2,10},{10,2},{3,11},{11,3},{4,12},{12,4},... | collective-permute-start | bytes 294920 | tf_op jit(solution)/shard_map/ppermute | solution.py:71
  116.1 14.7 %collective-permute-start.32 = (bf16[2,2,48,768]{3,2,1,0:T(8,128)(2,1)}, bf16[2,2,48,768]{3,2,1,0:T(8,128)(2,1)S(1)}, u32[]{:S(2)}, u32[]{:S(2)}) collective-permute-start(bf16[2,2,48,768]{3,2,1,0:T(8,128)(2,1)} %pad_maximum_fusion), channel_id=1, source_target_pairs={{0,16},{16,32},{32,48},{48,64},{64,80},{80,96},{96,112},{112,0},{1... | collective-permute-start | bytes 884744 | tf_op jit(solution)/shard_map/ppermute | solution.py:79
  118.3 4.4 %collective-permute-start.25 = (bf16[16,1536]{1,0:T(8,128)(2,1)S(1)}, bf16[16,1536]{1,0:T(8,128)(2,1)S(1)}, u32[]{:S(2)}, u32[]{:S(2)}) collective-permute-start(bf16[16,1536]{1,0:T(8,128)(2,1)S(1)} %get-tuple-element.79), channel_id=1, source_target_pairs={{0,4},{4,8},{8,12},{12,0},{16,20},{20,24},{24,28},{28,16},{32,36},... | collective-permute-start | bytes 147464 | tf_op jit(solution)/shard_map/ppermute | solution.py:63
  121.5 7.1 %collective-permute-start.24 = (bf16[16,1536]{1,0:T(8,128)(2,1)S(1)}, bf16[16,1536]{1,0:T(8,128)(2,1)S(1)}, u32[]{:S(2)}, u32[]{:S(2)}) collective-permute-start(bf16[16,1536]{1,0:T(8,128)(2,1)S(1)} %get-tuple-element.77), channel_id=1, source_target_pairs={{0,16},{4,20},{8,24},{12,28},{16,32},{20,36},{24,40},{28,44},{32,4... | collective-permute-start | bytes 147464 | tf_op jit(solution)/shard_map/ppermute | solution.py:63
  121.7 8.7 %collective-permute-start.23 = (bf16[16,1536]{1,0:T(8,128)(2,1)S(1)}, bf16[16,1536]{1,0:T(8,128)(2,1)S(1)}, u32[]{:S(2)}, u32[]{:S(2)}) collective-permute-start(bf16[16,1536]{1,0:T(8,128)(2,1)S(1)} %get-tuple-element.76), channel_id=1, source_target_pairs={{0,20},{4,24},{8,28},{12,16},{16,36},{20,40},{24,44},{28,32},{32,5... | collective-permute-start | bytes 147464 | tf_op jit(solution)/shard_map/ppermute | solution.py:63
  122.7 9.6 %collective-permute-start.29 = (bf16[2,2,48,768]{3,2,1,0:T(8,128)(2,1)S(1)}, bf16[2,2,48,768]{3,2,1,0:T(8,128)(2,1)S(1)}, u32[]{:S(2)}, u32[]{:S(2)}) collective-permute-start(bf16[2,2,48,768]{3,2,1,0:T(8,128)(2,1)S(1)} %maximum_add_fusion), channel_id=1, source_target_pairs={{0,112},{16,0},{32,16},{48,32},{64,48},{80,64},{96,80},{112,96},{1... | collective-permute-start | bytes 884744 | tf_op jit(solution)/shard_map/ppermute | solution.py:79
  130.8 9.7 %collective-permute-start.33 = (bf16[2,2,48,768]{3,2,1,0:T(8,128)(2,1)S(1)}, bf16[2,2,48,768]{3,2,1,0:T(8,128)(2,1)S(1)}, u32[]{:S(2)}, u32[]{:S(2)}) collective-permute-start(bf16[2,2,48,768]{3,2,1,0:T(8,128)(2,1)S(1)} %maximum_add_fusion.2), channel_id=1, source_target_pairs={{0,16},{16,32},{32,48},{48,64},{64,80},{80,96},{96,112},{112,0},{1... | collective-permute-start | bytes 884744 | tf_op jit(solution)/shard_map/ppermute | solution.py:79
  132.4 13.0 %collective-permute-start.30 = (bf16[2,48,768]{2,1,0:T(8,128)(2,1)S(1)}, bf16[2,48,768]{2,1,0:T(8,128)(2,1)S(1)}, u32[]{:S(2)}, u32[]{:S(2)}) collective-permute-start(bf16[2,48,768]{2,1,0:T(8,128)(2,1)S(1)} %get-tuple-element.71), channel_id=1, source_target_pairs={{0,112},{16,0},{32,16},{48,32},{64,48},{80,64},{96,80},{112,96},{1... | collective-permute-start | bytes 442376 | tf_op jit(solution)/shard_map/ppermute | solution.py:79
  140.5 5.7 %collective-permute-start.34 = (bf16[2,48,768]{2,1,0:T(8,128)(2,1)S(1)}, bf16[2,48,768]{2,1,0:T(8,128)(2,1)S(1)}, u32[]{:S(2)}, u32[]{:S(2)}) collective-permute-start(bf16[2,48,768]{2,1,0:T(8,128)(2,1)S(1)} %get-tuple-element.69), channel_id=1, source_target_pairs={{0,16},{16,32},{32,48},{48,64},{64,80},{80,96},{96,112},{112,0},{1... | collective-permute-start | bytes 442376 | tf_op jit(solution)/shard_map/ppermute | solution.py:79
  140.6 6.9 %collective-permute-start.35 = (bf16[2,48,768]{2,1,0:T(8,128)(2,1)S(1)}, bf16[2,48,768]{2,1,0:T(8,128)(2,1)S(1)}, u32[]{:S(2)}, u32[]{:S(2)}) collective-permute-start(bf16[2,48,768]{2,1,0:T(8,128)(2,1)S(1)} %get-tuple-element.70), channel_id=1, source_target_pairs={{0,240},{16,128},{32,144},{48,160},{64,176},{80,192},{96,208},{112... | collective-permute-start | bytes 442376 | tf_op jit(solution)/shard_map/ppermute | solution.py:87
  144.6 7.6 %collective-permute-start.36 = (bf16[2,48,768]{2,1,0:T(8,128)(2,1)S(1)}, bf16[2,48,768]{2,1,0:T(8,128)(2,1)S(1)}, u32[]{:S(2)}, u32[]{:S(2)}) collective-permute-start(bf16[2,48,768]{2,1,0:T(8,128)(2,1)S(1)} %get-tuple-element.68), channel_id=1, source_target_pairs={{0,144},{16,160},{32,176},{48,192},{64,208},{80,224},{96,240},{112... | collective-permute-start | bytes 442376 | tf_op jit(solution)/shard_map/ppermute | solution.py:87

commit v5 on v4

--- a/solution.py
+++ b/solution.py
@@ -90,7 +90,8 @@
 def scatter_cols(low, high):
     quarter = low.shape[0] // 2
     near = low.astype(F32) + swap_core(high).astype(F32)
-    return near[:quarter] + swap_xl(near[quarter:].astype(BF)).astype(F32)
+    far = swap_xl(near[quarter:].astype(BF))
+    return near[:quarter] + far.astype(F32)
 
 
 def gather_rows(shard):
@@ -113,15 +114,13 @@
 
 
 def scatter_rows(terms):
-    blocks = [term.reshape(NX, NZ, -1, term.shape[-1]) for term in terms]
-    z = lax.axis_index("z")
+    apart = lax.optimization_barrier(terms)
 
     def block(k):
-        return jnp.stack([lax.dynamic_index_in_dim(b, (z + k) % NZ, 1, False) for b in blocks], 1)
-
-    own = block(0)
-    own_other = swap_half(jnp.where(lax.axis_index("xh") == 0, own[1], own[0]))
-    far = block(4)
+        return (terms if k < 5 else apart)[k]
+
+    own, far = block(0), block(4)
+    own_other = swap_half(own[1])
     left, right = along_z(far[0], -1), along_z(far[1], 1)
     near_left, near_right = block(NZ - 3), block(3)
     left = jnp.stack([near_left[0] + left, near_left[1]])
@@ -129,16 +128,8 @@
     for k in (2, 1):
         left, right = along_z(left, -1), along_z(right, 1)
         left, right = left + block(NZ - k), right + block(k)
-    first = lax.axis_index("xh") == 0
-
-    def mine(v):
-        return jnp.where(first, v[0], v[1])
-
-    def theirs(v):
-        return jnp.where(first, v[1], v[0])
-
-    near = [along_z(mine(left), -1), along_z(mine(right), 1)]
-    cross = [across_z(theirs(left), -1), across_z(theirs(right), 1)]
+    near = [along_z(left[0], -1), along_z(right[0], 1)]
+    cross = [across_z(left[1], -1), across_z(right[1], 1)]
     shape = jax.ShapeDtypeStruct(own.shape[2:], F32)
     return pl.pallas_call(
         finish_kernel,
@@ -147,7 +138,7 @@
         out_specs=whole(2),
         compiler_params=pltpu.CompilerParams(vmem_limit_bytes=LIMIT),
         name="finish",
-    )(*(in_vmem(v) for v in (mine(own), own_other, *near, *cross)))
+    )(*(in_vmem(v) for v in (own[0], own_other, *near, *cross)))
 
 
 def pair_kernel(own_ref, other_ref, out_ref):
@@ -190,14 +181,24 @@
 
 def backward_kernel(*refs):
     own_ref, near, across, level_b, up, down, hidden, gelu_slope = refs[:8]
-    down_term, up_term, low_ref, high_ref, slope = refs[8:]
+    terms, low_ref, high_ref, slope = refs[8:]
     own = own_ref.shape[0]
     slope[:own] = own_ref[...]
     slope[own : 2 * own] = near[...]
     slope[2 * own :] = across[...]
-    down_term[...] = dot_tn(slope[...], hidden[...]).astype(BF)
+    z, xh = lax.axis_index("z"), lax.axis_index("xh")
+    rows = terms.shape[3]
+
+    def put(term, which):
+        for half in range(NX):
+            for at in range(NZ):
+                start = (half * NZ + at) * rows
+                block = term[start : start + rows]
+                terms[lax.rem(at + NZ - z, NZ), lax.rem(half + xh, NX), which] = block
+
+    put(dot_tn(slope[...], hidden[...]).astype(BF), 0)
     pre = (gelu_slope[...] * dot(slope[...], down[...])).astype(BF)
-    up_term[...] = dot_tn(level_b[...], pre).astype(BF)
+    put(dot_tn(level_b[...], pre).astype(BF), 1)
     sums = dot_nt(pre, up[...]).astype(BF)
     low_ref[...] = sums[: 2 * own]
     high_ref[...] = sums[2 * own :]
@@ -379,16 +380,15 @@
     slope_own = norm_slope(upstream, branch_norm, branch_inv).astype(BF)
     slope_near = swap_xl(slope_own)
     slope_across = swap_core(jnp.concatenate([slope_own, slope_near], axis=0))
-    term_down, term_up, low, high = pl.pallas_call(
+    terms, low, high = pl.pallas_call(
         backward_kernel,
         out_shape=[
-            vmem((wide, hid), BF),
-            vmem((wide, hid), BF),
+            vmem((NZ, NX, 2, w_up.shape[0], hid), BF),
             vmem((2 * own, wide), BF),
             vmem((2 * own, wide), BF),
         ],
         in_specs=whole(8),
-        out_specs=whole(4),
+        out_specs=whole(3),
         scratch_shapes=[pltpu.VMEM((tokens, wide), BF)],
         cost_estimate=pl.CostEstimate(
             flops=8 * tokens * wide * hid, transcendentals=0, bytes_accessed=6_000_000
@@ -410,7 +410,7 @@
             )
         )
     )
-    grad_down, grad_up = scatter_rows((term_down, term_up))
+    grad_down, grad_up = scatter_rows(terms)
     grad_coarse = upstream + scatter_cols(low, high)
 
     both = jnp.concatenate([coarse, grad_coarse], axis=1).astype(BF)

time: 155 us -> 153 us (0.987); the launches traced: 153 us -> 153 us
  starting transfers between devices: 61.2 us -> 58.4 us
  waiting for transfers between devices: 69.3 us -> 71.7 us
    ppermute x16, starting transfers between devices: 28.5 us -> 24.4 us  [along_z(): return lax.ppermute(array, 'z', [(i, (i + step) % NZ) for i in range(NZ)])]
    ppermute x5, waiting for transfers between devices: 9.45 us -> 13.5 us  [swap_xl(): return lax.ppermute(array, 'xl', [(0, 1), (1, 0)])]
    add x4, other arithmetic: 0.15 us -> 2.78 us  [scatter_rows(): left, right = (left + block(NZ - k), right + block(k))]
    ppermute x2, waiting for transfers between devices: 6.02 us -> 3.55 us  [across_z(): return lax.ppermute(array, ROWS, pairs)]
    ppermute x6, waiting for transfers between devices: 11.1 us -> 13 us  [to_grid(): return lax.ppermute(array, GRID, pairs)]
    ppermute x6, starting transfers between devices: 12.6 us -> 14.5 us  [to_grid(): return lax.ppermute(array, GRID, pairs)]
    unnamed x20 -> x12, local copies, waits for them, and re-layouts: 5.07 us -> 4.68 us
  transfers between devices with their start and end apart: 37 -> 37, of which waited for: 23 -> 21; matrix products, arithmetic and copies ran while one was open for 3% -> 4% of each run, Pallas kernels for 4% -> 4%
where the time goes in v5:
time: 153 us
  waiting for transfers between devices  71.7 us (47%)
  starting transfers between devices  58.4 us (38%)
  Pallas kernels  10 us (7%)
  local copies, waits for them, and re-layouts  6.53 us (4%)
  other arithmetic  5.42 us (4%)
    ppermute x16, waiting for transfers between devices, along_z(): return lax.ppermute(array, 'z', [(i, (i + step) % NZ) for i in range(NZ)])  24.5 us
    ppermute x16, starting transfers between devices, along_z(): return lax.ppermute(array, 'z', [(i, (i + step) % NZ) for i in range(NZ)])  24.4 us
    ppermute x2, waiting for transfers between devices, swap_half(): return lax.ppermute(array, 'xh', [(0, 1), (1, 0)])  15.1 us
    ppermute x6, starting transfers between devices, to_grid(): return lax.ppermute(array, GRID, pairs)  14.5 us
    ppermute x5, waiting for transfers between devices, swap_xl(): return lax.ppermute(array, 'xl', [(0, 1), (1, 0)])  13.5 us
    ppermute x6, waiting for transfers between devices, to_grid(): return lax.ppermute(array, GRID, pairs)  13 us
    ppermute x6, starting transfers between devices, swap_core(): return lax.ppermute(array, 'core', [(0, 1), (1, 0)])  8.25 us
    pallas_call x1, Pallas kernels, whole_step(): pl.pallas_call(window_kernel, out_shape=[vmem((own, 4 * channels), BF), v...  5.2 us
  transfers between devices with their start and end apart: 37, of which 21 were waited for; matrix products, arithmetic and copies ran while one was open for 4% of the time, Pallas kernels for 4%

profile of v5, /device:TPU:1, one launch (start us, length us, event | category | flops | bytes accessed | tf_op | source)
XLA Modules:
  0.0 153.1 jit_solution(7048486491523288143)
XLA Ops:
  0.6 2.1 %collective-permute-start.4 = (bf16[192,1536]{1,0:T(8,128)(2,1)}, bf16[192,1536]{1,0:T(8,128)(2,1)S(1)}, u32[]{:S(2)}, u32[]{:S(2)}) collective-permute-start(bf16[192,1536]{1,0:T(8,128)(2,1)} %bitcast.64), channel_id=1, source_target_pairs={{0,8},{8,0},{1,9},{9,1},{2,10},{10,2},{3,11},{11,3},{4,12},{12,4},... | collective-permute-start | bytes 1769480 | tf_op jit(solution)/shard_map/ppermute | solution.py:71
  3.7 2.5 %collective-permute-start.8 = (bf16[2,48,768]{2,1,0:T(8,128)(2,1)S(1)}, bf16[2,48,768]{2,1,0:T(8,128)(2,1)S(1)}, u32[]{:S(2)}, u32[]{:S(2)}) collective-permute-start(bf16[2,48,768]{2,1,0:T(8,128)(2,1)S(1)} %pad_maximum_fusion.4.own_ref), channel_id=1, source_target_pairs={{0,128},{128,0},{1,129},{129,1},{2,130},{130,2},{3,131},{131,3},{4... | collective-permute-start | bytes 442376 | tf_op jit(solution)/shard_map/ppermute | solution.py:75
  6.2 15.1 %collective-permute-done.8.other_ref = bf16[2,48,768]{2,1,0:T(8,128)(2,1)S(1)} collective-permute-done((bf16[2,48,768]{2,1,0:T(8,128)(2,1)S(1)}, bf16[2,48,768]{2,1,0:T(8,128)(2,1)S(1)}, u32[]{:S(2)}, u32[]{:S(2)}) %collective-permute-start.8) | collective-permute-done | bytes 147488 | tf_op jit(solution)/shard_map/ppermute | solution.py:75
  21.4 1.7 %collective-permute-start.10 = (bf16[2,2,48,768]{3,2,1,0:T(8,128)(2,1)S(1)}, bf16[2,2,48,768]{3,2,1,0:T(8,128)(2,1)S(1)}, u32[]{:S(2)}, u32[]{:S(2)}) collective-permute-start(bf16[2,2,48,768]{3,2,1,0:T(8,128)(2,1)S(1)} %pair.1.refs_3_), channel_id=1, source_target_pairs={{0,16},{16,32},{32,48},{48,64},{64,80},{80,96},{96,112},{112,0},{1... | collective-permute-start | bytes 884744 | tf_op jit(solution)/shard_map/ppermute | solution.py:79
  23.1 4.0 %collective-permute-start.9 = (bf16[2,2,48,768]{3,2,1,0:T(8,128)(2,1)S(1)}, bf16[2,2,48,768]{3,2,1,0:T(8,128)(2,1)S(1)}, u32[]{:S(2)}, u32[]{:S(2)}) collective-permute-start(bf16[2,2,48,768]{3,2,1,0:T(8,128)(2,1)S(1)} %pair.1.refs_3_), channel_id=1, source_target_pairs={{0,112},{16,0},{32,16},{48,32},{64,48},{80,64},{96,80},{112,96},{1... | collective-permute-start | bytes 884744 | tf_op jit(solution)/shard_map/ppermute | solution.py:79
  27.1 1.8 %collective-permute-start.3 = (bf16[192,1536]{1,0:T(8,128)(2,1)}, bf16[192,1536]{1,0:T(8,128)(2,1)S(1)}, u32[]{:S(2)}, u32[]{:S(2)}) collective-permute-start(bf16[192,1536]{1,0:T(8,128)(2,1)} %bitcast.65), channel_id=1, source_target_pairs={{0,4},{4,0},{1,5},{5,1},{2,6},{6,2},{3,7},{7,3},{8,12},{12,8},{9,1... | collective-permute-start | bytes 1769480 | tf_op jit(solution)/shard_map/ppermute | solution.py:67
  28.9 3.9 %collective-permute-done.10.refs_5_ = bf16[2,2,48,768]{3,2,1,0:T(8,128)(2,1)S(1)} collective-permute-done((bf16[2,2,48,768]{3,2,1,0:T(8,128)(2,1)S(1)}, bf16[2,2,48,768]{3,2,1,0:T(8,128)(2,1)S(1)}, u32[]{:S(2)}, u32[]{:S(2)}) %collective-permute-start.10) | collective-permute-done | bytes 294944 | tf_op jit(solution)/shard_map/ppermute | solution.py:79
  32.9 2.7 %collective-permute-start.11 = (bf16[2,2,48,768]{3,2,1,0:T(8,128)(2,1)S(1)}, bf16[2,2,48,768]{3,2,1,0:T(8,128)(2,1)S(1)}, u32[]{:S(2)}, u32[]{:S(2)}) collective-permute-start(bf16[2,2,48,768]{3,2,1,0:T(8,128)(2,1)S(1)} %collective-permute-done.9.refs_4_), channel_id=1, source_target_pairs={{0,112},{16,0},{32,16},{48,32},{64,48},{80,64},{96,80},{112,96},{1... | collective-permute-start | bytes 884744 | tf_op jit(solution)/shard_map/ppermute | solution.py:79
  35.6 5.0 %collective-permute-done.12.refs_7_ = bf16[2,2,48,768]{3,2,1,0:T(8,128)(2,1)S(1)} collective-permute-done((bf16[2,2,48,768]{3,2,1,0:T(8,128)(2,1)S(1)}, bf16[2,2,48,768]{3,2,1,0:T(8,128)(2,1)S(1)}, u32[]{:S(2)}, u32[]{:S(2)}) %collective-permute-start.12) | collective-permute-done | bytes 294944 | tf_op jit(solution)/shard_map/ppermute | solution.py:79
  40.5 1.0 copy-done.1
  42.7 3.0 %collective-permute-start = (bf16[96,384]{1,0:T(8,128)(2,1)S(1)}, bf16[96,384]{1,0:T(8,128)(2,1)S(1)}, u32[]{:S(2)}, u32[]{:S(2)}) collective-permute-start(bf16[96,384]{1,0:T(8,128)(2,1)S(1)} %get-tuple-element.25), channel_id=1, source_target_pairs={{0,12},{4,0},{8,4},{12,8},{16,28},{20,16},{24,20},{28,24},{32,44},... | collective-permute-start | bytes 221192 | tf_op jit(solution)/shard_map/ppermute | solution.py:63
  45.8 2.2 %collective-permute-done.x1 = bf16[96,384]{1,0:T(8,128)(2,1)S(1)} collective-permute-done((bf16[96,384]{1,0:T(8,128)(2,1)S(1)}, bf16[96,384]{1,0:T(8,128)(2,1)S(1)}, u32[]{:S(2)}, u32[]{:S(2)}) %collective-permute-start) | collective-permute-done | bytes 73760 | tf_op jit(solution)/shard_map/ppermute | solution.py:63
  47.9 3.8 %collective-permute-start.1 = (bf16[96,384]{1,0:T(8,128)(2,1)S(1)}, bf16[96,384]{1,0:T(8,128)(2,1)S(1)}, u32[]{:S(2)}, u32[]{:S(2)}) collective-permute-start(bf16[96,384]{1,0:T(8,128)(2,1)S(1)} %get-tuple-element.26), channel_id=1, source_target_pairs={{0,240},{4,244},{8,248},{12,252},{16,0},{20,4},{24,8},{28,12},{32,... | collective-permute-start | bytes 221192 | tf_op jit(solution)/shard_map/ppermute | solution.py:63
  51.7 1.8 %collective-permute-done.1.x2 = bf16[96,384]{1,0:T(8,128)(2,1)S(1)} collective-permute-done((bf16[96,384]{1,0:T(8,128)(2,1)S(1)}, bf16[96,384]{1,0:T(8,128)(2,1)S(1)}, u32[]{:S(2)}, u32[]{:S(2)}) %collective-permute-start.1) | collective-permute-done | bytes 73760 | tf_op jit(solution)/shard_map/ppermute | solution.py:63
  53.5 5.8 %collective-permute-start.2 = (bf16[96,384]{1,0:T(8,128)(2,1)S(1)}, bf16[96,384]{1,0:T(8,128)(2,1)S(1)}, u32[]{:S(2)}, u32[]{:S(2)}) collective-permute-start(bf16[96,384]{1,0:T(8,128)(2,1)S(1)} %get-tuple-element.27), channel_id=1, source_target_pairs={{0,252},{4,240},{8,244},{12,248},{16,12},{20,0},{24,4},{28,8},{32,... | collective-permute-start | bytes 221192 | tf_op jit(solution)/shard_map/ppermute | solution.py:63
  59.2 1.9 %collective-permute-done.2.x3 = bf16[96,384]{1,0:T(8,128)(2,1)S(1)} collective-permute-done((bf16[96,384]{1,0:T(8,128)(2,1)S(1)}, bf16[96,384]{1,0:T(8,128)(2,1)S(1)}, u32[]{:S(2)}, u32[]{:S(2)}) %collective-permute-start.2) | collective-permute-done | bytes 73760 | tf_op jit(solution)/shard_map/ppermute | solution.py:63
  61.1 1.2 copy-done.3
  63.9 5.2 %window.1 = (bf16[64,1536]{1,0:T(8,128)(2,1)S(1)}, bf16[64,768]{1,0:T(8,128)(2,1)S(1)}) custom-call(f32[6]{0:T(128)S(1)} %copy-done.5, bf16[96,384]{1,0:T(8,128)(2,1)S(1)} %get-tuple-element.24.x0, bf16[96,384]{1,0:T(8,128)(2,1)S(1)} %collective-permute-done.x1, bf16[96,384]{1,0:T(8,128)(2,1)S(1)} %collective-permute-done.1.x2, ...), custom_call_target="tpu_custom_call" | custom-call | flops 402653184 | bytes 2000000 | tf_op jit(solution)/shard_map/window/pallas_call | solution.py:322
  69.1 5.0 %collective-permute-start.13 = (bf16[2,2,48,768]{3,2,1,0:T(8,128)(2,1)S(1)}, bf16[2,2,48,768]{3,2,1,0:T(8,128)(2,1)S(1)}, u32[]{:S(2)}, u32[]{:S(2)}) collective-permute-start(bf16[2,2,48,768]{3,2,1,0:T(8,128)(2,1)S(1)} %collective-permute-done.11.refs_6_), channel_id=1, source_target_pairs={{0,112},{16,0},{32,16},{48,32},{64,48},{80,64},{96,80},{112,96},{1... | collective-permute-start | bytes 884744 | tf_op jit(solution)/shard_map/ppermute | solution.py:79
  74.1 1.1 level.1
  75.5 3.3 %collective-permute-done.6.refs_1_ = bf16[64,768]{1,0:T(8,128)(2,1)S(1)} collective-permute-done((bf16[64,768]{1,0:T(8,128)(2,1)S(1)}, bf16[64,768]{1,0:T(8,128)(2,1)S(1)}, u32[]{:S(2)}, u32[]{:S(2)}) %collective-permute-start.6) | collective-permute-done | bytes 98336 | tf_op jit(solution)/shard_map/ppermute | solution.py:71
  78.8 2.5 %collective-permute-start.7 = (bf16[128,768]{1,0:T(8,128)(2,1)S(1)}, bf16[128,768]{1,0:T(8,128)(2,1)S(1)}, u32[]{:S(2)}, u32[]{:S(2)}) collective-permute-start(bf16[128,768]{1,0:T(8,128)(2,1)S(1)} %pad_maximum_fusion.2), channel_id=1, source_target_pairs={{0,4},{4,0},{1,5},{5,1},{2,6},{6,2},{3,7},{7,3},{8,12},{12,8},{9,1... | collective-permute-start | bytes 589832 | tf_op jit(solution)/shard_map/ppermute | solution.py:67
  81.3 1.7 %collective-permute-start.15 = (bf16[2,48,768]{2,1,0:T(8,128)(2,1)S(1)}, bf16[2,48,768]{2,1,0:T(8,128)(2,1)S(1)}, u32[]{:S(2)}, u32[]{:S(2)}) collective-permute-start(bf16[2,48,768]{2,1,0:T(8,128)(2,1)S(1)} %slice_bitcast_fusion.9), channel_id=1, source_target_pairs={{0,112},{16,0},{32,16},{48,32},{64,48},{80,64},{96,80},{112,96},{1... | collective-permute-start | bytes 442376 | tf_op jit(solution)/shard_map/ppermute | solution.py:79
  83.0 3.7 %collective-permute-done.15.refs_10_ = bf16[2,48,768]{2,1,0:T(8,128)(2,1)S(1)} collective-permute-done((bf16[2,48,768]{2,1,0:T(8,128)(2,1)S(1)}, bf16[2,48,768]{2,1,0:T(8,128)(2,1)S(1)}, u32[]{:S(2)}, u32[]{:S(2)}) %collective-permute-start.15) | collective-permute-done | bytes 147488 | tf_op jit(solution)/shard_map/ppermute | solution.py:79
  86.7 1.1 forward.1
  87.8 1.1 collective-permute-start.17
  89.0 1.1 collective-permute-done.17
  90.2 4.0 %collective-permute-done.18 = bf16[64,768]{1,0:T(8,128)(2,1)S(1)} collective-permute-done((bf16[64,768]{1,0:T(8,128)(2,1)S(1)}, bf16[64,768]{1,0:T(8,128)(2,1)S(1)}, u32[]{:S(2)}, u32[]{:S(2)}) %collective-permute-start.18) | collective-permute-done | bytes 98336 | tf_op jit(solution)/shard_map/ppermute | solution.py:71
  95.2 3.2 %collective-permute-done.19.refs_1_ = bf16[64,768]{1,0:T(8,128)(2,1)S(1)} collective-permute-done((bf16[64,768]{1,0:T(8,128)(2,1)S(1)}, bf16[64,768]{1,0:T(8,128)(2,1)S(1)}, u32[]{:S(2)}, u32[]{:S(2)}) %collective-permute-start.19) | collective-permute-done | bytes 98336 | tf_op jit(solution)/shard_map/ppermute | solution.py:71
  98.4 2.5 %collective-permute-start.20 = (bf16[128,768]{1,0:T(8,128)(2,1)S(1)}, bf16[128,768]{1,0:T(8,128)(2,1)S(1)}, u32[]{:S(2)}, u32[]{:S(2)}) collective-permute-start(bf16[128,768]{1,0:T(8,128)(2,1)S(1)} %pad_maximum_fusion.3), channel_id=1, source_target_pairs={{0,4},{4,0},{1,5},{5,1},{2,6},{6,2},{3,7},{7,3},{8,12},{12,8},{9,1... | collective-permute-start | bytes 589832 | tf_op jit(solution)/shard_map/ppermute | solution.py:67
  100.9 1.1 collective-permute-done.20.refs_2_
  102.0 1.5 %backward.1 = (bf16[8,2,2,48,768]{4,3,2,1,0:T(8,128)(2,1)S(1)}, bf16[128,768]{1,0:T(8,128)(2,1)S(1)}, bf16[128,768]{1,0:T(8,128)(2,1)S(1)}) custom-call(bf16[64,768]{1,0:T(8,128)(2,1)S(1)} %get-tuple-element.52.refs_0_, bf16[64,768]{1,0:T(8,128)(2,1)S(1)} %collective-permute-done.19.refs_1_, bf16[128,768]{1,0:T(8,128)(2,1)S(1)} %collective-permute-done.20.refs_2_, ...), custom_call_target="tpu_custom_call" | custom-call | flops 1207959552 | bytes 6000000 | tf_op jit(solution)/shard_map/backward/pallas_call | solution.py:383
  104.6 3.4 %collective-permute-start.27 = (bf16[2,48,768]{2,1,0:T(8,128)(2,1)S(1)}, bf16[2,48,768]{2,1,0:T(8,128)(2,1)S(1)}, u32[]{:S(2)}, u32[]{:S(2)}) collective-permute-start(bf16[2,48,768]{2,1,0:T(8,128)(2,1)S(1)} %get-tuple-element.48), channel_id=1, source_target_pairs={{0,112},{16,0},{32,16},{48,32},{64,48},{80,64},{96,80},{112,96},{1... | collective-permute-start | bytes 442376 | tf_op jit(solution)/shard_map/ppermute | solution.py:79
  108.0 1.0 collective-permute-start.26
  109.0 2.1 %collective-permute-done.27 = bf16[2,48,768]{2,1,0:T(8,128)(2,1)S(1)} collective-permute-done((bf16[2,48,768]{2,1,0:T(8,128)(2,1)S(1)}, bf16[2,48,768]{2,1,0:T(8,128)(2,1)S(1)}, u32[]{:S(2)}, u32[]{:S(2)}) %collective-permute-start.27) | collective-permute-done | bytes 147488 | tf_op jit(solution)/shard_map/ppermute | solution.py:79
  111.1 3.5 %collective-permute-start.28 = (bf16[2,2,48,768]{3,2,1,0:T(8,128)(2,1)S(1)}, bf16[2,2,48,768]{3,2,1,0:T(8,128)(2,1)S(1)}, u32[]{:S(2)}, u32[]{:S(2)}) collective-permute-start(bf16[2,2,48,768]{3,2,1,0:T(8,128)(2,1)S(1)} %pad_maximum_fusion), channel_id=1, source_target_pairs={{0,112},{16,0},{32,16},{48,32},{64,48},{80,64},{96,80},{112,96},{1... | collective-permute-start | bytes 884744 | tf_op jit(solution)/shard_map/ppermute | solution.py:79
  115.8 3.0 %collective-permute-done.22 = bf16[64,768]{1,0:T(8,128)(2,1)S(1)} collective-permute-done((bf16[64,768]{1,0:T(8,128)(2,1)S(1)}, bf16[64,768]{1,0:T(8,128)(2,1)S(1)}, u32[]{:S(2)}, u32[]{:S(2)}) %collective-permute-start.22) | collective-permute-done | bytes 98336 | tf_op jit(solution)/shard_map/ppermute | solution.py:71
  120.0 1.8 %collective-permute-start.25 = (bf16[16,1536]{1,0:T(8,128)(2,1)S(1)}, bf16[16,1536]{1,0:T(8,128)(2,1)S(1)}, u32[]{:S(2)}, u32[]{:S(2)}) collective-permute-start(bf16[16,1536]{1,0:T(8,128)(2,1)S(1)} %get-tuple-element.62), channel_id=1, source_target_pairs={{0,4},{4,8},{8,12},{12,0},{16,20},{20,24},{24,28},{28,16},{32,36},... | collective-permute-start | bytes 147464 | tf_op jit(solution)/shard_map/ppermute | solution.py:63
  122.5 7.2 %collective-permute-done.23 = bf16[16,1536]{1,0:T(8,128)(2,1)S(1)} collective-permute-done((bf16[16,1536]{1,0:T(8,128)(2,1)S(1)}, bf16[16,1536]{1,0:T(8,128)(2,1)S(1)}, u32[]{:S(2)}, u32[]{:S(2)}) %collective-permute-start.23) | collective-permute-done | bytes 49184 | tf_op jit(solution)/shard_map/ppermute | solution.py:63
  130.0 1.0 bitcast_add_fusion.1
  131.0 1.5 %collective-permute-start.33 = (bf16[2,2,48,768]{3,2,1,0:T(8,128)(2,1)S(1)}, bf16[2,2,48,768]{3,2,1,0:T(8,128)(2,1)S(1)}, u32[]{:S(2)}, u32[]{:S(2)}) collective-permute-start(bf16[2,2,48,768]{3,2,1,0:T(8,128)(2,1)S(1)} %bitcast_add_fusion.1), channel_id=1, source_target_pairs={{0,16},{16,32},{32,48},{48,64},{64,80},{80,96},{96,112},{112,0},{1... | collective-permute-start | bytes 884744 | tf_op jit(solution)/shard_map/ppermute | solution.py:79
  132.6 5.6 %collective-permute-done.29 = bf16[2,2,48,768]{3,2,1,0:T(8,128)(2,1)} collective-permute-done((bf16[2,2,48,768]{3,2,1,0:T(8,128)(2,1)}, bf16[2,2,48,768]{3,2,1,0:T(8,128)(2,1)}, u32[]{:S(2)}, u32[]{:S(2)}) %collective-permute-start.29) | collective-permute-done | bytes 294944 | tf_op jit(solution)/shard_map/ppermute | solution.py:79
  138.1 1.0 fusion
  139.1 2.1 %collective-permute-start.35 = (bf16[2,48,768]{2,1,0:T(8,128)(2,1)S(1)}, bf16[2,48,768]{2,1,0:T(8,128)(2,1)S(1)}, u32[]{:S(2)}, u32[]{:S(2)}) collective-permute-start(bf16[2,48,768]{2,1,0:T(8,128)(2,1)S(1)} %get-tuple-element.57), channel_id=1, source_target_pairs={{0,240},{16,128},{32,144},{48,160},{64,176},{80,192},{96,208},{112... | collective-permute-start | bytes 442376 | tf_op jit(solution)/shard_map/ppermute | solution.py:87
  141.3 2.7 %collective-permute-start.36 = (bf16[2,48,768]{2,1,0:T(8,128)(2,1)S(1)}, bf16[2,48,768]{2,1,0:T(8,128)(2,1)S(1)}, u32[]{:S(2)}, u32[]{:S(2)}) collective-permute-start(bf16[2,48,768]{2,1,0:T(8,128)(2,1)S(1)} %get-tuple-element.55), channel_id=1, source_target_pairs={{0,144},{16,160},{32,176},{48,192},{64,208},{80,224},{96,240},{112... | collective-permute-start | bytes 442376 | tf_op jit(solution)/shard_map/ppermute | solution.py:87
  145.5 1.8 %collective-permute-done.35.refs_4_ = bf16[2,48,768]{2,1,0:T(8,128)(2,1)S(1)} collective-permute-done((bf16[2,48,768]{2,1,0:T(8,128)(2,1)S(1)}, bf16[2,48,768]{2,1,0:T(8,128)(2,1)S(1)}, u32[]{:S(2)}, u32[]{:S(2)}) %collective-permute-start.35) | collective-permute-done | bytes 147488 | tf_op jit(solution)/shard_map/ppermute | solution.py:87
  147.8 1.7 %collective-permute-done.36.refs_5_ = bf16[2,48,768]{2,1,0:T(8,128)(2,1)S(1)} collective-permute-done((bf16[2,48,768]{2,1,0:T(8,128)(2,1)S(1)}, bf16[2,48,768]{2,1,0:T(8,128)(2,1)S(1)}, u32[]{:S(2)}, u32[]{:S(2)}) %collective-permute-start.36) | collective-permute-done | bytes 147488 | tf_op jit(solution)/shard_map/ppermute | solution.py:87
  149.5 2.8 %collective-permute-done.34.refs_3_ = bf16[2,48,768]{2,1,0:T(8,128)(2,1)S(1)} collective-permute-done((bf16[2,48,768]{2,1,0:T(8,128)(2,1)S(1)}, bf16[2,48,768]{2,1,0:T(8,128)(2,1)S(1)}, u32[]{:S(2)}, u32[]{:S(2)}) %collective-permute-start.34) | collective-permute-done | bytes 147488 | tf_op jit(solution)/shard_map/ppermute | solution.py:79
  (80 shorter events, 12.5 us)
Async XLA Ops:
  0.6 73.5 %copy-start = (bf16[1536,192]{0,1:T(8,128)(2,1)S(1)}, bf16[1536,192]{0,1:T(8,128)(2,1)}, u32[]{:S(2)}) copy-start(bf16[1536,192]{0,1:T(8,128)(2,1)} %param.12) | copy-start | bytes 1769476
  0.6 28.3 %collective-permute-start.4 = (bf16[192,1536]{1,0:T(8,128)(2,1)}, bf16[192,1536]{1,0:T(8,128)(2,1)S(1)}, u32[]{:S(2)}, u32[]{:S(2)}) collective-permute-start(bf16[192,1536]{1,0:T(8,128)(2,1)} %bitcast.64), channel_id=1, source_target_pairs={{0,8},{8,0},{1,9},{9,1},{2,10},{10,2},{3,11},{11,3},{4,12},{12,4},... | collective-permute-start | bytes 1769480 | tf_op jit(solution)/shard_map/ppermute | solution.py:71
  3.7 17.6 %collective-permute-start.8 = (bf16[2,48,768]{2,1,0:T(8,128)(2,1)S(1)}, bf16[2,48,768]{2,1,0:T(8,128)(2,1)S(1)}, u32[]{:S(2)}, u32[]{:S(2)}) collective-permute-start(bf16[2,48,768]{2,1,0:T(8,128)(2,1)S(1)} %pad_maximum_fusion.4.own_ref), channel_id=1, source_target_pairs={{0,128},{128,0},{1,129},{129,1},{2,130},{130,2},{3,131},{131,3},{4... | collective-permute-start | bytes 442376 | tf_op jit(solution)/shard_map/ppermute | solution.py:75
  21.4 11.5 %collective-permute-start.10 = (bf16[2,2,48,768]{3,2,1,0:T(8,128)(2,1)S(1)}, bf16[2,2,48,768]{3,2,1,0:T(8,128)(2,1)S(1)}, u32[]{:S(2)}, u32[]{:S(2)}) collective-permute-start(bf16[2,2,48,768]{3,2,1,0:T(8,128)(2,1)S(1)} %pair.1.refs_3_), channel_id=1, source_target_pairs={{0,16},{16,32},{32,48},{48,64},{64,80},{80,96},{96,112},{112,0},{1... | collective-permute-start | bytes 884744 | tf_op jit(solution)/shard_map/ppermute | solution.py:79
  23.1 9.8 %collective-permute-start.9 = (bf16[2,2,48,768]{3,2,1,0:T(8,128)(2,1)S(1)}, bf16[2,2,48,768]{3,2,1,0:T(8,128)(2,1)S(1)}, u32[]{:S(2)}, u32[]{:S(2)}) collective-permute-start(bf16[2,2,48,768]{3,2,1,0:T(8,128)(2,1)S(1)} %pair.1.refs_3_), channel_id=1, source_target_pairs={{0,112},{16,0},{32,16},{48,32},{64,48},{80,64},{96,80},{112,96},{1... | collective-permute-start | bytes 884744 | tf_op jit(solution)/shard_map/ppermute | solution.py:79
  27.1 47.0 %collective-permute-start.3 = (bf16[192,1536]{1,0:T(8,128)(2,1)}, bf16[192,1536]{1,0:T(8,128)(2,1)S(1)}, u32[]{:S(2)}, u32[]{:S(2)}) collective-permute-start(bf16[192,1536]{1,0:T(8,128)(2,1)} %bitcast.65), channel_id=1, source_target_pairs={{0,4},{4,0},{1,5},{5,1},{2,6},{6,2},{3,7},{7,3},{8,12},{12,8},{9,1... | collective-permute-start | bytes 1769480 | tf_op jit(solution)/shard_map/ppermute | solution.py:67
  28.9 45.2 %collective-permute-start.5 = (bf16[192,1536]{1,0:T(8,128)(2,1)S(1)}, bf16[192,1536]{1,0:T(8,128)(2,1)S(1)}, u32[]{:S(2)}, u32[]{:S(2)}) collective-permute-start(bf16[192,1536]{1,0:T(8,128)(2,1)S(1)} %collective-permute-done.4.near_ref), channel_id=1, source_target_pairs={{0,4},{4,0},{1,5},{5,1},{2,6},{6,2},{3,7},{7,3},{8,12},{12,8},{9,1... | collective-permute-start | bytes 1769480 | tf_op jit(solution)/shard_map/ppermute | solution.py:67
  32.9 7.7 %collective-permute-start.12 = (bf16[2,2,48,768]{3,2,1,0:T(8,128)(2,1)S(1)}, bf16[2,2,48,768]{3,2,1,0:T(8,128)(2,1)S(1)}, u32[]{:S(2)}, u32[]{:S(2)}) collective-permute-start(bf16[2,2,48,768]{3,2,1,0:T(8,128)(2,1)S(1)} %collective-permute-done.10.refs_5_), channel_id=1, source_target_pairs={{0,16},{16,32},{32,48},{48,64},{64,80},{80,96},{96,112},{112,0},{1... | collective-permute-start | bytes 884744 | tf_op jit(solution)/shard_map/ppermute | solution.py:79
  32.9 36.2 %collective-permute-start.11 = (bf16[2,2,48,768]{3,2,1,0:T(8,128)(2,1)S(1)}, bf16[2,2,48,768]{3,2,1,0:T(8,128)(2,1)S(1)}, u32[]{:S(2)}, u32[]{:S(2)}) collective-permute-start(bf16[2,2,48,768]{3,2,1,0:T(8,128)(2,1)S(1)} %collective-permute-done.9.refs_4_), channel_id=1, source_target_pairs={{0,112},{16,0},{32,16},{48,32},{64,48},{80,64},{96,80},{112,96},{1... | collective-permute-start | bytes 884744 | tf_op jit(solution)/shard_map/ppermute | solution.py:79
  40.5 34.8 %collective-permute-start.14 = (bf16[2,2,48,768]{3,2,1,0:T(8,128)(2,1)S(1)}, bf16[2,2,48,768]{3,2,1,0:T(8,128)(2,1)S(1)}, u32[]{:S(2)}, u32[]{:S(2)}) collective-permute-start(bf16[2,2,48,768]{3,2,1,0:T(8,128)(2,1)S(1)} %collective-permute-done.12.refs_7_), channel_id=1, source_target_pairs={{0,16},{16,32},{32,48},{48,64},{64,80},{80,96},{96,112},{112,0},{1... | collective-permute-start | bytes 884744 | tf_op jit(solution)/shard_map/ppermute | solution.py:79
  40.5 1.0 copy-start.1
  41.5 0.9 copy-start.2
  42.7 5.2 %collective-permute-start = (bf16[96,384]{1,0:T(8,128)(2,1)S(1)}, bf16[96,384]{1,0:T(8,128)(2,1)S(1)}, u32[]{:S(2)}, u32[]{:S(2)}) collective-permute-start(bf16[96,384]{1,0:T(8,128)(2,1)S(1)} %get-tuple-element.25), channel_id=1, source_target_pairs={{0,12},{4,0},{8,4},{12,8},{16,28},{20,16},{24,20},{28,24},{32,44},... | collective-permute-start | bytes 221192 | tf_op jit(solution)/shard_map/ppermute | solution.py:63
  47.9 5.6 %collective-permute-start.1 = (bf16[96,384]{1,0:T(8,128)(2,1)S(1)}, bf16[96,384]{1,0:T(8,128)(2,1)S(1)}, u32[]{:S(2)}, u32[]{:S(2)}) collective-permute-start(bf16[96,384]{1,0:T(8,128)(2,1)S(1)} %get-tuple-element.26), channel_id=1, source_target_pairs={{0,240},{4,244},{8,248},{12,252},{16,0},{20,4},{24,8},{28,12},{32,... | collective-permute-start | bytes 221192 | tf_op jit(solution)/shard_map/ppermute | solution.py:63
  53.5 7.6 %collective-permute-start.2 = (bf16[96,384]{1,0:T(8,128)(2,1)S(1)}, bf16[96,384]{1,0:T(8,128)(2,1)S(1)}, u32[]{:S(2)}, u32[]{:S(2)}) collective-permute-start(bf16[96,384]{1,0:T(8,128)(2,1)S(1)} %get-tuple-element.27), channel_id=1, source_target_pairs={{0,252},{4,240},{8,244},{12,248},{16,12},{20,0},{24,4},{28,8},{32,... | collective-permute-start | bytes 221192 | tf_op jit(solution)/shard_map/ppermute | solution.py:63
  61.1 1.2 copy-start.3
  62.3 1.0 copy-start.4
  63.2 0.7 copy-start.5
  69.1 12.2 %collective-permute-start.13 = (bf16[2,2,48,768]{3,2,1,0:T(8,128)(2,1)S(1)}, bf16[2,2,48,768]{3,2,1,0:T(8,128)(2,1)S(1)}, u32[]{:S(2)}, u32[]{:S(2)}) collective-permute-start(bf16[2,2,48,768]{3,2,1,0:T(8,128)(2,1)S(1)} %collective-permute-done.11.refs_6_), channel_id=1, source_target_pairs={{0,112},{16,0},{32,16},{48,32},{64,48},{80,64},{96,80},{112,96},{1... | collective-permute-start | bytes 884744 | tf_op jit(solution)/shard_map/ppermute | solution.py:79
  75.2 3.6 %collective-permute-start.6 = (bf16[64,768]{1,0:T(8,128)(2,1)S(1)}, bf16[64,768]{1,0:T(8,128)(2,1)S(1)}, u32[]{:S(2)}, u32[]{:S(2)}) collective-permute-start(bf16[64,768]{1,0:T(8,128)(2,1)S(1)} %get-tuple-element.30.refs_0_), channel_id=1, source_target_pairs={{0,8},{8,0},{1,9},{9,1},{2,10},{10,2},{3,11},{11,3},{4,12},{12,4},... | collective-permute-start | bytes 294920 | tf_op jit(solution)/shard_map/ppermute | solution.py:71
  75.4 7.7 %collective-permute-start.16 = (bf16[2,48,768]{2,1,0:T(8,128)(2,1)S(1)}, bf16[2,48,768]{2,1,0:T(8,128)(2,1)S(1)}, u32[]{:S(2)}, u32[]{:S(2)}) collective-permute-start(bf16[2,48,768]{2,1,0:T(8,128)(2,1)S(1)} %slice_bitcast_fusion.8), channel_id=1, source_target_pairs={{0,16},{16,32},{32,48},{48,64},{64,80},{80,96},{96,112},{112,0},{1... | collective-permute-start | bytes 442376 | tf_op jit(solution)/shard_map/ppermute | solution.py:79
  78.8 7.9 %collective-permute-start.7 = (bf16[128,768]{1,0:T(8,128)(2,1)S(1)}, bf16[128,768]{1,0:T(8,128)(2,1)S(1)}, u32[]{:S(2)}, u32[]{:S(2)}) collective-permute-start(bf16[128,768]{1,0:T(8,128)(2,1)S(1)} %pad_maximum_fusion.2), channel_id=1, source_target_pairs={{0,4},{4,0},{1,5},{5,1},{2,6},{6,2},{3,7},{7,3},{8,12},{12,8},{9,1... | collective-permute-start | bytes 589832 | tf_op jit(solution)/shard_map/ppermute | solution.py:67
  81.3 5.4 %collective-permute-start.15 = (bf16[2,48,768]{2,1,0:T(8,128)(2,1)S(1)}, bf16[2,48,768]{2,1,0:T(8,128)(2,1)S(1)}, u32[]{:S(2)}, u32[]{:S(2)}) collective-permute-start(bf16[2,48,768]{2,1,0:T(8,128)(2,1)S(1)} %slice_bitcast_fusion.9), channel_id=1, source_target_pairs={{0,112},{16,0},{32,16},{48,32},{64,48},{80,64},{96,80},{112,96},{1... | collective-permute-start | bytes 442376 | tf_op jit(solution)/shard_map/ppermute | solution.py:79
  87.8 2.2 %collective-permute-start.17 = (bf16[128,768]{1,0:T(8,128)(2,1)S(1)}, bf16[128,768]{1,0:T(8,128)(2,1)S(1)}, u32[]{:S(2)}, u32[]{:S(2)}) collective-permute-start(bf16[128,768]{1,0:T(8,128)(2,1)S(1)} %get-tuple-element.32), channel_id=1, source_target_pairs={{0,4},{4,0},{1,5},{5,1},{2,6},{6,2},{3,7},{7,3},{8,12},{12,8},{9,1... | collective-permute-start | bytes 589832 | tf_op jit(solution)/shard_map/ppermute | solution.py:67
  90.1 4.1 %collective-permute-start.18 = (bf16[64,768]{1,0:T(8,128)(2,1)S(1)}, bf16[64,768]{1,0:T(8,128)(2,1)S(1)}, u32[]{:S(2)}, u32[]{:S(2)}) collective-permute-start(bf16[64,768]{1,0:T(8,128)(2,1)S(1)} %slice.223), channel_id=1, source_target_pairs={{0,8},{8,0},{1,9},{9,1},{2,10},{10,2},{3,11},{11,3},{4,12},{12,4},... | collective-permute-start | bytes 294920 | tf_op jit(solution)/shard_map/ppermute | solution.py:71
  94.9 3.6 %collective-permute-start.19 = (bf16[64,768]{1,0:T(8,128)(2,1)S(1)}, bf16[64,768]{1,0:T(8,128)(2,1)S(1)}, u32[]{:S(2)}, u32[]{:S(2)}) collective-permute-start(bf16[64,768]{1,0:T(8,128)(2,1)S(1)} %get-tuple-element.52.refs_0_), channel_id=1, source_target_pairs={{0,8},{8,0},{1,9},{9,1},{2,10},{10,2},{3,11},{11,3},{4,12},{12,4},... | collective-permute-start | bytes 294920 | tf_op jit(solution)/shard_map/ppermute | solution.py:71
  98.4 3.5 %collective-permute-start.20 = (bf16[128,768]{1,0:T(8,128)(2,1)S(1)}, bf16[128,768]{1,0:T(8,128)(2,1)S(1)}, u32[]{:S(2)}, u32[]{:S(2)}) collective-permute-start(bf16[128,768]{1,0:T(8,128)(2,1)S(1)} %pad_maximum_fusion.3), channel_id=1, source_target_pairs={{0,4},{4,0},{1,5},{5,1},{2,6},{6,2},{3,7},{7,3},{8,12},{12,8},{9,1... | collective-permute-start | bytes 589832 | tf_op jit(solution)/shard_map/ppermute | solution.py:67
  104.2 10.4 %collective-permute-start.21 = (bf16[128,768]{1,0:T(8,128)(2,1)S(1)}, bf16[128,768]{1,0:T(8,128)(2,1)S(1)}, u32[]{:S(2)}, u32[]{:S(2)}) collective-permute-start(bf16[128,768]{1,0:T(8,128)(2,1)S(1)} %get-tuple-element.40), channel_id=1, source_target_pairs={{0,4},{4,0},{1,5},{5,1},{2,6},{6,2},{3,7},{7,3},{8,12},{12,8},{9,1... | collective-permute-start | bytes 589832 | tf_op jit(solution)/shard_map/ppermute | solution.py:67
  104.6 10.0 %collective-permute-start.31 = (bf16[2,48,768]{2,1,0:T(8,128)(2,1)S(1)}, bf16[2,48,768]{2,1,0:T(8,128)(2,1)S(1)}, u32[]{:S(2)}, u32[]{:S(2)}) collective-permute-start(bf16[2,48,768]{2,1,0:T(8,128)(2,1)S(1)} %get-tuple-element.47), channel_id=1, source_target_pairs={{0,16},{16,32},{32,48},{48,64},{64,80},{80,96},{96,112},{112,0},{1... | collective-permute-start | bytes 442376 | tf_op jit(solution)/shard_map/ppermute | solution.py:79
  104.6 6.5 %collective-permute-start.27 = (bf16[2,48,768]{2,1,0:T(8,128)(2,1)S(1)}, bf16[2,48,768]{2,1,0:T(8,128)(2,1)S(1)}, u32[]{:S(2)}, u32[]{:S(2)}) collective-permute-start(bf16[2,48,768]{2,1,0:T(8,128)(2,1)S(1)} %get-tuple-element.48), channel_id=1, source_target_pairs={{0,112},{16,0},{32,16},{48,32},{64,48},{80,64},{96,80},{112,96},{1... | collective-permute-start | bytes 442376 | tf_op jit(solution)/shard_map/ppermute | solution.py:79
  108.0 37.5 %collective-permute-start.26 = (bf16[2,48,768]{2,1,0:T(8,128)(2,1)}, bf16[2,48,768]{2,1,0:T(8,128)(2,1)S(1)}, u32[]{:S(2)}, u32[]{:S(2)}) collective-permute-start(bf16[2,48,768]{2,1,0:T(8,128)(2,1)} %get-tuple-element.49), channel_id=1, source_target_pairs={{0,128},{128,0},{1,129},{129,1},{2,130},{130,2},{3,131},{131,3},{4... | collective-permute-start | bytes 442376 | tf_op jit(solution)/shard_map/ppermute | solution.py:75
  111.1 8.9 %collective-permute-start.28 = (bf16[2,2,48,768]{3,2,1,0:T(8,128)(2,1)S(1)}, bf16[2,2,48,768]{3,2,1,0:T(8,128)(2,1)S(1)}, u32[]{:S(2)}, u32[]{:S(2)}) collective-permute-start(bf16[2,2,48,768]{3,2,1,0:T(8,128)(2,1)S(1)} %pad_maximum_fusion), channel_id=1, source_target_pairs={{0,112},{16,0},{32,16},{48,32},{64,48},{80,64},{96,80},{112,96},{1... | collective-permute-start | bytes 884744 | tf_op jit(solution)/shard_map/ppermute | solution.py:79
  114.7 4.1 %collective-permute-start.22 = (bf16[64,768]{1,0:T(8,128)(2,1)S(1)}, bf16[64,768]{1,0:T(8,128)(2,1)S(1)}, u32[]{:S(2)}, u32[]{:S(2)}) collective-permute-start(bf16[64,768]{1,0:T(8,128)(2,1)S(1)} %slice.222), channel_id=1, source_target_pairs={{0,8},{8,0},{1,9},{9,1},{2,10},{10,2},{3,11},{11,3},{4,12},{12,4},... | collective-permute-start | bytes 294920 | tf_op jit(solution)/shard_map/ppermute | solution.py:71
  115.8 14.2 %collective-permute-start.32 = (bf16[2,2,48,768]{3,2,1,0:T(8,128)(2,1)}, bf16[2,2,48,768]{3,2,1,0:T(8,128)(2,1)}, u32[]{:S(2)}, u32[]{:S(2)}) collective-permute-start(bf16[2,2,48,768]{3,2,1,0:T(8,128)(2,1)} %pad_maximum_fusion.1), channel_id=1, source_target_pairs={{0,16},{16,32},{32,48},{48,64},{64,80},{80,96},{96,112},{112,0},{1... | collective-permute-start | bytes 884744 | tf_op jit(solution)/shard_map/ppermute | solution.py:79
  118.8 10.8 %collective-permute-start.23 = (bf16[16,1536]{1,0:T(8,128)(2,1)S(1)}, bf16[16,1536]{1,0:T(8,128)(2,1)S(1)}, u32[]{:S(2)}, u32[]{:S(2)}) collective-permute-start(bf16[16,1536]{1,0:T(8,128)(2,1)S(1)} %get-tuple-element.59), channel_id=1, source_target_pairs={{0,20},{4,24},{8,28},{12,16},{16,36},{20,40},{24,44},{28,32},{32,5... | collective-permute-start | bytes 147464 | tf_op jit(solution)/shard_map/ppermute | solution.py:63
  118.9 10.7 %collective-permute-start.24 = (bf16[16,1536]{1,0:T(8,128)(2,1)S(1)}, bf16[16,1536]{1,0:T(8,128)(2,1)S(1)}, u32[]{:S(2)}, u32[]{:S(2)}) collective-permute-start(bf16[16,1536]{1,0:T(8,128)(2,1)S(1)} %get-tuple-element.60), channel_id=1, source_target_pairs={{0,16},{4,20},{8,24},{12,28},{16,32},{20,36},{24,40},{28,44},{32,4... | collective-permute-start | bytes 147464 | tf_op jit(solution)/shard_map/ppermute | solution.py:63
  120.0 9.7 %collective-permute-start.25 = (bf16[16,1536]{1,0:T(8,128)(2,1)S(1)}, bf16[16,1536]{1,0:T(8,128)(2,1)S(1)}, u32[]{:S(2)}, u32[]{:S(2)}) collective-permute-start(bf16[16,1536]{1,0:T(8,128)(2,1)S(1)} %get-tuple-element.62), channel_id=1, source_target_pairs={{0,4},{4,8},{8,12},{12,0},{16,20},{20,24},{24,28},{28,16},{32,36},... | collective-permute-start | bytes 147464 | tf_op jit(solution)/shard_map/ppermute | solution.py:63
  129.7 8.5 %collective-permute-start.29 = (bf16[2,2,48,768]{3,2,1,0:T(8,128)(2,1)}, bf16[2,2,48,768]{3,2,1,0:T(8,128)(2,1)}, u32[]{:S(2)}, u32[]{:S(2)}) collective-permute-start(bf16[2,2,48,768]{3,2,1,0:T(8,128)(2,1)} %fusion.1), channel_id=1, source_target_pairs={{0,112},{16,0},{32,16},{48,32},{64,48},{80,64},{96,80},{112,96},{1... | collective-permute-start | bytes 884744 | tf_op jit(solution)/shard_map/ppermute | solution.py:79
  131.0 10.2 %collective-permute-start.33 = (bf16[2,2,48,768]{3,2,1,0:T(8,128)(2,1)S(1)}, bf16[2,2,48,768]{3,2,1,0:T(8,128)(2,1)S(1)}, u32[]{:S(2)}, u32[]{:S(2)}) collective-permute-start(bf16[2,2,48,768]{3,2,1,0:T(8,128)(2,1)S(1)} %bitcast_add_fusion.1), channel_id=1, source_target_pairs={{0,16},{16,32},{32,48},{48,64},{64,80},{80,96},{96,112},{112,0},{1... | collective-permute-start | bytes 884744 | tf_op jit(solution)/shard_map/ppermute | solution.py:79
  139.1 8.2 %collective-permute-start.35 = (bf16[2,48,768]{2,1,0:T(8,128)(2,1)S(1)}, bf16[2,48,768]{2,1,0:T(8,128)(2,1)S(1)}, u32[]{:S(2)}, u32[]{:S(2)}) collective-permute-start(bf16[2,48,768]{2,1,0:T(8,128)(2,1)S(1)} %get-tuple-element.57), channel_id=1, source_target_pairs={{0,240},{16,128},{32,144},{48,160},{64,176},{80,192},{96,208},{112... | collective-permute-start | bytes 442376 | tf_op jit(solution)/shard_map/ppermute | solution.py:87
  141.2 6.5 %collective-permute-start.30 = (bf16[2,48,768]{2,1,0:T(8,128)(2,1)S(1)}, bf16[2,48,768]{2,1,0:T(8,128)(2,1)S(1)}, u32[]{:S(2)}, u32[]{:S(2)}) collective-permute-start(bf16[2,48,768]{2,1,0:T(8,128)(2,1)S(1)} %get-tuple-element.58), channel_id=1, source_target_pairs={{0,112},{16,0},{32,16},{48,32},{64,48},{80,64},{96,80},{112,96},{1... | collective-permute-start | bytes 442376 | tf_op jit(solution)/shard_map/ppermute | solution.py:79
  141.3 8.2 %collective-permute-start.36 = (bf16[2,48,768]{2,1,0:T(8,128)(2,1)S(1)}, bf16[2,48,768]{2,1,0:T(8,128)(2,1)S(1)}, u32[]{:S(2)}, u32[]{:S(2)}) collective-permute-start(bf16[2,48,768]{2,1,0:T(8,128)(2,1)S(1)} %get-tuple-element.55), channel_id=1, source_target_pairs={{0,144},{16,160},{32,176},{48,192},{64,208},{80,224},{96,240},{112... | collective-permute-start | bytes 442376 | tf_op jit(solution)/shard_map/ppermute | solution.py:87
  144.0 8.3 %collective-permute-start.34 = (bf16[2,48,768]{2,1,0:T(8,128)(2,1)S(1)}, bf16[2,48,768]{2,1,0:T(8,128)(2,1)S(1)}, u32[]{:S(2)}, u32[]{:S(2)}) collective-permute-start(bf16[2,48,768]{2,1,0:T(8,128)(2,1)S(1)} %get-tuple-element.56), channel_id=1, source_target_pairs={{0,16},{16,32},{32,48},{48,64},{64,80},{80,96},{96,112},{112,0},{1... | collective-permute-start | bytes 442376 | tf_op jit(solution)/shard_map/ppermute | solution.py:79

commit v6 on v5

--- a/solution.py
+++ b/solution.py
@@ -126,10 +126,11 @@
     left = jnp.stack([near_left[0] + left, near_left[1]])
     right = jnp.stack([near_right[0], near_right[1] + right])
     for k in (2, 1):
-        left, right = along_z(left, -1), along_z(right, 1)
+        left = along_z(left, -1)
+        right = along_z(right, 1)
         left, right = left + block(NZ - k), right + block(k)
-    near = [along_z(left[0], -1), along_z(right[0], 1)]
-    cross = [across_z(left[1], -1), across_z(right[1], 1)]
+    near, cross = [along_z(left[0], -1)], [across_z(left[1], -1)]
+    near, cross = near + [along_z(right[0], 1)], cross + [across_z(right[1], 1)]
     shape = jax.ShapeDtypeStruct(own.shape[2:], F32)
     return pl.pallas_call(
         finish_kernel,

time: 153 us -> 153 us (level)
  no operation moved by 1% of the time
where the time goes in v6:
time: 153 us
  waiting for transfers between devices  71.7 us (47%)
  starting transfers between devices  58.4 us (38%)
  Pallas kernels  10 us (7%)
  local copies, waits for them, and re-layouts  6.53 us (4%)
  other arithmetic  5.42 us (4%)
    ppermute x16, waiting for transfers between devices, along_z(): return lax.ppermute(array, 'z', [(i, (i + step) % NZ) for i in range(NZ)])  24.5 us
    ppermute x16, starting transfers between devices, along_z(): return lax.ppermute(array, 'z', [(i, (i + step) % NZ) for i in range(NZ)])  24.4 us
    ppermute x2, waiting for transfers between devices, swap_half(): return lax.ppermute(array, 'xh', [(0, 1), (1, 0)])  15.1 us
    ppermute x6, starting transfers between devices, to_grid(): return lax.ppermute(array, GRID, pairs)  14.5 us
    ppermute x5, waiting for transfers between devices, swap_xl(): return lax.ppermute(array, 'xl', [(0, 1), (1, 0)])  13.5 us
    ppermute x6, waiting for transfers between devices, to_grid(): return lax.ppermute(array, GRID, pairs)  13 us
    ppermute x6, starting transfers between devices, swap_core(): return lax.ppermute(array, 'core', [(0, 1), (1, 0)])  8.25 us
    pallas_call x1, Pallas kernels, whole_step(): pl.pallas_call(window_kernel, out_shape=[vmem((own, 4 * channels), BF), v...  5.2 us
  transfers between devices with their start and end apart: 37, of which 21 were waited for; matrix products, arithmetic and copies ran while one was open for 4% of the time, Pallas kernels for 4%

profile of v6, /device:TPU:1, one launch (start us, length us, event | category | flops | bytes accessed | tf_op | source)
XLA Modules:
  0.0 153.1 jit_solution(7048486491523288143)
XLA Ops:
  0.6 2.1 %collective-permute-start.4 = (bf16[192,1536]{1,0:T(8,128)(2,1)}, bf16[192,1536]{1,0:T(8,128)(2,1)S(1)}, u32[]{:S(2)}, u32[]{:S(2)}) collective-permute-start(bf16[192,1536]{1,0:T(8,128)(2,1)} %bitcast.64), channel_id=1, source_target_pairs={{0,8},{8,0},{1,9},{9,1},{2,10},{10,2},{3,11},{11,3},{4,12},{12,4},... | collective-permute-start | bytes 1769480 | tf_op jit(solution)/shard_map/ppermute | solution.py:71
  3.7 2.5 %collective-permute-start.8 = (bf16[2,48,768]{2,1,0:T(8,128)(2,1)S(1)}, bf16[2,48,768]{2,1,0:T(8,128)(2,1)S(1)}, u32[]{:S(2)}, u32[]{:S(2)}) collective-permute-start(bf16[2,48,768]{2,1,0:T(8,128)(2,1)S(1)} %pad_maximum_fusion.4.own_ref), channel_id=1, source_target_pairs={{0,128},{128,0},{1,129},{129,1},{2,130},{130,2},{3,131},{131,3},{4... | collective-permute-start | bytes 442376 | tf_op jit(solution)/shard_map/ppermute | solution.py:75
  6.2 15.1 %collective-permute-done.8.other_ref = bf16[2,48,768]{2,1,0:T(8,128)(2,1)S(1)} collective-permute-done((bf16[2,48,768]{2,1,0:T(8,128)(2,1)S(1)}, bf16[2,48,768]{2,1,0:T(8,128)(2,1)S(1)}, u32[]{:S(2)}, u32[]{:S(2)}) %collective-permute-start.8) | collective-permute-done | bytes 147488 | tf_op jit(solution)/shard_map/ppermute | solution.py:75
  21.4 1.7 %collective-permute-start.10 = (bf16[2,2,48,768]{3,2,1,0:T(8,128)(2,1)S(1)}, bf16[2,2,48,768]{3,2,1,0:T(8,128)(2,1)S(1)}, u32[]{:S(2)}, u32[]{:S(2)}) collective-permute-start(bf16[2,2,48,768]{3,2,1,0:T(8,128)(2,1)S(1)} %pair.1.refs_3_), channel_id=1, source_target_pairs={{0,16},{16,32},{32,48},{48,64},{64,80},{80,96},{96,112},{112,0},{1... | collective-permute-start | bytes 884744 | tf_op jit(solution)/shard_map/ppermute | solution.py:79
  23.1 4.0 %collective-permute-start.9 = (bf16[2,2,48,768]{3,2,1,0:T(8,128)(2,1)S(1)}, bf16[2,2,48,768]{3,2,1,0:T(8,128)(2,1)S(1)}, u32[]{:S(2)}, u32[]{:S(2)}) collective-permute-start(bf16[2,2,48,768]{3,2,1,0:T(8,128)(2,1)S(1)} %pair.1.refs_3_), channel_id=1, source_target_pairs={{0,112},{16,0},{32,16},{48,32},{64,48},{80,64},{96,80},{112,96},{1... | collective-permute-start | bytes 884744 | tf_op jit(solution)/shard_map/ppermute | solution.py:79
  27.1 1.8 %collective-permute-start.3 = (bf16[192,1536]{1,0:T(8,128)(2,1)}, bf16[192,1536]{1,0:T(8,128)(2,1)S(1)}, u32[]{:S(2)}, u32[]{:S(2)}) collective-permute-start(bf16[192,1536]{1,0:T(8,128)(2,1)} %bitcast.65), channel_id=1, source_target_pairs={{0,4},{4,0},{1,5},{5,1},{2,6},{6,2},{3,7},{7,3},{8,12},{12,8},{9,1... | collective-permute-start | bytes 1769480 | tf_op jit(solution)/shard_map/ppermute | solution.py:67
  28.9 3.9 %collective-permute-done.10.refs_5_ = bf16[2,2,48,768]{3,2,1,0:T(8,128)(2,1)S(1)} collective-permute-done((bf16[2,2,48,768]{3,2,1,0:T(8,128)(2,1)S(1)}, bf16[2,2,48,768]{3,2,1,0:T(8,128)(2,1)S(1)}, u32[]{:S(2)}, u32[]{:S(2)}) %collective-permute-start.10) | collective-permute-done | bytes 294944 | tf_op jit(solution)/shard_map/ppermute | solution.py:79
  32.9 2.7 %collective-permute-start.11 = (bf16[2,2,48,768]{3,2,1,0:T(8,128)(2,1)S(1)}, bf16[2,2,48,768]{3,2,1,0:T(8,128)(2,1)S(1)}, u32[]{:S(2)}, u32[]{:S(2)}) collective-permute-start(bf16[2,2,48,768]{3,2,1,0:T(8,128)(2,1)S(1)} %collective-permute-done.9.refs_4_), channel_id=1, source_target_pairs={{0,112},{16,0},{32,16},{48,32},{64,48},{80,64},{96,80},{112,96},{1... | collective-permute-start | bytes 884744 | tf_op jit(solution)/shard_map/ppermute | solution.py:79
  35.6 5.0 %collective-permute-done.12.refs_7_ = bf16[2,2,48,768]{3,2,1,0:T(8,128)(2,1)S(1)} collective-permute-done((bf16[2,2,48,768]{3,2,1,0:T(8,128)(2,1)S(1)}, bf16[2,2,48,768]{3,2,1,0:T(8,128)(2,1)S(1)}, u32[]{:S(2)}, u32[]{:S(2)}) %collective-permute-start.12) | collective-permute-done | bytes 294944 | tf_op jit(solution)/shard_map/ppermute | solution.py:79
  40.5 1.0 copy-done.1
  42.7 3.0 %collective-permute-start = (bf16[96,384]{1,0:T(8,128)(2,1)S(1)}, bf16[96,384]{1,0:T(8,128)(2,1)S(1)}, u32[]{:S(2)}, u32[]{:S(2)}) collective-permute-start(bf16[96,384]{1,0:T(8,128)(2,1)S(1)} %get-tuple-element.25), channel_id=1, source_target_pairs={{0,12},{4,0},{8,4},{12,8},{16,28},{20,16},{24,20},{28,24},{32,44},... | collective-permute-start | bytes 221192 | tf_op jit(solution)/shard_map/ppermute | solution.py:63
  45.8 2.2 %collective-permute-done.x1 = bf16[96,384]{1,0:T(8,128)(2,1)S(1)} collective-permute-done((bf16[96,384]{1,0:T(8,128)(2,1)S(1)}, bf16[96,384]{1,0:T(8,128)(2,1)S(1)}, u32[]{:S(2)}, u32[]{:S(2)}) %collective-permute-start) | collective-permute-done | bytes 73760 | tf_op jit(solution)/shard_map/ppermute | solution.py:63
  47.9 3.8 %collective-permute-start.1 = (bf16[96,384]{1,0:T(8,128)(2,1)S(1)}, bf16[96,384]{1,0:T(8,128)(2,1)S(1)}, u32[]{:S(2)}, u32[]{:S(2)}) collective-permute-start(bf16[96,384]{1,0:T(8,128)(2,1)S(1)} %get-tuple-element.26), channel_id=1, source_target_pairs={{0,240},{4,244},{8,248},{12,252},{16,0},{20,4},{24,8},{28,12},{32,... | collective-permute-start | bytes 221192 | tf_op jit(solution)/shard_map/ppermute | solution.py:63
  51.7 1.8 %collective-permute-done.1.x2 = bf16[96,384]{1,0:T(8,128)(2,1)S(1)} collective-permute-done((bf16[96,384]{1,0:T(8,128)(2,1)S(1)}, bf16[96,384]{1,0:T(8,128)(2,1)S(1)}, u32[]{:S(2)}, u32[]{:S(2)}) %collective-permute-start.1) | collective-permute-done | bytes 73760 | tf_op jit(solution)/shard_map/ppermute | solution.py:63
  53.5 5.8 %collective-permute-start.2 = (bf16[96,384]{1,0:T(8,128)(2,1)S(1)}, bf16[96,384]{1,0:T(8,128)(2,1)S(1)}, u32[]{:S(2)}, u32[]{:S(2)}) collective-permute-start(bf16[96,384]{1,0:T(8,128)(2,1)S(1)} %get-tuple-element.27), channel_id=1, source_target_pairs={{0,252},{4,240},{8,244},{12,248},{16,12},{20,0},{24,4},{28,8},{32,... | collective-permute-start | bytes 221192 | tf_op jit(solution)/shard_map/ppermute | solution.py:63
  59.2 1.9 %collective-permute-done.2.x3 = bf16[96,384]{1,0:T(8,128)(2,1)S(1)} collective-permute-done((bf16[96,384]{1,0:T(8,128)(2,1)S(1)}, bf16[96,384]{1,0:T(8,128)(2,1)S(1)}, u32[]{:S(2)}, u32[]{:S(2)}) %collective-permute-start.2) | collective-permute-done | bytes 73760 | tf_op jit(solution)/shard_map/ppermute | solution.py:63
  61.1 1.2 copy-done.3
  63.9 5.2 %window.1 = (bf16[64,1536]{1,0:T(8,128)(2,1)S(1)}, bf16[64,768]{1,0:T(8,128)(2,1)S(1)}) custom-call(f32[6]{0:T(128)S(1)} %copy-done.5, bf16[96,384]{1,0:T(8,128)(2,1)S(1)} %get-tuple-element.24.x0, bf16[96,384]{1,0:T(8,128)(2,1)S(1)} %collective-permute-done.x1, bf16[96,384]{1,0:T(8,128)(2,1)S(1)} %collective-permute-done.1.x2, ...), custom_call_target="tpu_custom_call" | custom-call | flops 402653184 | bytes 2000000 | tf_op jit(solution)/shard_map/window/pallas_call | solution.py:323
  69.1 5.0 %collective-permute-start.13 = (bf16[2,2,48,768]{3,2,1,0:T(8,128)(2,1)S(1)}, bf16[2,2,48,768]{3,2,1,0:T(8,128)(2,1)S(1)}, u32[]{:S(2)}, u32[]{:S(2)}) collective-permute-start(bf16[2,2,48,768]{3,2,1,0:T(8,128)(2,1)S(1)} %collective-permute-done.11.refs_6_), channel_id=1, source_target_pairs={{0,112},{16,0},{32,16},{48,32},{64,48},{80,64},{96,80},{112,96},{1... | collective-permute-start | bytes 884744 | tf_op jit(solution)/shard_map/ppermute | solution.py:79
  74.1 1.1 level.1
  75.5 3.3 %collective-permute-done.6.refs_1_ = bf16[64,768]{1,0:T(8,128)(2,1)S(1)} collective-permute-done((bf16[64,768]{1,0:T(8,128)(2,1)S(1)}, bf16[64,768]{1,0:T(8,128)(2,1)S(1)}, u32[]{:S(2)}, u32[]{:S(2)}) %collective-permute-start.6) | collective-permute-done | bytes 98336 | tf_op jit(solution)/shard_map/ppermute | solution.py:71
  78.8 2.5 %collective-permute-start.7 = (bf16[128,768]{1,0:T(8,128)(2,1)S(1)}, bf16[128,768]{1,0:T(8,128)(2,1)S(1)}, u32[]{:S(2)}, u32[]{:S(2)}) collective-permute-start(bf16[128,768]{1,0:T(8,128)(2,1)S(1)} %pad_maximum_fusion.2), channel_id=1, source_target_pairs={{0,4},{4,0},{1,5},{5,1},{2,6},{6,2},{3,7},{7,3},{8,12},{12,8},{9,1... | collective-permute-start | bytes 589832 | tf_op jit(solution)/shard_map/ppermute | solution.py:67
  81.3 1.7 %collective-permute-start.15 = (bf16[2,48,768]{2,1,0:T(8,128)(2,1)S(1)}, bf16[2,48,768]{2,1,0:T(8,128)(2,1)S(1)}, u32[]{:S(2)}, u32[]{:S(2)}) collective-permute-start(bf16[2,48,768]{2,1,0:T(8,128)(2,1)S(1)} %slice_bitcast_fusion.9), channel_id=1, source_target_pairs={{0,112},{16,0},{32,16},{48,32},{64,48},{80,64},{96,80},{112,96},{1... | collective-permute-start | bytes 442376 | tf_op jit(solution)/shard_map/ppermute | solution.py:79
  83.0 3.7 %collective-permute-done.15.refs_10_ = bf16[2,48,768]{2,1,0:T(8,128)(2,1)S(1)} collective-permute-done((bf16[2,48,768]{2,1,0:T(8,128)(2,1)S(1)}, bf16[2,48,768]{2,1,0:T(8,128)(2,1)S(1)}, u32[]{:S(2)}, u32[]{:S(2)}) %collective-permute-start.15) | collective-permute-done | bytes 147488 | tf_op jit(solution)/shard_map/ppermute | solution.py:79
  86.7 1.1 forward.1
  87.8 1.1 collective-permute-start.17
  89.0 1.1 collective-permute-done.17
  90.2 4.0 %collective-permute-done.18 = bf16[64,768]{1,0:T(8,128)(2,1)S(1)} collective-permute-done((bf16[64,768]{1,0:T(8,128)(2,1)S(1)}, bf16[64,768]{1,0:T(8,128)(2,1)S(1)}, u32[]{:S(2)}, u32[]{:S(2)}) %collective-permute-start.18) | collective-permute-done | bytes 98336 | tf_op jit(solution)/shard_map/ppermute | solution.py:71
  95.2 3.2 %collective-permute-done.19.refs_1_ = bf16[64,768]{1,0:T(8,128)(2,1)S(1)} collective-permute-done((bf16[64,768]{1,0:T(8,128)(2,1)S(1)}, bf16[64,768]{1,0:T(8,128)(2,1)S(1)}, u32[]{:S(2)}, u32[]{:S(2)}) %collective-permute-start.19) | collective-permute-done | bytes 98336 | tf_op jit(solution)/shard_map/ppermute | solution.py:71
  98.4 2.5 %collective-permute-start.20 = (bf16[128,768]{1,0:T(8,128)(2,1)S(1)}, bf16[128,768]{1,0:T(8,128)(2,1)S(1)}, u32[]{:S(2)}, u32[]{:S(2)}) collective-permute-start(bf16[128,768]{1,0:T(8,128)(2,1)S(1)} %pad_maximum_fusion.3), channel_id=1, source_target_pairs={{0,4},{4,0},{1,5},{5,1},{2,6},{6,2},{3,7},{7,3},{8,12},{12,8},{9,1... | collective-permute-start | bytes 589832 | tf_op jit(solution)/shard_map/ppermute | solution.py:67
  100.9 1.1 collective-permute-done.20.refs_2_
  102.0 1.5 %backward.1 = (bf16[8,2,2,48,768]{4,3,2,1,0:T(8,128)(2,1)S(1)}, bf16[128,768]{1,0:T(8,128)(2,1)S(1)}, bf16[128,768]{1,0:T(8,128)(2,1)S(1)}) custom-call(bf16[64,768]{1,0:T(8,128)(2,1)S(1)} %get-tuple-element.52.refs_0_, bf16[64,768]{1,0:T(8,128)(2,1)S(1)} %collective-permute-done.19.refs_1_, bf16[128,768]{1,0:T(8,128)(2,1)S(1)} %collective-permute-done.20.refs_2_, ...), custom_call_target="tpu_custom_call" | custom-call | flops 1207959552 | bytes 6000000 | tf_op jit(solution)/shard_map/backward/pallas_call | solution.py:384
  104.6 3.4 %collective-permute-start.27 = (bf16[2,48,768]{2,1,0:T(8,128)(2,1)S(1)}, bf16[2,48,768]{2,1,0:T(8,128)(2,1)S(1)}, u32[]{:S(2)}, u32[]{:S(2)}) collective-permute-start(bf16[2,48,768]{2,1,0:T(8,128)(2,1)S(1)} %get-tuple-element.48), channel_id=1, source_target_pairs={{0,112},{16,0},{32,16},{48,32},{64,48},{80,64},{96,80},{112,96},{1... | collective-permute-start | bytes 442376 | tf_op jit(solution)/shard_map/ppermute | solution.py:79
  108.0 1.0 collective-permute-start.26
  109.0 2.1 %collective-permute-done.27 = bf16[2,48,768]{2,1,0:T(8,128)(2,1)S(1)} collective-permute-done((bf16[2,48,768]{2,1,0:T(8,128)(2,1)S(1)}, bf16[2,48,768]{2,1,0:T(8,128)(2,1)S(1)}, u32[]{:S(2)}, u32[]{:S(2)}) %collective-permute-start.27) | collective-permute-done | bytes 147488 | tf_op jit(solution)/shard_map/ppermute | solution.py:79
  111.1 3.5 %collective-permute-start.28 = (bf16[2,2,48,768]{3,2,1,0:T(8,128)(2,1)S(1)}, bf16[2,2,48,768]{3,2,1,0:T(8,128)(2,1)S(1)}, u32[]{:S(2)}, u32[]{:S(2)}) collective-permute-start(bf16[2,2,48,768]{3,2,1,0:T(8,128)(2,1)S(1)} %pad_maximum_fusion), channel_id=1, source_target_pairs={{0,112},{16,0},{32,16},{48,32},{64,48},{80,64},{96,80},{112,96},{1... | collective-permute-start | bytes 884744 | tf_op jit(solution)/shard_map/ppermute | solution.py:79
  115.8 3.0 %collective-permute-done.22 = bf16[64,768]{1,0:T(8,128)(2,1)S(1)} collective-permute-done((bf16[64,768]{1,0:T(8,128)(2,1)S(1)}, bf16[64,768]{1,0:T(8,128)(2,1)S(1)}, u32[]{:S(2)}, u32[]{:S(2)}) %collective-permute-start.22) | collective-permute-done | bytes 98336 | tf_op jit(solution)/shard_map/ppermute | solution.py:71
  120.0 1.8 %collective-permute-start.25 = (bf16[16,1536]{1,0:T(8,128)(2,1)S(1)}, bf16[16,1536]{1,0:T(8,128)(2,1)S(1)}, u32[]{:S(2)}, u32[]{:S(2)}) collective-permute-start(bf16[16,1536]{1,0:T(8,128)(2,1)S(1)} %get-tuple-element.62), channel_id=1, source_target_pairs={{0,4},{4,8},{8,12},{12,0},{16,20},{20,24},{24,28},{28,16},{32,36},... | collective-permute-start | bytes 147464 | tf_op jit(solution)/shard_map/ppermute | solution.py:63
  122.5 7.2 %collective-permute-done.23 = bf16[16,1536]{1,0:T(8,128)(2,1)S(1)} collective-permute-done((bf16[16,1536]{1,0:T(8,128)(2,1)S(1)}, bf16[16,1536]{1,0:T(8,128)(2,1)S(1)}, u32[]{:S(2)}, u32[]{:S(2)}) %collective-permute-start.23) | collective-permute-done | bytes 49184 | tf_op jit(solution)/shard_map/ppermute | solution.py:63
  130.0 1.0 bitcast_add_fusion.1
  131.0 1.5 %collective-permute-start.33 = (bf16[2,2,48,768]{3,2,1,0:T(8,128)(2,1)S(1)}, bf16[2,2,48,768]{3,2,1,0:T(8,128)(2,1)S(1)}, u32[]{:S(2)}, u32[]{:S(2)}) collective-permute-start(bf16[2,2,48,768]{3,2,1,0:T(8,128)(2,1)S(1)} %bitcast_add_fusion.1), channel_id=1, source_target_pairs={{0,16},{16,32},{32,48},{48,64},{64,80},{80,96},{96,112},{112,0},{1... | collective-permute-start | bytes 884744 | tf_op jit(solution)/shard_map/ppermute | solution.py:79
  132.6 5.6 %collective-permute-done.29 = bf16[2,2,48,768]{3,2,1,0:T(8,128)(2,1)} collective-permute-done((bf16[2,2,48,768]{3,2,1,0:T(8,128)(2,1)}, bf16[2,2,48,768]{3,2,1,0:T(8,128)(2,1)}, u32[]{:S(2)}, u32[]{:S(2)}) %collective-permute-start.29) | collective-permute-done | bytes 294944 | tf_op jit(solution)/shard_map/ppermute | solution.py:79
  138.1 1.0 fusion
  139.1 2.1 %collective-permute-start.35 = (bf16[2,48,768]{2,1,0:T(8,128)(2,1)S(1)}, bf16[2,48,768]{2,1,0:T(8,128)(2,1)S(1)}, u32[]{:S(2)}, u32[]{:S(2)}) collective-permute-start(bf16[2,48,768]{2,1,0:T(8,128)(2,1)S(1)} %get-tuple-element.57), channel_id=1, source_target_pairs={{0,240},{16,128},{32,144},{48,160},{64,176},{80,192},{96,208},{112... | collective-permute-start | bytes 442376 | tf_op jit(solution)/shard_map/ppermute | solution.py:87
  141.3 2.7 %collective-permute-start.36 = (bf16[2,48,768]{2,1,0:T(8,128)(2,1)S(1)}, bf16[2,48,768]{2,1,0:T(8,128)(2,1)S(1)}, u32[]{:S(2)}, u32[]{:S(2)}) collective-permute-start(bf16[2,48,768]{2,1,0:T(8,128)(2,1)S(1)} %get-tuple-element.55), channel_id=1, source_target_pairs={{0,144},{16,160},{32,176},{48,192},{64,208},{80,224},{96,240},{112... | collective-permute-start | bytes 442376 | tf_op jit(solution)/shard_map/ppermute | solution.py:87
  145.5 1.8 %collective-permute-done.35.refs_4_ = bf16[2,48,768]{2,1,0:T(8,128)(2,1)S(1)} collective-permute-done((bf16[2,48,768]{2,1,0:T(8,128)(2,1)S(1)}, bf16[2,48,768]{2,1,0:T(8,128)(2,1)S(1)}, u32[]{:S(2)}, u32[]{:S(2)}) %collective-permute-start.35) | collective-permute-done | bytes 147488 | tf_op jit(solution)/shard_map/ppermute | solution.py:87
  147.8 1.7 %collective-permute-done.36.refs_5_ = bf16[2,48,768]{2,1,0:T(8,128)(2,1)S(1)} collective-permute-done((bf16[2,48,768]{2,1,0:T(8,128)(2,1)S(1)}, bf16[2,48,768]{2,1,0:T(8,128)(2,1)S(1)}, u32[]{:S(2)}, u32[]{:S(2)}) %collective-permute-start.36) | collective-permute-done | bytes 147488 | tf_op jit(solution)/shard_map/ppermute | solution.py:87
  149.5 2.8 %collective-permute-done.34.refs_3_ = bf16[2,48,768]{2,1,0:T(8,128)(2,1)S(1)} collective-permute-done((bf16[2,48,768]{2,1,0:T(8,128)(2,1)S(1)}, bf16[2,48,768]{2,1,0:T(8,128)(2,1)S(1)}, u32[]{:S(2)}, u32[]{:S(2)}) %collective-permute-start.34) | collective-permute-done | bytes 147488 | tf_op jit(solution)/shard_map/ppermute | solution.py:79
  (80 shorter events, 12.5 us)
Async XLA Ops:
  0.6 73.5 %copy-start = (bf16[1536,192]{0,1:T(8,128)(2,1)S(1)}, bf16[1536,192]{0,1:T(8,128)(2,1)}, u32[]{:S(2)}) copy-start(bf16[1536,192]{0,1:T(8,128)(2,1)} %param.12) | copy-start | bytes 1769476
  0.6 28.3 %collective-permute-start.4 = (bf16[192,1536]{1,0:T(8,128)(2,1)}, bf16[192,1536]{1,0:T(8,128)(2,1)S(1)}, u32[]{:S(2)}, u32[]{:S(2)}) collective-permute-start(bf16[192,1536]{1,0:T(8,128)(2,1)} %bitcast.64), channel_id=1, source_target_pairs={{0,8},{8,0},{1,9},{9,1},{2,10},{10,2},{3,11},{11,3},{4,12},{12,4},... | collective-permute-start | bytes 1769480 | tf_op jit(solution)/shard_map/ppermute | solution.py:71
  3.7 17.6 %collective-permute-start.8 = (bf16[2,48,768]{2,1,0:T(8,128)(2,1)S(1)}, bf16[2,48,768]{2,1,0:T(8,128)(2,1)S(1)}, u32[]{:S(2)}, u32[]{:S(2)}) collective-permute-start(bf16[2,48,768]{2,1,0:T(8,128)(2,1)S(1)} %pad_maximum_fusion.4.own_ref), channel_id=1, source_target_pairs={{0,128},{128,0},{1,129},{129,1},{2,130},{130,2},{3,131},{131,3},{4... | collective-permute-start | bytes 442376 | tf_op jit(solution)/shard_map/ppermute | solution.py:75
  21.4 11.5 %collective-permute-start.10 = (bf16[2,2,48,768]{3,2,1,0:T(8,128)(2,1)S(1)}, bf16[2,2,48,768]{3,2,1,0:T(8,128)(2,1)S(1)}, u32[]{:S(2)}, u32[]{:S(2)}) collective-permute-start(bf16[2,2,48,768]{3,2,1,0:T(8,128)(2,1)S(1)} %pair.1.refs_3_), channel_id=1, source_target_pairs={{0,16},{16,32},{32,48},{48,64},{64,80},{80,96},{96,112},{112,0},{1... | collective-permute-start | bytes 884744 | tf_op jit(solution)/shard_map/ppermute | solution.py:79
  23.1 9.8 %collective-permute-start.9 = (bf16[2,2,48,768]{3,2,1,0:T(8,128)(2,1)S(1)}, bf16[2,2,48,768]{3,2,1,0:T(8,128)(2,1)S(1)}, u32[]{:S(2)}, u32[]{:S(2)}) collective-permute-start(bf16[2,2,48,768]{3,2,1,0:T(8,128)(2,1)S(1)} %pair.1.refs_3_), channel_id=1, source_target_pairs={{0,112},{16,0},{32,16},{48,32},{64,48},{80,64},{96,80},{112,96},{1... | collective-permute-start | bytes 884744 | tf_op jit(solution)/shard_map/ppermute | solution.py:79
  27.1 47.0 %collective-permute-start.3 = (bf16[192,1536]{1,0:T(8,128)(2,1)}, bf16[192,1536]{1,0:T(8,128)(2,1)S(1)}, u32[]{:S(2)}, u32[]{:S(2)}) collective-permute-start(bf16[192,1536]{1,0:T(8,128)(2,1)} %bitcast.65), channel_id=1, source_target_pairs={{0,4},{4,0},{1,5},{5,1},{2,6},{6,2},{3,7},{7,3},{8,12},{12,8},{9,1... | collective-permute-start | bytes 1769480 | tf_op jit(solution)/shard_map/ppermute | solution.py:67
  28.9 45.2 %collective-permute-start.5 = (bf16[192,1536]{1,0:T(8,128)(2,1)S(1)}, bf16[192,1536]{1,0:T(8,128)(2,1)S(1)}, u32[]{:S(2)}, u32[]{:S(2)}) collective-permute-start(bf16[192,1536]{1,0:T(8,128)(2,1)S(1)} %collective-permute-done.4.near_ref), channel_id=1, source_target_pairs={{0,4},{4,0},{1,5},{5,1},{2,6},{6,2},{3,7},{7,3},{8,12},{12,8},{9,1... | collective-permute-start | bytes 1769480 | tf_op jit(solution)/shard_map/ppermute | solution.py:67
  32.9 7.7 %collective-permute-start.12 = (bf16[2,2,48,768]{3,2,1,0:T(8,128)(2,1)S(1)}, bf16[2,2,48,768]{3,2,1,0:T(8,128)(2,1)S(1)}, u32[]{:S(2)}, u32[]{:S(2)}) collective-permute-start(bf16[2,2,48,768]{3,2,1,0:T(8,128)(2,1)S(1)} %collective-permute-done.10.refs_5_), channel_id=1, source_target_pairs={{0,16},{16,32},{32,48},{48,64},{64,80},{80,96},{96,112},{112,0},{1... | collective-permute-start | bytes 884744 | tf_op jit(solution)/shard_map/ppermute | solution.py:79
  32.9 36.2 %collective-permute-start.11 = (bf16[2,2,48,768]{3,2,1,0:T(8,128)(2,1)S(1)}, bf16[2,2,48,768]{3,2,1,0:T(8,128)(2,1)S(1)}, u32[]{:S(2)}, u32[]{:S(2)}) collective-permute-start(bf16[2,2,48,768]{3,2,1,0:T(8,128)(2,1)S(1)} %collective-permute-done.9.refs_4_), channel_id=1, source_target_pairs={{0,112},{16,0},{32,16},{48,32},{64,48},{80,64},{96,80},{112,96},{1... | collective-permute-start | bytes 884744 | tf_op jit(solution)/shard_map/ppermute | solution.py:79
  40.5 34.8 %collective-permute-start.14 = (bf16[2,2,48,768]{3,2,1,0:T(8,128)(2,1)S(1)}, bf16[2,2,48,768]{3,2,1,0:T(8,128)(2,1)S(1)}, u32[]{:S(2)}, u32[]{:S(2)}) collective-permute-start(bf16[2,2,48,768]{3,2,1,0:T(8,128)(2,1)S(1)} %collective-permute-done.12.refs_7_), channel_id=1, source_target_pairs={{0,16},{16,32},{32,48},{48,64},{64,80},{80,96},{96,112},{112,0},{1... | collective-permute-start | bytes 884744 | tf_op jit(solution)/shard_map/ppermute | solution.py:79
  40.5 1.0 copy-start.1
  41.5 0.9 copy-start.2
  42.7 5.2 %collective-permute-start = (bf16[96,384]{1,0:T(8,128)(2,1)S(1)}, bf16[96,384]{1,0:T(8,128)(2,1)S(1)}, u32[]{:S(2)}, u32[]{:S(2)}) collective-permute-start(bf16[96,384]{1,0:T(8,128)(2,1)S(1)} %get-tuple-element.25), channel_id=1, source_target_pairs={{0,12},{4,0},{8,4},{12,8},{16,28},{20,16},{24,20},{28,24},{32,44},... | collective-permute-start | bytes 221192 | tf_op jit(solution)/shard_map/ppermute | solution.py:63
  47.9 5.6 %collective-permute-start.1 = (bf16[96,384]{1,0:T(8,128)(2,1)S(1)}, bf16[96,384]{1,0:T(8,128)(2,1)S(1)}, u32[]{:S(2)}, u32[]{:S(2)}) collective-permute-start(bf16[96,384]{1,0:T(8,128)(2,1)S(1)} %get-tuple-element.26), channel_id=1, source_target_pairs={{0,240},{4,244},{8,248},{12,252},{16,0},{20,4},{24,8},{28,12},{32,... | collective-permute-start | bytes 221192 | tf_op jit(solution)/shard_map/ppermute | solution.py:63
  53.5 7.6 %collective-permute-start.2 = (bf16[96,384]{1,0:T(8,128)(2,1)S(1)}, bf16[96,384]{1,0:T(8,128)(2,1)S(1)}, u32[]{:S(2)}, u32[]{:S(2)}) collective-permute-start(bf16[96,384]{1,0:T(8,128)(2,1)S(1)} %get-tuple-element.27), channel_id=1, source_target_pairs={{0,252},{4,240},{8,244},{12,248},{16,12},{20,0},{24,4},{28,8},{32,... | collective-permute-start | bytes 221192 | tf_op jit(solution)/shard_map/ppermute | solution.py:63
  61.1 1.2 copy-start.3
  62.3 1.0 copy-start.4
  63.2 0.7 copy-start.5
  69.1 12.2 %collective-permute-start.13 = (bf16[2,2,48,768]{3,2,1,0:T(8,128)(2,1)S(1)}, bf16[2,2,48,768]{3,2,1,0:T(8,128)(2,1)S(1)}, u32[]{:S(2)}, u32[]{:S(2)}) collective-permute-start(bf16[2,2,48,768]{3,2,1,0:T(8,128)(2,1)S(1)} %collective-permute-done.11.refs_6_), channel_id=1, source_target_pairs={{0,112},{16,0},{32,16},{48,32},{64,48},{80,64},{96,80},{112,96},{1... | collective-permute-start | bytes 884744 | tf_op jit(solution)/shard_map/ppermute | solution.py:79
  75.2 3.6 %collective-permute-start.6 = (bf16[64,768]{1,0:T(8,128)(2,1)S(1)}, bf16[64,768]{1,0:T(8,128)(2,1)S(1)}, u32[]{:S(2)}, u32[]{:S(2)}) collective-permute-start(bf16[64,768]{1,0:T(8,128)(2,1)S(1)} %get-tuple-element.30.refs_0_), channel_id=1, source_target_pairs={{0,8},{8,0},{1,9},{9,1},{2,10},{10,2},{3,11},{11,3},{4,12},{12,4},... | collective-permute-start | bytes 294920 | tf_op jit(solution)/shard_map/ppermute | solution.py:71
  75.4 7.7 %collective-permute-start.16 = (bf16[2,48,768]{2,1,0:T(8,128)(2,1)S(1)}, bf16[2,48,768]{2,1,0:T(8,128)(2,1)S(1)}, u32[]{:S(2)}, u32[]{:S(2)}) collective-permute-start(bf16[2,48,768]{2,1,0:T(8,128)(2,1)S(1)} %slice_bitcast_fusion.8), channel_id=1, source_target_pairs={{0,16},{16,32},{32,48},{48,64},{64,80},{80,96},{96,112},{112,0},{1... | collective-permute-start | bytes 442376 | tf_op jit(solution)/shard_map/ppermute | solution.py:79
  78.8 7.9 %collective-permute-start.7 = (bf16[128,768]{1,0:T(8,128)(2,1)S(1)}, bf16[128,768]{1,0:T(8,128)(2,1)S(1)}, u32[]{:S(2)}, u32[]{:S(2)}) collective-permute-start(bf16[128,768]{1,0:T(8,128)(2,1)S(1)} %pad_maximum_fusion.2), channel_id=1, source_target_pairs={{0,4},{4,0},{1,5},{5,1},{2,6},{6,2},{3,7},{7,3},{8,12},{12,8},{9,1... | collective-permute-start | bytes 589832 | tf_op jit(solution)/shard_map/ppermute | solution.py:67
  81.3 5.4 %collective-permute-start.15 = (bf16[2,48,768]{2,1,0:T(8,128)(2,1)S(1)}, bf16[2,48,768]{2,1,0:T(8,128)(2,1)S(1)}, u32[]{:S(2)}, u32[]{:S(2)}) collective-permute-start(bf16[2,48,768]{2,1,0:T(8,128)(2,1)S(1)} %slice_bitcast_fusion.9), channel_id=1, source_target_pairs={{0,112},{16,0},{32,16},{48,32},{64,48},{80,64},{96,80},{112,96},{1... | collective-permute-start | bytes 442376 | tf_op jit(solution)/shard_map/ppermute | solution.py:79
  87.8 2.2 %collective-permute-start.17 = (bf16[128,768]{1,0:T(8,128)(2,1)S(1)}, bf16[128,768]{1,0:T(8,128)(2,1)S(1)}, u32[]{:S(2)}, u32[]{:S(2)}) collective-permute-start(bf16[128,768]{1,0:T(8,128)(2,1)S(1)} %get-tuple-element.32), channel_id=1, source_target_pairs={{0,4},{4,0},{1,5},{5,1},{2,6},{6,2},{3,7},{7,3},{8,12},{12,8},{9,1... | collective-permute-start | bytes 589832 | tf_op jit(solution)/shard_map/ppermute | solution.py:67
  90.1 4.1 %collective-permute-start.18 = (bf16[64,768]{1,0:T(8,128)(2,1)S(1)}, bf16[64,768]{1,0:T(8,128)(2,1)S(1)}, u32[]{:S(2)}, u32[]{:S(2)}) collective-permute-start(bf16[64,768]{1,0:T(8,128)(2,1)S(1)} %slice.223), channel_id=1, source_target_pairs={{0,8},{8,0},{1,9},{9,1},{2,10},{10,2},{3,11},{11,3},{4,12},{12,4},... | collective-permute-start | bytes 294920 | tf_op jit(solution)/shard_map/ppermute | solution.py:71
  94.9 3.6 %collective-permute-start.19 = (bf16[64,768]{1,0:T(8,128)(2,1)S(1)}, bf16[64,768]{1,0:T(8,128)(2,1)S(1)}, u32[]{:S(2)}, u32[]{:S(2)}) collective-permute-start(bf16[64,768]{1,0:T(8,128)(2,1)S(1)} %get-tuple-element.52.refs_0_), channel_id=1, source_target_pairs={{0,8},{8,0},{1,9},{9,1},{2,10},{10,2},{3,11},{11,3},{4,12},{12,4},... | collective-permute-start | bytes 294920 | tf_op jit(solution)/shard_map/ppermute | solution.py:71
  98.4 3.5 %collective-permute-start.20 = (bf16[128,768]{1,0:T(8,128)(2,1)S(1)}, bf16[128,768]{1,0:T(8,128)(2,1)S(1)}, u32[]{:S(2)}, u32[]{:S(2)}) collective-permute-start(bf16[128,768]{1,0:T(8,128)(2,1)S(1)} %pad_maximum_fusion.3), channel_id=1, source_target_pairs={{0,4},{4,0},{1,5},{5,1},{2,6},{6,2},{3,7},{7,3},{8,12},{12,8},{9,1... | collective-permute-start | bytes 589832 | tf_op jit(solution)/shard_map/ppermute | solution.py:67
  104.2 10.4 %collective-permute-start.21 = (bf16[128,768]{1,0:T(8,128)(2,1)S(1)}, bf16[128,768]{1,0:T(8,128)(2,1)S(1)}, u32[]{:S(2)}, u32[]{:S(2)}) collective-permute-start(bf16[128,768]{1,0:T(8,128)(2,1)S(1)} %get-tuple-element.40), channel_id=1, source_target_pairs={{0,4},{4,0},{1,5},{5,1},{2,6},{6,2},{3,7},{7,3},{8,12},{12,8},{9,1... | collective-permute-start | bytes 589832 | tf_op jit(solution)/shard_map/ppermute | solution.py:67
  104.6 10.0 %collective-permute-start.31 = (bf16[2,48,768]{2,1,0:T(8,128)(2,1)S(1)}, bf16[2,48,768]{2,1,0:T(8,128)(2,1)S(1)}, u32[]{:S(2)}, u32[]{:S(2)}) collective-permute-start(bf16[2,48,768]{2,1,0:T(8,128)(2,1)S(1)} %get-tuple-element.47), channel_id=1, source_target_pairs={{0,16},{16,32},{32,48},{48,64},{64,80},{80,96},{96,112},{112,0},{1... | collective-permute-start | bytes 442376 | tf_op jit(solution)/shard_map/ppermute | solution.py:79
  104.6 6.5 %collective-permute-start.27 = (bf16[2,48,768]{2,1,0:T(8,128)(2,1)S(1)}, bf16[2,48,768]{2,1,0:T(8,128)(2,1)S(1)}, u32[]{:S(2)}, u32[]{:S(2)}) collective-permute-start(bf16[2,48,768]{2,1,0:T(8,128)(2,1)S(1)} %get-tuple-element.48), channel_id=1, source_target_pairs={{0,112},{16,0},{32,16},{48,32},{64,48},{80,64},{96,80},{112,96},{1... | collective-permute-start | bytes 442376 | tf_op jit(solution)/shard_map/ppermute | solution.py:79
  108.0 37.5 %collective-permute-start.26 = (bf16[2,48,768]{2,1,0:T(8,128)(2,1)}, bf16[2,48,768]{2,1,0:T(8,128)(2,1)S(1)}, u32[]{:S(2)}, u32[]{:S(2)}) collective-permute-start(bf16[2,48,768]{2,1,0:T(8,128)(2,1)} %get-tuple-element.49), channel_id=1, source_target_pairs={{0,128},{128,0},{1,129},{129,1},{2,130},{130,2},{3,131},{131,3},{4... | collective-permute-start | bytes 442376 | tf_op jit(solution)/shard_map/ppermute | solution.py:75
  111.1 8.9 %collective-permute-start.28 = (bf16[2,2,48,768]{3,2,1,0:T(8,128)(2,1)S(1)}, bf16[2,2,48,768]{3,2,1,0:T(8,128)(2,1)S(1)}, u32[]{:S(2)}, u32[]{:S(2)}) collective-permute-start(bf16[2,2,48,768]{3,2,1,0:T(8,128)(2,1)S(1)} %pad_maximum_fusion), channel_id=1, source_target_pairs={{0,112},{16,0},{32,16},{48,32},{64,48},{80,64},{96,80},{112,96},{1... | collective-permute-start | bytes 884744 | tf_op jit(solution)/shard_map/ppermute | solution.py:79
  114.7 4.1 %collective-permute-start.22 = (bf16[64,768]{1,0:T(8,128)(2,1)S(1)}, bf16[64,768]{1,0:T(8,128)(2,1)S(1)}, u32[]{:S(2)}, u32[]{:S(2)}) collective-permute-start(bf16[64,768]{1,0:T(8,128)(2,1)S(1)} %slice.222), channel_id=1, source_target_pairs={{0,8},{8,0},{1,9},{9,1},{2,10},{10,2},{3,11},{11,3},{4,12},{12,4},... | collective-permute-start | bytes 294920 | tf_op jit(solution)/shard_map/ppermute | solution.py:71
  115.8 14.2 %collective-permute-start.32 = (bf16[2,2,48,768]{3,2,1,0:T(8,128)(2,1)}, bf16[2,2,48,768]{3,2,1,0:T(8,128)(2,1)}, u32[]{:S(2)}, u32[]{:S(2)}) collective-permute-start(bf16[2,2,48,768]{3,2,1,0:T(8,128)(2,1)} %pad_maximum_fusion.1), channel_id=1, source_target_pairs={{0,16},{16,32},{32,48},{48,64},{64,80},{80,96},{96,112},{112,0},{1... | collective-permute-start | bytes 884744 | tf_op jit(solution)/shard_map/ppermute | solution.py:79
  118.8 10.8 %collective-permute-start.23 = (bf16[16,1536]{1,0:T(8,128)(2,1)S(1)}, bf16[16,1536]{1,0:T(8,128)(2,1)S(1)}, u32[]{:S(2)}, u32[]{:S(2)}) collective-permute-start(bf16[16,1536]{1,0:T(8,128)(2,1)S(1)} %get-tuple-element.59), channel_id=1, source_target_pairs={{0,20},{4,24},{8,28},{12,16},{16,36},{20,40},{24,44},{28,32},{32,5... | collective-permute-start | bytes 147464 | tf_op jit(solution)/shard_map/ppermute | solution.py:63
  118.9 10.7 %collective-permute-start.24 = (bf16[16,1536]{1,0:T(8,128)(2,1)S(1)}, bf16[16,1536]{1,0:T(8,128)(2,1)S(1)}, u32[]{:S(2)}, u32[]{:S(2)}) collective-permute-start(bf16[16,1536]{1,0:T(8,128)(2,1)S(1)} %get-tuple-element.60), channel_id=1, source_target_pairs={{0,16},{4,20},{8,24},{12,28},{16,32},{20,36},{24,40},{28,44},{32,4... | collective-permute-start | bytes 147464 | tf_op jit(solution)/shard_map/ppermute | solution.py:63
  120.0 9.7 %collective-permute-start.25 = (bf16[16,1536]{1,0:T(8,128)(2,1)S(1)}, bf16[16,1536]{1,0:T(8,128)(2,1)S(1)}, u32[]{:S(2)}, u32[]{:S(2)}) collective-permute-start(bf16[16,1536]{1,0:T(8,128)(2,1)S(1)} %get-tuple-element.62), channel_id=1, source_target_pairs={{0,4},{4,8},{8,12},{12,0},{16,20},{20,24},{24,28},{28,16},{32,36},... | collective-permute-start | bytes 147464 | tf_op jit(solution)/shard_map/ppermute | solution.py:63
  129.7 8.5 %collective-permute-start.29 = (bf16[2,2,48,768]{3,2,1,0:T(8,128)(2,1)}, bf16[2,2,48,768]{3,2,1,0:T(8,128)(2,1)}, u32[]{:S(2)}, u32[]{:S(2)}) collective-permute-start(bf16[2,2,48,768]{3,2,1,0:T(8,128)(2,1)} %fusion.1), channel_id=1, source_target_pairs={{0,112},{16,0},{32,16},{48,32},{64,48},{80,64},{96,80},{112,96},{1... | collective-permute-start | bytes 884744 | tf_op jit(solution)/shard_map/ppermute | solution.py:79
  131.0 10.2 %collective-permute-start.33 = (bf16[2,2,48,768]{3,2,1,0:T(8,128)(2,1)S(1)}, bf16[2,2,48,768]{3,2,1,0:T(8,128)(2,1)S(1)}, u32[]{:S(2)}, u32[]{:S(2)}) collective-permute-start(bf16[2,2,48,768]{3,2,1,0:T(8,128)(2,1)S(1)} %bitcast_add_fusion.1), channel_id=1, source_target_pairs={{0,16},{16,32},{32,48},{48,64},{64,80},{80,96},{96,112},{112,0},{1... | collective-permute-start | bytes 884744 | tf_op jit(solution)/shard_map/ppermute | solution.py:79
  139.1 8.2 %collective-permute-start.35 = (bf16[2,48,768]{2,1,0:T(8,128)(2,1)S(1)}, bf16[2,48,768]{2,1,0:T(8,128)(2,1)S(1)}, u32[]{:S(2)}, u32[]{:S(2)}) collective-permute-start(bf16[2,48,768]{2,1,0:T(8,128)(2,1)S(1)} %get-tuple-element.57), channel_id=1, source_target_pairs={{0,240},{16,128},{32,144},{48,160},{64,176},{80,192},{96,208},{112... | collective-permute-start | bytes 442376 | tf_op jit(solution)/shard_map/ppermute | solution.py:87
  141.2 6.5 %collective-permute-start.30 = (bf16[2,48,768]{2,1,0:T(8,128)(2,1)S(1)}, bf16[2,48,768]{2,1,0:T(8,128)(2,1)S(1)}, u32[]{:S(2)}, u32[]{:S(2)}) collective-permute-start(bf16[2,48,768]{2,1,0:T(8,128)(2,1)S(1)} %get-tuple-element.58), channel_id=1, source_target_pairs={{0,112},{16,0},{32,16},{48,32},{64,48},{80,64},{96,80},{112,96},{1... | collective-permute-start | bytes 442376 | tf_op jit(solution)/shard_map/ppermute | solution.py:79
  141.3 8.2 %collective-permute-start.36 = (bf16[2,48,768]{2,1,0:T(8,128)(2,1)S(1)}, bf16[2,48,768]{2,1,0:T(8,128)(2,1)S(1)}, u32[]{:S(2)}, u32[]{:S(2)}) collective-permute-start(bf16[2,48,768]{2,1,0:T(8,128)(2,1)S(1)} %get-tuple-element.55), channel_id=1, source_target_pairs={{0,144},{16,160},{32,176},{48,192},{64,208},{80,224},{96,240},{112... | collective-permute-start | bytes 442376 | tf_op jit(solution)/shard_map/ppermute | solution.py:87
  144.0 8.3 %collective-permute-start.34 = (bf16[2,48,768]{2,1,0:T(8,128)(2,1)S(1)}, bf16[2,48,768]{2,1,0:T(8,128)(2,1)S(1)}, u32[]{:S(2)}, u32[]{:S(2)}) collective-permute-start(bf16[2,48,768]{2,1,0:T(8,128)(2,1)S(1)} %get-tuple-element.56), channel_id=1, source_target_pairs={{0,16},{16,32},{32,48},{48,64},{64,80},{80,96},{96,112},{112,0},{1... | collective-permute-start | bytes 442376 | tf_op jit(solution)/shard_map/ppermute | solution.py:79
